TPU v7x, 32 devices: a whole 2x2x4 slice. The times are simulated.
32 devices in a mesh: gx: 8 (over z, y), gy: 4 (over x, core).
Axes of the slice: x: 2, y: 2, z: 4, core: 2. Of those that a mesh axis runs over, the one named last changes fastest.
Arguments:
- cell_state: float32 [39, 65536], P(None, ('gx', 'gy')), may hold values from 0.1 to 2
- coupling: float32 [39, 39], replicated, may hold values from -1 to 1
- basal_rate: float32 [39], replicated, may hold values from 0.1 to 1
- half_sat: float32 [39], replicated, may hold values from 0.2 to 2
- decay_rate: float32 [39], replicated, may hold values from 0.1 to 1
- uptake_weight: float32 [39], replicated, may hold values from -1 to 1
- agent_counts: int32 [32], P(('gx', 'gy')), may hold values from 512 to 2048, as said below
- divider_ids: int32 [4096], P(('gx', 'gy')), may hold values from 0 to 2047, as said below
- destinations: int32 [4096, 1], P(('gx', 'gy')), may hold values from 0 to 7; in each aligned block of 128 rows (0 to 127, 128 to 255, ...) at most 32 rows name the same one
- voxel_index: int32 [65536], P(('gx', 'gy')), may hold values from 0 to 196607, as said below
- oxygen: float32 [64, 64, 512], P(None, 'gx', 'gy'), may hold values from 0.5 to 1.5
Outputs:
- new_state: float32 [39, 65536], P(None, ('gx', 'gy'))
- daughter_state: float32 [39, 8192], P(None, ('gx', 'gy'))
- new_oxygen: float32 [64, 64, 512], P(None, 'gx', 'gy')
Inputs may be any that keep to these rules, and one draw needn't show every extreme that they name: Live agents of a device are its first agent_counts slots; at least 512, and some device holds 2048. `divider_ids`: each entry is below the live count of its device; entries may repeat. `destinations`: within the list of one device no x-slab is named by more than 32 rows. `voxel_index`: the named voxel lies in the agent's own x-slab or an adjacent one (s = 0, 1 or 2) and inside the grid, with y inside its device's range.
All inputs are finite; a program needn't handle non-finite values.
Results may differ from a plain program's by a relative error of at most 0.0011.
Values may be sent and summed in bfloat16 or wider, within the bound.
No kernel may reach another device: no remote copies, remote signals or barrier semaphores. Data moves between devices by JAX's collectives and lax.ppermute only.
A program may use at most 64 MiB of HBM per device.

v0:
```python
import math

import jax
import jax.numpy as jnp
from jax import lax
from jax.sharding import PartitionSpec as P

time_step = 0.25
diffusion_number = 0.16


def shifted(block, axis, distance):
    devices = range(lax.axis_size(axis))
    route = [(i - distance, i) for i in devices if i - distance in devices]
    return lax.ppermute(block, axis, route)


def with_halo(cells, sides, width):
    for axis, dim in sides:
        count = lax.axis_size(axis)
        ends = count - 1
        head = lax.slice_in_dim(cells, 0, width, axis=dim)
        tail = lax.slice_in_dim(cells, cells.shape[dim] - width, cells.shape[dim], axis=dim)
        cells = jnp.concatenate(
            [
                lax.ppermute(tail, axis, [(i, (i + 1) % count) for i in range(ends)]),
                cells,
                lax.ppermute(head, axis, [((i + 1) % count, i) for i in range(ends)]),
            ],
            axis=dim,
        )
    return cells


def network_rates(current, coupling, basal_rate, half_sat, decay_rate):
    square = current * current
    occupancy = square / (half_sat[:, None] * half_sat[:, None] + square)
    drive_sum = jnp.dot(
        coupling, occupancy, precision=lax.Precision.HIGHEST, preferred_element_type=jnp.float32
    )
    return basal_rate[:, None] + drive_sum - decay_rate[:, None] * current


def advance(current, coupling, basal_rate, half_sat, decay_rate):
    for substep in range(2):
        middle = current + 0.5 * time_step * network_rates(
            current, coupling, basal_rate, half_sat, decay_rate
        )
        current = current + time_step * network_rates(
            middle, coupling, basal_rate, half_sat, decay_rate
        )
    return current


def deposit_rows(weights, row_index, columns, row_count, column_count):
    block_size = math.gcd(weights.shape[0], 512)
    block_count = weights.shape[0] // block_size
    row_ids = jnp.arange(row_count, dtype=jnp.int32)
    column_ids = jnp.arange(column_count, dtype=jnp.int32)

    def one_block(running, block_turn):
        start = block_turn * block_size
        piece_weight = lax.dynamic_slice_in_dim(weights, start, block_size)
        piece_row = lax.dynamic_slice_in_dim(row_index, start, block_size)
        piece_column = lax.dynamic_slice_in_dim(columns, start, block_size)
        left_table = (piece_row[:, None] == row_ids[None, :]).astype(jnp.bfloat16)
        right_table = (piece_column[:, None] == column_ids[None, :]).astype(
            jnp.bfloat16
        ) * piece_weight[:, None]
        product = lax.dot_general(
            left_table, right_table, (((0,), (0,)), ((), ())), preferred_element_type=jnp.float32
        )
        return (running + product, None)

    running, unused = lax.scan(
        one_block, jnp.zeros((row_count, column_count), jnp.float32), jnp.arange(block_count)
    )
    return running


def sweep_once(padded):
    z_padded = jnp.pad(padded, ((1, 1), (0, 0), (0, 0)))
    center = padded[:, 1:-1, 1:-1]
    beside = z_padded[2:, 1:-1, 1:-1] + z_padded[:-2, 1:-1, 1:-1]
    beside = beside + padded[:, 2:, 1:-1] + padded[:, :-2, 1:-1]
    beside = beside + padded[:, 1:-1, 2:] + padded[:, 1:-1, :-2]
    return center + diffusion_number * (beside - 6.0 * center)


def shards(
    cell_state,
    coupling,
    basal_rate,
    half_sat,
    decay_rate,
    uptake_weight,
    agent_counts,
    divider_ids,
    destinations,
    voxel_index,
    oxygen,
):
    grid_count = lax.axis_size("gx")
    picks_count = divider_ids.shape[0]
    capacity = max(2, 2 * picks_count // grid_count)
    target_slab = destinations[:, 0]
    onehot = (target_slab[:, None] == jnp.arange(grid_count, dtype=jnp.int32)[None, :]).astype(
        jnp.int32
    )
    earlier = jnp.cumsum(onehot, axis=0) - onehot
    slot_rank = jnp.sum(earlier * onehot, axis=1)
    position = target_slab * capacity + slot_rank
    placing = (
        position[:, None] == jnp.arange(grid_count * capacity, dtype=jnp.int32)[None, :]
    ).astype(jnp.float32)
    mothers = jnp.take(cell_state, divider_ids, axis=1)
    outgoing = jnp.dot(
        mothers, placing, precision=lax.Precision.HIGHEST, preferred_element_type=jnp.float32
    )
    occupied = jnp.sum(placing, axis=0)[None, :]
    received, arrived = (
        lax.all_to_all(outgoing, "gx", split_axis=1, concat_axis=1, tiled=True),
        lax.all_to_all(occupied, "gx", split_axis=1, concat_axis=1, tiled=True),
    )
    new_state = advance(cell_state, coupling, basal_rate, half_sat, decay_rate)
    daughter_state = advance(received, coupling, basal_rate, half_sat, decay_rate) * arrived
    agents = cell_state.shape[1]
    drive_sum = jnp.dot(
        uptake_weight,
        new_state,
        precision=lax.Precision.HIGHEST,
        preferred_element_type=jnp.float32,
    )
    alive_mask = jnp.arange(agents, dtype=jnp.int32) < agent_counts[0]
    uptake = jnp.where(alive_mask, jax.nn.softplus(drive_sum), 0.0).astype(jnp.bfloat16)
    depth_cells, width_x, width_y = oxygen.shape
    slab_rows = depth_cells * width_x
    row_index = voxel_index // width_y
    columns = voxel_index % width_y
    partial_value = deposit_rows(uptake, row_index, columns, 3 * slab_rows, width_y).reshape(
        3, depth_cells, width_x, width_y
    )
    from_lower = shifted(partial_value[2].astype(jnp.bfloat16), "gx", 1).astype(jnp.float32)
    from_upper = shifted(partial_value[0].astype(jnp.bfloat16), "gx", -1).astype(jnp.float32)
    deposit = partial_value[1] + from_lower + from_upper
    oxygen_field = oxygen - deposit
    for sweep_turn in range(4):
        padded = with_halo(oxygen_field, (("gx", 1), ("gy", 2)), 1)
        oxygen_field = sweep_once(padded)
    return (new_state, daughter_state, oxygen_field)


def solution(mesh):
    return jax.shard_map(
        shards,
        mesh=mesh,
        in_specs=(
            P(None, ("gx", "gy")),
            P(),
            P(),
            P(),
            P(),
            P(),
            P(("gx", "gy")),
            P(("gx", "gy")),
            P(("gx", "gy"), None),
            P(("gx", "gy")),
            P(None, "gx", "gy"),
        ),
        out_specs=(P(None, ("gx", "gy")), P(None, ("gx", "gy")), P(None, "gx", "gy")),
        check_vma=False,
    )
```

profile of v0, /device:TPU:1, one launch (start us, length us, event | category | flops | bytes accessed | tf_op | source)
XLA Modules:
  0.0 136.2 jit_solution(7530949191528294205)
XLA Ops:
  1.4 1.7 %fusion.28 = f32[39,2048]{1,0:T(8,128)S(1)} fusion(f32[39,2048]{1,0:T(8,128)} %param.13, f32[39,39]{1,0:T(8,128)S(1)} %copy-done, f32[39]{0:T(128)} %param.17, f32[39]{0:T(128)S(1)} %mul.170, f32[39]{0:T(128)} %param.15), kind=kOutput, calls=%fused_computation.32 | convolution fusion | flops 38019072 | bytes 645528 | tf_op jit(solution)/shard_map/dot_general | solution.py:38
  6.1 12.0 %while.11 = (s32[]{:T(128)}, f32[1536,128]{1,0:T(8,128)S(1)}, s32[4]{0:T(128)S(1)}, s32[2048]{0:T(1024)S(1)}, s32[2048]{0:T(1024)S(1)}, /*index=5*/bf16[2048]{0:...) while((s32[]{:T(128)}, f32[1536,128]{1,0:T(8,128)S(1)}, s32[4]{0:T(128)S(1)}, ...), condition=%wide.region_4.5_spmd.clone, body=%wide.region_3.4_spmd.clone.sunk | while | flops 202637312 | bytes 1588405 | solution.py:75
  7.6 1.5 %fusion.127 = f32[1536,128]{1,0:T(8,128)S(1)} fusion(s32[512]{0:T(512)S(1)} %dynamic_slice.22, f32[1536,128]{1,0:T(8,128)S(1)} %get-tuple-element.151, pred[]{:T(512)S(6)} %compare.72, s32[512]{0:T(512)S(1)} %dynamic_slice.23, bf16[512]{0:T(512)(128)(2,1)S(1)} %dynamic_slice.24), kind=kOutput, calls=%fused_computation.5.clone.1 | convolution fusion | flops 202637312 | bytes 1577985 | tf_op jit(solution)/shard_map/while/body/eval_jaxpr/dot_general | solution.py:70
  10.6 1.5 %fusion.127 = f32[1536,128]{1,0:T(8,128)S(1)} fusion(s32[512]{0:T(512)S(1)} %dynamic_slice.22, f32[1536,128]{1,0:T(8,128)S(1)} %get-tuple-element.151, pred[]{:T(512)S(6)} %compare.72, s32[512]{0:T(512)S(1)} %dynamic_slice.23, bf16[512]{0:T(512)(128)(2,1)S(1)} %dynamic_slice.24), kind=kOutput, calls=%fused_computation.5.clone.1 | convolution fusion | flops 202637312 | bytes 1577985 | tf_op jit(solution)/shard_map/while/body/eval_jaxpr/dot_general | solution.py:70
  13.6 1.5 %fusion.127 = f32[1536,128]{1,0:T(8,128)S(1)} fusion(s32[512]{0:T(512)S(1)} %dynamic_slice.22, f32[1536,128]{1,0:T(8,128)S(1)} %get-tuple-element.151, pred[]{:T(512)S(6)} %compare.72, s32[512]{0:T(512)S(1)} %dynamic_slice.23, bf16[512]{0:T(512)(128)(2,1)S(1)} %dynamic_slice.24), kind=kOutput, calls=%fused_computation.5.clone.1 | convolution fusion | flops 202637312 | bytes 1577985 | tf_op jit(solution)/shard_map/while/body/eval_jaxpr/dot_general | solution.py:70
  16.6 1.5 %fusion.127 = f32[1536,128]{1,0:T(8,128)S(1)} fusion(s32[512]{0:T(512)S(1)} %dynamic_slice.22, f32[1536,128]{1,0:T(8,128)S(1)} %get-tuple-element.151, pred[]{:T(512)S(6)} %compare.72, s32[512]{0:T(512)S(1)} %dynamic_slice.23, bf16[512]{0:T(512)(128)(2,1)S(1)} %dynamic_slice.24), kind=kOutput, calls=%fused_computation.5.clone.1 | convolution fusion | flops 202637312 | bytes 1577985 | tf_op jit(solution)/shard_map/while/body/eval_jaxpr/dot_general | solution.py:70
  18.2 4.0 %collective-permute-start = (bf16[64,8,128]{2,1,0:T(8,128)(2,1)S(1)}, bf16[64,8,128]{2,1,0:T(8,128)(2,1)S(1)}, u32[]{:S(2)}, u32[]{:S(2)}) collective-permute-start(bf16[64,8,128]{2,1,0:T(8,128)(2,1)S(1)} %get-tuple-element.91), channel_id=1, source_target_pairs={{0,4},{4,8},{8,12},{12,16},{16,20},{20,24},{24,28},{1,5},{5,9},{9,... | collective-permute-start | bytes 393224 | tf_op jit(solution)/shard_map/ppermute | solution.py:15
  22.2 1.3 collective-permute-start.1
  24.7 6.4 %all-to-all-start.1 = ((f32[1,8,32]{2,0,1:T(1,128)}), f32[1,8,32]{2,0,1:T(1,128)S(1)}, u32[]{:S(2)}, u32[]{:S(2)}) async-start(f32[1,8,32]{2,0,1:T(1,128)} %all_to_all.17), calls=%async_computation.1 | async-start | bytes 8192 | tf_op jit(solution)/shard_map/all_to_all | solution.py:123
  31.3 3.4 %collective-permute-start.2 = (f32[64,1,128]{2,1,0:T(1,128)S(1)}, f32[64,1,128]{2,1,0:T(1,128)S(1)}, u32[]{:S(2)}, u32[]{:S(2)}) collective-permute-start(f32[64,1,128]{2,1,0:T(1,128)S(1)} %get-tuple-element.99), channel_id=1, source_target_pairs={{0,4},{4,8},{8,12},{12,16},{16,20},{20,24},{24,28},{1,5},{5,9},{9,... | collective-permute-start | bytes 98312 | tf_op jit(solution)/shard_map/ppermute | solution.py:26
  34.7 1.3 collective-permute-start.3
  36.0 3.3 %collective-permute-done.3 = f32[64,1,128]{2,1,0:T(1,128)S(1)} collective-permute-done((f32[64,1,128]{2,1,0:T(1,128)S(1)}, f32[64,1,128]{2,1,0:T(1,128)S(1)}, u32[]{:S(2)}, u32[]{:S(2)}) %collective-permute-start.3) | collective-permute-done | bytes 32800 | tf_op jit(solution)/shard_map/ppermute | solution.py:28
  39.4 1.0 fusion.110
  40.5 6.2 %collective-permute-start.4 = (f32[64,10,1]{2,1,0:T(8,128)}, f32[64,10,1]{2,1,0:T(8,128)S(1)}, u32[]{:S(2)}, u32[]{:S(2)}) collective-permute-start(f32[64,10,1]{2,1,0:T(8,128)} %get-tuple-element.90), channel_id=1, source_target_pairs={{0,1},{1,2},{2,3},{4,5},{5,6},{6,7},{8,9},{9,10},{10,11},{12,13},{... | collective-permute-start | bytes 7688 | tf_op jit(solution)/shard_map/ppermute | solution.py:26
  46.7 1.9 %collective-permute-start.5 = (f32[64,10,1]{2,1,0:T(8,128)S(1)}, f32[64,10,1]{2,1,0:T(8,128)S(1)}, u32[]{:S(2)}, u32[]{:S(2)}) collective-permute-start(f32[64,10,1]{2,1,0:T(8,128)S(1)} %get-tuple-element.89), channel_id=1, source_target_pairs={{1,0},{2,1},{3,2},{5,4},{6,5},{7,6},{9,8},{10,9},{11,10},{13,12},{... | collective-permute-start | bytes 7688 | tf_op jit(solution)/shard_map/ppermute | solution.py:28
  49.7 3.5 %collective-permute-done.4 = f32[64,10,1]{2,1,0:T(8,128)S(1)} collective-permute-done((f32[64,10,1]{2,1,0:T(8,128)}, f32[64,10,1]{2,1,0:T(8,128)S(1)}, u32[]{:S(2)}, u32[]{:S(2)}) %collective-permute-start.4) | collective-permute-done | bytes 2592 | tf_op jit(solution)/shard_map/ppermute | solution.py:26
  53.1 4.1 %collective-permute-done.5 = f32[64,10,1]{2,1,0:T(8,128)S(1)} collective-permute-done((f32[64,10,1]{2,1,0:T(8,128)S(1)}, f32[64,10,1]{2,1,0:T(8,128)S(1)}, u32[]{:S(2)}, u32[]{:S(2)}) %collective-permute-start.5) | collective-permute-done | bytes 2592 | tf_op jit(solution)/shard_map/ppermute | solution.py:28
  57.2 0.7 select_maximum_fusion.12
  57.9 1.3 fusion.75
  59.3 4.0 %collective-permute-start.6 = (f32[64,1,128]{2,1,0:T(1,128)S(1)}, f32[64,1,128]{2,1,0:T(1,128)S(1)}, u32[]{:S(2)}, u32[]{:S(2)}) collective-permute-start(f32[64,1,128]{2,1,0:T(1,128)S(1)} %get-tuple-element.97), channel_id=1, source_target_pairs={{0,4},{4,8},{8,12},{12,16},{16,20},{20,24},{24,28},{1,5},{5,9},{9,... | collective-permute-start | bytes 98312 | tf_op jit(solution)/shard_map/ppermute | solution.py:26
  63.3 1.3 collective-permute-start.7
  65.0 0.8 reshape.58
  65.8 2.2 %collective-permute-done.7 = f32[64,1,128]{2,1,0:T(1,128)S(1)} collective-permute-done((f32[64,1,128]{2,1,0:T(1,128)S(1)}, f32[64,1,128]{2,1,0:T(1,128)S(1)}, u32[]{:S(2)}, u32[]{:S(2)}) %collective-permute-start.7) | collective-permute-done | bytes 32800 | tf_op jit(solution)/shard_map/ppermute | solution.py:28
  68.1 4.3 %all-to-all-start = ((f32[8,1,1248]{2,1,0:T(1,128)}), f32[8,1,1248]{2,1,0:T(1,128)S(1)}, u32[]{:S(2)}, u32[]{:S(2)}) async-start(f32[8,1,1248]{2,1,0:T(1,128)} %reshape.58), calls=%async_computation | async-start | bytes 81920 | tf_op jit(solution)/shard_map/all_to_all | solution.py:122
  72.6 3.5 %collective-permute-start.8 = (f32[64,10,1]{2,1,0:T(8,128)S(1)}, f32[64,10,1]{2,1,0:T(8,128)S(1)}, u32[]{:S(2)}, u32[]{:S(2)}) collective-permute-start(f32[64,10,1]{2,1,0:T(8,128)S(1)} %get-tuple-element.88), channel_id=1, source_target_pairs={{0,1},{1,2},{2,3},{4,5},{5,6},{6,7},{8,9},{9,10},{10,11},{12,13},{... | collective-permute-start | bytes 7688 | tf_op jit(solution)/shard_map/ppermute | solution.py:26
  76.1 1.9 %collective-permute-start.9 = (f32[64,10,1]{2,1,0:T(8,128)S(1)}, f32[64,10,1]{2,1,0:T(8,128)S(1)}, u32[]{:S(2)}, u32[]{:S(2)}) collective-permute-start(f32[64,10,1]{2,1,0:T(8,128)S(1)} %get-tuple-element.87), channel_id=1, source_target_pairs={{1,0},{2,1},{3,2},{5,4},{6,5},{7,6},{9,8},{10,9},{11,10},{13,12},{... | collective-permute-start | bytes 7688 | tf_op jit(solution)/shard_map/ppermute | solution.py:28
  79.8 0.7 reduce.4
  80.8 1.4 %collective-permute-done.8 = f32[64,10,1]{2,1,0:T(8,128)S(1)} collective-permute-done((f32[64,10,1]{2,1,0:T(8,128)S(1)}, f32[64,10,1]{2,1,0:T(8,128)S(1)}, u32[]{:S(2)}, u32[]{:S(2)}) %collective-permute-start.8) | collective-permute-done | bytes 2592 | tf_op jit(solution)/shard_map/ppermute | solution.py:26
  82.2 4.4 %collective-permute-done.9 = f32[64,10,1]{2,1,0:T(8,128)S(1)} collective-permute-done((f32[64,10,1]{2,1,0:T(8,128)S(1)}, f32[64,10,1]{2,1,0:T(8,128)S(1)}, u32[]{:S(2)}, u32[]{:S(2)}) %collective-permute-start.9) | collective-permute-done | bytes 2592 | tf_op jit(solution)/shard_map/ppermute | solution.py:28
  86.6 0.7 select_maximum_fusion.8
  88.0 3.7 %collective-permute-start.10 = (f32[64,1,128]{2,1,0:T(1,128)S(1)}, f32[64,1,128]{2,1,0:T(1,128)S(1)}, u32[]{:S(2)}, u32[]{:S(2)}) collective-permute-start(f32[64,1,128]{2,1,0:T(1,128)S(1)} %get-tuple-element.95), channel_id=1, source_target_pairs={{0,4},{4,8},{8,12},{12,16},{16,20},{20,24},{24,28},{1,5},{5,9},{9,... | collective-permute-start | bytes 98312 | tf_op jit(solution)/shard_map/ppermute | solution.py:26
  91.7 1.3 collective-permute-start.11
  93.3 3.1 %collective-permute-done.11 = f32[64,1,128]{2,1,0:T(1,128)S(1)} collective-permute-done((f32[64,1,128]{2,1,0:T(1,128)S(1)}, f32[64,1,128]{2,1,0:T(1,128)S(1)}, u32[]{:S(2)}, u32[]{:S(2)}) %collective-permute-start.11) | collective-permute-done | bytes 32800 | tf_op jit(solution)/shard_map/ppermute | solution.py:28
  96.7 3.1 %collective-permute-start.12 = (f32[64,10,1]{2,1,0:T(8,128)S(1)}, f32[64,10,1]{2,1,0:T(8,128)S(1)}, u32[]{:S(2)}, u32[]{:S(2)}) collective-permute-start(f32[64,10,1]{2,1,0:T(8,128)S(1)} %get-tuple-element.86), channel_id=1, source_target_pairs={{0,1},{1,2},{2,3},{4,5},{5,6},{6,7},{8,9},{9,10},{10,11},{12,13},{... | collective-permute-start | bytes 7688 | tf_op jit(solution)/shard_map/ppermute | solution.py:26
  99.8 1.9 %collective-permute-start.13 = (f32[64,10,1]{2,1,0:T(8,128)S(1)}, f32[64,10,1]{2,1,0:T(8,128)S(1)}, u32[]{:S(2)}, u32[]{:S(2)}) collective-permute-start(f32[64,10,1]{2,1,0:T(8,128)S(1)} %get-tuple-element.85), channel_id=1, source_target_pairs={{1,0},{2,1},{3,2},{5,4},{6,5},{7,6},{9,8},{10,9},{11,10},{13,12},{... | collective-permute-start | bytes 7688 | tf_op jit(solution)/shard_map/ppermute | solution.py:28
  101.9 3.9 %collective-permute-done.12 = f32[64,10,1]{2,1,0:T(8,128)S(1)} collective-permute-done((f32[64,10,1]{2,1,0:T(8,128)S(1)}, f32[64,10,1]{2,1,0:T(8,128)S(1)}, u32[]{:S(2)}, u32[]{:S(2)}) %collective-permute-start.12) | collective-permute-done | bytes 2592 | tf_op jit(solution)/shard_map/ppermute | solution.py:26
  105.9 4.4 %collective-permute-done.13 = f32[64,10,1]{2,1,0:T(8,128)S(1)} collective-permute-done((f32[64,10,1]{2,1,0:T(8,128)S(1)}, f32[64,10,1]{2,1,0:T(8,128)S(1)}, u32[]{:S(2)}, u32[]{:S(2)}) %collective-permute-start.13) | collective-permute-done | bytes 2592 | tf_op jit(solution)/shard_map/ppermute | solution.py:28
  110.3 0.7 select_maximum_fusion.4
  111.6 4.1 %collective-permute-start.14 = (f32[64,1,128]{2,1,0:T(1,128)S(1)}, f32[64,1,128]{2,1,0:T(1,128)S(1)}, u32[]{:S(2)}, u32[]{:S(2)}) collective-permute-start(f32[64,1,128]{2,1,0:T(1,128)S(1)} %get-tuple-element.93), channel_id=1, source_target_pairs={{0,4},{4,8},{8,12},{12,16},{16,20},{20,24},{24,28},{1,5},{5,9},{9,... | collective-permute-start | bytes 98312 | tf_op jit(solution)/shard_map/ppermute | solution.py:26
  115.7 1.3 collective-permute-start.15
  117.3 3.1 %collective-permute-done.15 = f32[64,1,128]{2,1,0:T(1,128)S(1)} collective-permute-done((f32[64,1,128]{2,1,0:T(1,128)S(1)}, f32[64,1,128]{2,1,0:T(1,128)S(1)}, u32[]{:S(2)}, u32[]{:S(2)}) %collective-permute-start.15) | collective-permute-done | bytes 32800 | tf_op jit(solution)/shard_map/ppermute | solution.py:28
  120.6 3.1 %collective-permute-start.16 = (f32[64,10,1]{2,1,0:T(8,128)S(1)}, f32[64,10,1]{2,1,0:T(8,128)S(1)}, u32[]{:S(2)}, u32[]{:S(2)}) collective-permute-start(f32[64,10,1]{2,1,0:T(8,128)S(1)} %get-tuple-element.84), channel_id=1, source_target_pairs={{0,1},{1,2},{2,3},{4,5},{5,6},{6,7},{8,9},{9,10},{10,11},{12,13},{... | collective-permute-start | bytes 7688 | tf_op jit(solution)/shard_map/ppermute | solution.py:26
  123.7 1.9 %collective-permute-start.17 = (f32[64,10,1]{2,1,0:T(8,128)S(1)}, f32[64,10,1]{2,1,0:T(8,128)S(1)}, u32[]{:S(2)}, u32[]{:S(2)}) collective-permute-start(f32[64,10,1]{2,1,0:T(8,128)S(1)} %get-tuple-element.83), channel_id=1, source_target_pairs={{1,0},{2,1},{3,2},{5,4},{6,5},{7,6},{9,8},{10,9},{11,10},{13,12},{... | collective-permute-start | bytes 7688 | tf_op jit(solution)/shard_map/ppermute | solution.py:28
  125.7 0.9 fusion.33
  126.5 3.3 %collective-permute-done.16 = f32[64,10,1]{2,1,0:T(8,128)S(1)} collective-permute-done((f32[64,10,1]{2,1,0:T(8,128)S(1)}, f32[64,10,1]{2,1,0:T(8,128)S(1)}, u32[]{:S(2)}, u32[]{:S(2)}) %collective-permute-start.16) | collective-permute-done | bytes 2592 | tf_op jit(solution)/shard_map/ppermute | solution.py:26
  129.8 4.4 %collective-permute-done.17 = f32[64,10,1]{2,1,0:T(8,128)S(1)} collective-permute-done((f32[64,10,1]{2,1,0:T(8,128)S(1)}, f32[64,10,1]{2,1,0:T(8,128)S(1)}, u32[]{:S(2)}, u32[]{:S(2)}) %collective-permute-start.17) | collective-permute-done | bytes 2592 | tf_op jit(solution)/shard_map/ppermute | solution.py:28
  134.2 0.7 select_maximum_fusion
  135.0 1.3 fusion.54
  (94 shorter events, 14.0 us)
Async XLA Ops:
  0.6 0.8 copy-start
  0.6 2.5 %copy-start.2 = (f32[39,2048]{1,0:T(8,128)S(1)}, f32[39,2048]{1,0:T(8,128)}, u32[]{:S(2)}) copy-start(f32[39,2048]{1,0:T(8,128)} %param.13) | copy-start | bytes 958468
  0.7 2.5 %copy-start.11 = (f32[39]{0:T(128)S(1)}, f32[39]{0:T(128)}, u32[]{:S(2)}) copy-start(f32[39]{0:T(128)} %param.15) | copy-start | bytes 472
  0.7 2.5 %copy-start.10 = (f32[39]{0:T(128)S(1)}, f32[39]{0:T(128)}, u32[]{:S(2)}) copy-start(f32[39]{0:T(128)} %param.17) | copy-start | bytes 472
  4.4 1.3 copy-start.6
  4.4 1.3 copy-start.8
  5.0 1.0 copy-start.1
  18.1 5.4 %copy-start.7 = (s32[128,1]{0,1:T(1,128)S(1)}, s32[128,1]{0,1:T(1,128)}, u32[]{:S(2)}) copy-start(s32[128,1]{0,1:T(1,128)} %param.21) | copy-start | bytes 1540
  18.1 13.0 %copy-start.9 = (s32[128]{0:T(128)S(1)}, s32[128]{0:T(128)}, u32[]{:S(2)}) copy-start(s32[128]{0:T(128)} %param.20) | copy-start | bytes 1540
  18.1 13.1 %copy-start.5 = (f32[64,8,128]{2,1,0:T(8,128)S(1)}, f32[64,8,128]{2,1,0:T(8,128)}, u32[]{:S(2)}) copy-start(f32[64,8,128]{2,1,0:T(8,128)} %param.23) | copy-start | bytes 786436
  18.2 13.0 %collective-permute-start = (bf16[64,8,128]{2,1,0:T(8,128)(2,1)S(1)}, bf16[64,8,128]{2,1,0:T(8,128)(2,1)S(1)}, u32[]{:S(2)}, u32[]{:S(2)}) collective-permute-start(bf16[64,8,128]{2,1,0:T(8,128)(2,1)S(1)} %get-tuple-element.91), channel_id=1, source_target_pairs={{0,4},{4,8},{8,12},{12,16},{16,20},{20,24},{24,28},{1,5},{5,9},{9,... | collective-permute-start | bytes 393224 | tf_op jit(solution)/shard_map/ppermute | solution.py:15
  22.2 9.0 %collective-permute-start.1 = (bf16[64,8,128]{2,1,0:T(8,128)(2,1)S(1)}, bf16[64,8,128]{2,1,0:T(8,128)(2,1)S(1)}, u32[]{:S(2)}, u32[]{:S(2)}) collective-permute-start(bf16[64,8,128]{2,1,0:T(8,128)(2,1)S(1)} %get-tuple-element.92), channel_id=1, source_target_pairs={{4,0},{8,4},{12,8},{16,12},{20,16},{24,20},{28,24},{5,1},{9,5},{13... | collective-permute-start | bytes 393224 | tf_op jit(solution)/shard_map/ppermute | solution.py:15
  24.7 43.4 %all-to-all-start.1 = ((f32[1,8,32]{2,0,1:T(1,128)}), f32[1,8,32]{2,0,1:T(1,128)S(1)}, u32[]{:S(2)}, u32[]{:S(2)}) async-start(f32[1,8,32]{2,0,1:T(1,128)} %all_to_all.17), calls=%async_computation.1 | async-start | bytes 8192 | tf_op jit(solution)/shard_map/all_to_all | solution.py:123
  31.3 4.7 %collective-permute-start.2 = (f32[64,1,128]{2,1,0:T(1,128)S(1)}, f32[64,1,128]{2,1,0:T(1,128)S(1)}, u32[]{:S(2)}, u32[]{:S(2)}) collective-permute-start(f32[64,1,128]{2,1,0:T(1,128)S(1)} %get-tuple-element.99), channel_id=1, source_target_pairs={{0,4},{4,8},{8,12},{12,16},{16,20},{20,24},{24,28},{1,5},{5,9},{9,... | collective-permute-start | bytes 98312 | tf_op jit(solution)/shard_map/ppermute | solution.py:26
  34.7 4.7 %collective-permute-start.3 = (f32[64,1,128]{2,1,0:T(1,128)S(1)}, f32[64,1,128]{2,1,0:T(1,128)S(1)}, u32[]{:S(2)}, u32[]{:S(2)}) collective-permute-start(f32[64,1,128]{2,1,0:T(1,128)S(1)} %get-tuple-element.100), channel_id=1, source_target_pairs={{4,0},{8,4},{12,8},{16,12},{20,16},{24,20},{28,24},{5,1},{9,5},{13... | collective-permute-start | bytes 98312 | tf_op jit(solution)/shard_map/ppermute | solution.py:28
  39.3 17.9 %copy-start.4 = (f32[64,1,128]{2,1,0:T(1,128)}, f32[64,1,128]{2,1,0:T(1,128)S(1)}, u32[]{:S(2)}) copy-start(f32[64,1,128]{2,1,0:T(1,128)S(1)} %collective-permute-done.3) | copy-start | bytes 98308
  39.4 9.2 %copy-start.3 = (f32[39,2048]{1,0:T(8,128)S(1)}, f32[39,2048]{1,0:T(8,128)}, u32[]{:S(2)}) copy-start(f32[39,2048]{1,0:T(8,128)} %param.13) | copy-start | bytes 958468
  40.5 12.6 %collective-permute-start.4 = (f32[64,10,1]{2,1,0:T(8,128)}, f32[64,10,1]{2,1,0:T(8,128)S(1)}, u32[]{:S(2)}, u32[]{:S(2)}) collective-permute-start(f32[64,10,1]{2,1,0:T(8,128)} %get-tuple-element.90), channel_id=1, source_target_pairs={{0,1},{1,2},{2,3},{4,5},{5,6},{6,7},{8,9},{9,10},{10,11},{12,13},{... | collective-permute-start | bytes 7688 | tf_op jit(solution)/shard_map/ppermute | solution.py:26
  46.7 10.5 %collective-permute-start.5 = (f32[64,10,1]{2,1,0:T(8,128)S(1)}, f32[64,10,1]{2,1,0:T(8,128)S(1)}, u32[]{:S(2)}, u32[]{:S(2)}) collective-permute-start(f32[64,10,1]{2,1,0:T(8,128)S(1)} %get-tuple-element.89), channel_id=1, source_target_pairs={{1,0},{2,1},{3,2},{5,4},{6,5},{7,6},{9,8},{10,9},{11,10},{13,12},{... | collective-permute-start | bytes 7688 | tf_op jit(solution)/shard_map/ppermute | solution.py:28
  59.3 6.4 %collective-permute-start.6 = (f32[64,1,128]{2,1,0:T(1,128)S(1)}, f32[64,1,128]{2,1,0:T(1,128)S(1)}, u32[]{:S(2)}, u32[]{:S(2)}) collective-permute-start(f32[64,1,128]{2,1,0:T(1,128)S(1)} %get-tuple-element.97), channel_id=1, source_target_pairs={{0,4},{4,8},{8,12},{12,16},{16,20},{20,24},{24,28},{1,5},{5,9},{9,... | collective-permute-start | bytes 98312 | tf_op jit(solution)/shard_map/ppermute | solution.py:26
  63.3 4.7 %collective-permute-start.7 = (f32[64,1,128]{2,1,0:T(1,128)S(1)}, f32[64,1,128]{2,1,0:T(1,128)S(1)}, u32[]{:S(2)}, u32[]{:S(2)}) collective-permute-start(f32[64,1,128]{2,1,0:T(1,128)S(1)} %get-tuple-element.98), channel_id=1, source_target_pairs={{4,0},{8,4},{12,8},{16,12},{20,16},{24,20},{28,24},{5,1},{9,5},{13... | collective-permute-start | bytes 98312 | tf_op jit(solution)/shard_map/ppermute | solution.py:28
  68.1 11.2 %all-to-all-start = ((f32[8,1,1248]{2,1,0:T(1,128)}), f32[8,1,1248]{2,1,0:T(1,128)S(1)}, u32[]{:S(2)}, u32[]{:S(2)}) async-start(f32[8,1,1248]{2,1,0:T(1,128)} %reshape.58), calls=%async_computation | async-start | bytes 81920 | tf_op jit(solution)/shard_map/all_to_all | solution.py:122
  72.6 9.6 %collective-permute-start.8 = (f32[64,10,1]{2,1,0:T(8,128)S(1)}, f32[64,10,1]{2,1,0:T(8,128)S(1)}, u32[]{:S(2)}, u32[]{:S(2)}) collective-permute-start(f32[64,10,1]{2,1,0:T(8,128)S(1)} %get-tuple-element.88), channel_id=1, source_target_pairs={{0,1},{1,2},{2,3},{4,5},{5,6},{6,7},{8,9},{9,10},{10,11},{12,13},{... | collective-permute-start | bytes 7688 | tf_op jit(solution)/shard_map/ppermute | solution.py:26
  76.1 10.5 %collective-permute-start.9 = (f32[64,10,1]{2,1,0:T(8,128)S(1)}, f32[64,10,1]{2,1,0:T(8,128)S(1)}, u32[]{:S(2)}, u32[]{:S(2)}) collective-permute-start(f32[64,10,1]{2,1,0:T(8,128)S(1)} %get-tuple-element.87), channel_id=1, source_target_pairs={{1,0},{2,1},{3,2},{5,4},{6,5},{7,6},{9,8},{10,9},{11,10},{13,12},{... | collective-permute-start | bytes 7688 | tf_op jit(solution)/shard_map/ppermute | solution.py:28
  88.0 5.3 %collective-permute-start.10 = (f32[64,1,128]{2,1,0:T(1,128)S(1)}, f32[64,1,128]{2,1,0:T(1,128)S(1)}, u32[]{:S(2)}, u32[]{:S(2)}) collective-permute-start(f32[64,1,128]{2,1,0:T(1,128)S(1)} %get-tuple-element.95), channel_id=1, source_target_pairs={{0,4},{4,8},{8,12},{12,16},{16,20},{20,24},{24,28},{1,5},{5,9},{9,... | collective-permute-start | bytes 98312 | tf_op jit(solution)/shard_map/ppermute | solution.py:26
  91.7 4.7 %collective-permute-start.11 = (f32[64,1,128]{2,1,0:T(1,128)S(1)}, f32[64,1,128]{2,1,0:T(1,128)S(1)}, u32[]{:S(2)}, u32[]{:S(2)}) collective-permute-start(f32[64,1,128]{2,1,0:T(1,128)S(1)} %get-tuple-element.96), channel_id=1, source_target_pairs={{4,0},{8,4},{12,8},{16,12},{20,16},{24,20},{28,24},{5,1},{9,5},{13... | collective-permute-start | bytes 98312 | tf_op jit(solution)/shard_map/ppermute | solution.py:28
  96.7 9.2 %collective-permute-start.12 = (f32[64,10,1]{2,1,0:T(8,128)S(1)}, f32[64,10,1]{2,1,0:T(8,128)S(1)}, u32[]{:S(2)}, u32[]{:S(2)}) collective-permute-start(f32[64,10,1]{2,1,0:T(8,128)S(1)} %get-tuple-element.86), channel_id=1, source_target_pairs={{0,1},{1,2},{2,3},{4,5},{5,6},{6,7},{8,9},{9,10},{10,11},{12,13},{... | collective-permute-start | bytes 7688 | tf_op jit(solution)/shard_map/ppermute | solution.py:26
  99.8 10.5 %collective-permute-start.13 = (f32[64,10,1]{2,1,0:T(8,128)S(1)}, f32[64,10,1]{2,1,0:T(8,128)S(1)}, u32[]{:S(2)}, u32[]{:S(2)}) collective-permute-start(f32[64,10,1]{2,1,0:T(8,128)S(1)} %get-tuple-element.85), channel_id=1, source_target_pairs={{1,0},{2,1},{3,2},{5,4},{6,5},{7,6},{9,8},{10,9},{11,10},{13,12},{... | collective-permute-start | bytes 7688 | tf_op jit(solution)/shard_map/ppermute | solution.py:28
  111.6 5.6 %collective-permute-start.14 = (f32[64,1,128]{2,1,0:T(1,128)S(1)}, f32[64,1,128]{2,1,0:T(1,128)S(1)}, u32[]{:S(2)}, u32[]{:S(2)}) collective-permute-start(f32[64,1,128]{2,1,0:T(1,128)S(1)} %get-tuple-element.93), channel_id=1, source_target_pairs={{0,4},{4,8},{8,12},{12,16},{16,20},{20,24},{24,28},{1,5},{5,9},{9,... | collective-permute-start | bytes 98312 | tf_op jit(solution)/shard_map/ppermute | solution.py:26
  115.7 4.7 %collective-permute-start.15 = (f32[64,1,128]{2,1,0:T(1,128)S(1)}, f32[64,1,128]{2,1,0:T(1,128)S(1)}, u32[]{:S(2)}, u32[]{:S(2)}) collective-permute-start(f32[64,1,128]{2,1,0:T(1,128)S(1)} %get-tuple-element.94), channel_id=1, source_target_pairs={{4,0},{8,4},{12,8},{16,12},{20,16},{24,20},{28,24},{5,1},{9,5},{13... | collective-permute-start | bytes 98312 | tf_op jit(solution)/shard_map/ppermute | solution.py:28
  120.6 9.2 %collective-permute-start.16 = (f32[64,10,1]{2,1,0:T(8,128)S(1)}, f32[64,10,1]{2,1,0:T(8,128)S(1)}, u32[]{:S(2)}, u32[]{:S(2)}) collective-permute-start(f32[64,10,1]{2,1,0:T(8,128)S(1)} %get-tuple-element.84), channel_id=1, source_target_pairs={{0,1},{1,2},{2,3},{4,5},{5,6},{6,7},{8,9},{9,10},{10,11},{12,13},{... | collective-permute-start | bytes 7688 | tf_op jit(solution)/shard_map/ppermute | solution.py:26
  123.7 10.5 %collective-permute-start.17 = (f32[64,10,1]{2,1,0:T(8,128)S(1)}, f32[64,10,1]{2,1,0:T(8,128)S(1)}, u32[]{:S(2)}, u32[]{:S(2)}) collective-permute-start(f32[64,10,1]{2,1,0:T(8,128)S(1)} %get-tuple-element.83), channel_id=1, source_target_pairs={{1,0},{2,1},{3,2},{5,4},{6,5},{7,6},{9,8},{10,9},{11,10},{13,12},{... | collective-permute-start | bytes 7688 | tf_op jit(solution)/shard_map/ppermute | solution.py:28
where the time goes:
time: 137 us; the launch traced here: 136 us
  starting transfers between devices  59.8 us (44%)
  waiting for transfers between devices  41.1 us (30%)
  matrix products  11.8 us (9%)
  other arithmetic  9.87 us (7%)
  local copies, waits for them, and re-layouts  8.97 us (7%)
  loops' own time  2.72 us (2%)
  between operations  1.92 us (1%)
    ppermute x8, starting transfers between devices, with_halo(): lax.ppermute(tail, axis, [(i, (i + 1) % count) for i in range(ends)])  31 us
    ppermute x8, waiting for transfers between devices, with_halo(): lax.ppermute(head, axis, [((i + 1) % count, i) for i in range(ends)])  29 us
    ppermute x8, starting transfers between devices, with_halo(): lax.ppermute(head, axis, [((i + 1) % count, i) for i in range(ends)])  12.9 us
    ppermute x8, waiting for transfers between devices, with_halo(): lax.ppermute(tail, axis, [(i, (i + 1) % count) for i in range(ends)])  12.1 us
    all_to_all x1, starting transfers between devices, shards(): lax.all_to_all(occupied, 'gx', split_axis=1, concat_axis=1, tiled=True)  6.4 us
    dot_general x4, matrix products, one_block(): lax.dot_general(left_table, right_table, (((0,), (0,)), ((), ())), prefer...  6.01 us
    ppermute x2, starting transfers between devices, shifted(): return lax.ppermute(block, axis, route)  5.28 us
    dot_general x8, matrix products, network_rates(): jnp.dot(coupling, occupancy, precision=lax.Precision.HIGHEST, preferred_e...  5.17 us
  transfers between devices with their start and end apart: 20, of which 12 were waited for; matrix products, arithmetic and copies ran while one was open for 8% of the time, Pallas kernels for 0%

commit v1 on v0

v1 whole, which is shorter than its diff:
```python
import jax
import jax.numpy as jnp
from jax import lax
from jax.experimental import pallas as pl
from jax.experimental.pallas import tpu as pltpu
from jax.sharding import PartitionSpec as P

time_step = 0.25
diffusion_number = 0.16
sweeps = 4
GRID = ("gx", "gy")
LANES = 128
EXACT = lax.Precision.HIGHEST
f32, bf16, i32 = jnp.float32, jnp.bfloat16, jnp.int32
VMEM_LIMIT = 48 << 20


def full(shape):
    return pl.BlockSpec(shape, lambda: (0,) * len(shape))


def call(body, outs, name, inputs, smem=(), scratch=()):
    specs = [
        pl.BlockSpec(memory_space=pltpu.SMEM) if at in smem else full(value.shape)
        for at, value in enumerate(inputs)
    ]
    return pl.pallas_call(
        body,
        out_shape=tuple(jax.ShapeDtypeStruct(s, t) for s, t in outs),
        in_specs=specs,
        out_specs=tuple(full(s) for s, t in outs),
        scratch_shapes=scratch,
        compiler_params=pltpu.CompilerParams(vmem_limit_bytes=VMEM_LIMIT),
        name=name,
    )(*inputs)


def swap_pairs(grid_count, row_count, partner):
    pairs = []
    for g in range(grid_count):
        for h in range(row_count):
            p, q = partner(g, h)
            if not (0 <= p < grid_count and 0 <= q < row_count):
                p, q = g, h ^ 1
            pairs.append((g * row_count + h, p * row_count + q))
    return pairs


def near_even(g, h):
    return g ^ 1, h


def near_odd(g, h):
    return (g + 1 if g % 2 else g - 1), h


def far_even(g, h):
    return g ^ 2, h


def far_odd(g, h):
    return (g + 2 if g & 2 else g - 2), h


def side_even(g, h):
    return g, h ^ 1


def column(row, count):
    shape = (count, count)
    same = lax.broadcasted_iota(i32, shape, 0) == lax.broadcasted_iota(i32, shape, 1)
    return jnp.sum(jnp.where(same, jnp.broadcast_to(row, shape), 0), axis=1, keepdims=True)


def advance_kernel(
    count_ref, cell, coupling, basal, half, decay, weight, voxel, oxygen,
    new_state, message_even, message_odd, message_far, drive, *, cy, cx, nz,
):
    species, agents = cell.shape
    basal_c, half_c, decay_c, weight_c = (column(r[...], species) for r in (basal, half, decay, weight))
    half_square = half_c * half_c
    matrix = coupling[...]

    def rates(current):
        square = current * current
        occupancy = square / (half_square + square)
        product = jnp.dot(matrix, occupancy, precision=EXACT, preferred_element_type=f32)
        return basal_c + product - decay_c * current

    current = cell[...]
    for substep in range(2):
        middle = current + (0.5 * time_step) * rates(current)
        current = current + time_step * rates(middle)
    new_state[...] = current
    total = jnp.sum(weight_c * current, axis=0, keepdims=True)
    rows = agents // LANES
    for c in range(rows):
        drive[c : c + 1, :] = total[:, c * LANES : (c + 1) * LANES]
    x = drive[...]
    soft = jnp.maximum(x, 0.0) + jnp.log1p(jnp.exp(-jnp.abs(x)))
    slot = lax.broadcasted_iota(i32, (rows, LANES), 0) * LANES + lax.broadcasted_iota(i32, (rows, LANES), 1)
    uptake = jnp.where(slot < count_ref[0], soft, 0.0)
    code = voxel[...]
    at_y = code % cy
    at_x = (code // cy) % cx
    at_z = (code // (cy * cx)) % nz
    slab_x = (code // (cy * cx * nz)) * cx + at_x + cx // 2
    row = at_z * cx + slab_x % cx - nz * cx // 2
    col = (slab_x // cx) * cy + at_y - 2 * cy
    listing = jnp.concatenate([uptake, row.astype(f32), col.astype(f32)], axis=0).astype(bf16)
    own = oxygen[...] - 1.0
    turned = pltpu.roll(own, cx // 2, 1)
    low = lax.broadcasted_iota(i32, (nz // 2, cx, cy), 1) < cx // 2
    a, b = own[: nz // 2], own[nz // 2 :]
    ta, tb = turned[: nz // 2], turned[nz // 2 :]
    upper = jnp.where(low, ta, b)
    lower = jnp.where(low, a, tb)
    even = lax.axis_index("gx") % 2 == 0
    to_next = upper.reshape(nz // 2 * cx, cy)
    to_previous = lower.reshape(nz // 2 * cx, cy)
    head = nz // 2 * cx
    message_even[:head, :] = jnp.where(even, to_next, to_previous).astype(bf16)
    message_odd[:head, :] = jnp.where(even, to_previous, to_next).astype(bf16)
    message_even[head:, :] = listing
    message_odd[head:, :] = listing
    message_far[...] = listing


def deposit_kernel(
    oxygen, own_list, near_e, near_o, far_e, far_o, field, strips, strip_even, strip_odd,
    lists, total, *, grid_count,
):
    nz, cx, cy = oxygen.shape
    half = cx // 2
    head = nz // 2 * cx
    rows = own_list.shape[0] // 3
    g = lax.axis_index("gx")
    even = g % 2 == 0
    low_pair = g % 4 < 2
    has_next, has_previous = g + 1 < grid_count, g >= 1
    has_next2, has_previous2 = g + 2 < grid_count, g >= 2

    def keep(listing, valid):
        wide = listing.astype(f32)
        index = lax.broadcasted_iota(i32, wide.shape, 0)
        return jnp.where((index < rows) & jnp.logical_not(valid), 0.0, wide)

    e, o = near_e[...].astype(f32), near_o[...].astype(f32)
    after, before = jnp.where(even, e, o), jnp.where(even, o, e)
    fe, fo = far_e[...].astype(f32), far_o[...].astype(f32)
    lists[0] = own_list[...].astype(f32)
    lists[1] = keep(after[head:], has_next)
    lists[2] = keep(before[head:], has_previous)
    lists[3] = keep(jnp.where(low_pair, fe, fo), has_next2)
    lists[4] = keep(jnp.where(low_pair, fo, fe), has_previous2)
    chunk = 2 if rows % 2 == 0 else 1
    m = nz * cx
    row_at = (lax.broadcasted_iota(i32, (m, LANES), 0) - m // 2).astype(f32)
    col_at = lax.broadcasted_iota(i32, (2 * cy, LANES), 0).astype(f32)
    plan = ((0, -cy, 0, 2), (1, -2 * cy, 0, 2), (2, 0, 0, 2), (3, -2 * cy, 1, 2), (4, cy, 0, 1))
    total[...] = jnp.zeros_like(total)

    def block(turn, carry):
        for which, base, first, last in plan:
            width = (last - first) * cy
            lefts, rights = [], []
            for part in range(chunk):
                at = turn * chunk + part
                weight = lists[which, pl.ds(at, 1), :]
                row = lists[which, pl.ds(rows + at, 1), :]
                col = lists[which, pl.ds(2 * rows + at, 1), :]
                lefts.append(jnp.where(row_at == row, 1.0, 0.0).astype(bf16))
                rights.append(jnp.where(col_at[:width] + base == col, weight, 0.0).astype(bf16))
            left = jnp.concatenate(lefts, axis=1)
            right = jnp.concatenate(rights, axis=1)
            total[:, first * cy : last * cy] += lax.dot_general(
                left, right, (((1,), (1,)), ((), ())), preferred_element_type=f32
            )
        return carry

    lax.fori_loop(0, rows // chunk, block, 0)

    low = lax.broadcasted_iota(i32, (nz // 2, cx, cy), 1) < half
    inner = pltpu.roll(oxygen[...], half, 1)
    from_before = jnp.where(has_previous, before[:head] + 1.0, 0.0).reshape(nz // 2, cx, cy)
    from_after = jnp.where(has_next, after[:head] + 1.0, 0.0).reshape(nz // 2, cx, cy)
    before_b = pltpu.roll(from_before, half, 1)
    after_a, after_b = pltpu.roll(from_after, half, 1), from_after
    zh = nz // 2
    field[0, :zh] = jnp.where(low, from_before, inner[:zh]) - total[: head, :cy].reshape(zh, cx, cy)
    field[0, zh:] = jnp.where(low, before_b, inner[zh:]) - total[head:, :cy].reshape(zh, cx, cy)
    field[1, :zh] = jnp.where(low, inner[:zh], after_a) - total[: head, cy:].reshape(zh, cx, cy)
    field[1, zh:] = jnp.where(low, inner[zh:], after_b) - total[head:, cy:].reshape(zh, cx, cy)

    edge = 2 * sweeps
    picked = lax.broadcasted_iota(i32, (2 * edge, cy), 0)
    picked = jnp.where(picked < edge, picked, picked + cy - 2 * edge)
    picker = (picked == lax.broadcasted_iota(i32, (2 * edge, cy), 1)).astype(f32)
    for tile in range(2):
        flat = field[tile].reshape(m, cy)
        strips[:, tile * m : (tile + 1) * m] = lax.dot_general(
            picker, flat, (((1,), (1,)), ((), ())), precision=EXACT, preferred_element_type=f32
        )
    h_even = lax.axis_index("gy") % 2 == 0
    head_rows, tail_rows = strips[:sweeps, :], strips[2 * edge - sweeps :, :]
    strip_even[...] = jnp.where(h_even, tail_rows, head_rows)
    strip_odd[...] = jnp.where(h_even, head_rows, tail_rows)


def sweep_kernel(field, strips, got_even, got_odd, out, ping, pong, *, grid_count, row_count):
    two, nz, cx, cy = field.shape
    half = cx // 2
    m = nz * cx
    g, h = lax.axis_index("gx"), lax.axis_index("gy")
    h_even = h % 2 == 0
    keep_self = 1.0 - 6.0 * diffusion_number
    sub = lax.broadcasted_iota(i32, (cx, cy), 0)
    mask0 = jnp.where((g == 0) & (sub < half), 0.0, 1.0)
    mask1 = jnp.where((g == grid_count - 1) & (sub >= half), 0.0, 1.0)
    first_row, last_row = sub == 0, sub == cx - 1

    zero = jnp.zeros((cx, cy), f32)
    for buffer in (ping, pong):
        for tile in range(2):
            buffer[tile, 0] = zero
            buffer[tile, nz + 1] = zero
    ping[:, 1 : nz + 1] = field[...]

    def one_sweep(source, target):
        def plane(z, carry):
            c0, c1 = source[0, z], source[1, z]
            b0, b1 = source[0, z - 1] + source[0, z + 1], source[1, z - 1] + source[1, z + 1]
            d0, d1 = pltpu.roll(c0, cx - 1, 0), pltpu.roll(c1, cx - 1, 0)
            u0, u1 = pltpu.roll(c0, 1, 0), pltpu.roll(c1, 1, 0)
            b0 = b0 + jnp.where(last_row, d1, d0) + u0
            b1 = b1 + d1 + jnp.where(first_row, u0, u1)
            b0 = b0 + pltpu.roll(c0, 1, 1) + pltpu.roll(c0, cy - 1, 1)
            b1 = b1 + pltpu.roll(c1, 1, 1) + pltpu.roll(c1, cy - 1, 1)
            target[0, z] = (c0 + diffusion_number * (b0 - 6.0 * c0)) * mask0
            target[1, z] = (c1 + diffusion_number * (b1 - 6.0 * c1)) * mask1
            return carry

        lax.fori_loop(1, nz + 1, plane, 0, unroll=8)

    for turn in range(sweeps):
        one_sweep(*((ping, pong) if turn % 2 == 0 else (pong, ping)))
    main = ping if sweeps % 2 == 0 else pong

    edge = 2 * sweeps
    has_right, has_left = h + 1 < row_count, h >= 1
    a, b = got_even[...], got_odd[...]
    right = jnp.where(has_right, jnp.where(h_even, a, b), 0.0)
    left = jnp.where(has_left, jnp.where(h_even, b, a), 0.0)
    own = strips[...]
    band = jnp.concatenate([left, own, right], axis=0)
    count = band.shape[0]
    lane = lax.broadcasted_iota(i32, (count, m), 1)
    line = lax.broadcasted_iota(i32, (count, m), 0)
    outside = (line < sweeps) & jnp.logical_not(has_left) | (line >= count - sweeps) & jnp.logical_not(has_right)
    at_x = lane % cx
    on0 = jnp.where(outside | ((g == 0) & (at_x < half)), 0.0, 1.0)
    on1 = jnp.where(outside | ((g == grid_count - 1) & (at_x >= half)), 0.0, 1.0)
    x_first, x_last = at_x == 0, at_x == cx - 1
    z_first, z_last = lane < cx, lane >= m - cx
    s0, s1 = band[:, :m], band[:, m:]

    def beside(s):
        up = jnp.where(z_first, 0.0, pltpu.roll(s, cx, 1))
        down = jnp.where(z_last, 0.0, pltpu.roll(s, m - cx, 1))
        return up + down + pltpu.roll(s, 1, 0) + pltpu.roll(s, count - 1, 0)

    for turn in range(sweeps):
        n0 = jnp.where(x_last, pltpu.roll(s1, cx - 1, 1), pltpu.roll(s0, m - 1, 1)) + pltpu.roll(s0, 1, 1)
        n1 = pltpu.roll(s1, m - 1, 1) + jnp.where(x_first, pltpu.roll(s0, m - cx + 1, 1), pltpu.roll(s1, 1, 1))
        n0, n1 = n0 + beside(s0), n1 + beside(s1)
        s0 = (s0 + diffusion_number * (n0 - 6.0 * s0)) * on0
        s1 = (s1 + diffusion_number * (n1 - 6.0 * s1)) * on1
    mixed = jnp.where(at_x < half, s1, s0)
    final = jnp.concatenate([mixed[sweeps : 2 * sweeps], mixed[count - 2 * sweeps : count - sweeps]], axis=0)
    placed = lax.broadcasted_iota(i32, (edge, cy), 0)
    placed = jnp.where(placed < sweeps, placed, placed + cy - edge)
    placer = (placed == lax.broadcasted_iota(i32, (edge, cy), 1)).astype(f32)
    edges = lax.dot_general(
        final, placer, (((0,), (0,)), ((), ())), precision=EXACT, preferred_element_type=f32
    ).reshape(nz, cx, cy)
    shape = (nz, cx, cy)
    at_y = lax.broadcasted_iota(i32, shape, 2)
    low = lax.broadcasted_iota(i32, shape, 1) < half
    inside = jnp.where(low, main[1, 1 : nz + 1], main[0, 1 : nz + 1])
    merged = jnp.where((at_y < sweeps) | (at_y >= cy - sweeps), edges, inside)
    out[...] = pltpu.roll(merged, half, 1)


def pieces(value):
    high = value.astype(bf16)
    rest = value - high.astype(f32)
    middle = rest.astype(bf16)
    return high, middle, (rest - middle.astype(f32)).astype(bf16)


def part_shape(columns, capacity, step):
    return capacity * step


def first_send(buffer, mine, width):
    count = buffer.shape[1]
    half = count // 2
    left, right = buffer[:, :half], buffer[:, half:]
    if width == half:
        return jnp.where(mine, left, right)
    bit = (lax.broadcasted_iota(i32, left.shape, 1) // width) % 2 == 1
    moved = jnp.where(mine, pltpu.roll(right, width, 1), pltpu.roll(right, half - width, 1))
    return jnp.where(jnp.logical_xor(bit, mine), left, moved)


def take_in(buffer, got, mine, width):
    count = buffer.shape[1]
    half = count // 2
    left, right = buffer[:, :half], buffer[:, half:]
    if width == half:
        left, right = jnp.where(mine, got, left), jnp.where(mine, right, got)
    else:
        bit = (lax.broadcasted_iota(i32, left.shape, 1) // width) % 2 == 1
        other = jnp.logical_xor(bit, mine)
        moved = jnp.where(mine, pltpu.roll(got, half - width, 1), pltpu.roll(got, width, 1))
        left, right = jnp.where(other, moved, left), jnp.where(other, got, right)
    return jnp.concatenate([left, right], axis=1)


def daughter_kernel(state, ids, targets, buffer, send, *, capacity, step):
    species, agents = state.shape
    picks = ids.shape[1]
    columns = buffer.shape[1]
    target = targets[...]
    square = (picks, picks)
    across = jnp.broadcast_to(target, square)
    down = jnp.broadcast_to(column(target, picks), square)
    earlier = lax.broadcasted_iota(i32, square, 0) < lax.broadcasted_iota(i32, square, 1)
    rank = jnp.sum(jnp.where((across == down) & earlier, 1, 0), axis=0, keepdims=True)
    position = target * capacity + rank
    chosen = (lax.broadcasted_iota(i32, (agents, picks), 0) == ids[...]).astype(f32).astype(bf16)
    mothers = sum(jnp.dot(p, chosen, preferred_element_type=f32) for p in pieces(state[...]))
    placing = (lax.broadcasted_iota(i32, (columns, picks), 0) == position).astype(f32).astype(bf16)
    placed = sum(
        lax.dot_general(p, placing, (((1,), (1,)), ((), ())), preferred_element_type=f32)
        for p in pieces(mothers)
    )
    buffer[...] = placed
    mine = (lax.axis_index("gx") // step) % 2 == 1
    send[...] = first_send(placed, mine, capacity * step)


def relay_kernel(buffer, got, merged, *send, capacity, step, after):
    g = lax.axis_index("gx")
    value = take_in(buffer[...], got[...], (g // step) % 2 == 1, capacity * step)
    merged[...] = value
    if after:
        send[0][...] = first_send(value, (g // after) % 2 == 1, capacity * after)


def solution(mesh):
    grid_count, row_count = mesh.shape["gx"], mesh.shape["gy"]

    def swap(value, partner):
        return lax.ppermute(value, GRID, swap_pairs(grid_count, row_count, partner))

    def side_odd(g, h):
        p = h + 1 if h % 2 else h - 1
        return (g, p) if 0 <= p < row_count else (g, h ^ (row_count - 1))

    def shards(
        cell_state, coupling, basal_rate, half_sat, decay_rate, uptake_weight,
        agent_counts, divider_ids, destinations, voxel_index, oxygen,
    ):
        species, agents = cell_state.shape
        nz, cx, cy = oxygen.shape
        picks = divider_ids.shape[0]
        rows = agents // LANES
        head = nz // 2 * cx
        capacity = max(2, 2 * picks // grid_count)
        columns = grid_count * capacity

        def line(value):
            return value.reshape(1, -1)

        def kernel(body, **sizes):
            def run(*refs):
                return body(*refs, **sizes)

            return run

        new_state, message_even, message_odd, listing = call(
            kernel(advance_kernel, cy=cy, cx=cx, nz=nz),
            [((species, agents), f32), ((head + 3 * rows, LANES), bf16), ((head + 3 * rows, LANES), bf16),
             ((3 * rows, LANES), bf16)],
            "advance",
            [agent_counts, cell_state, coupling, line(basal_rate), line(half_sat), line(decay_rate),
             line(uptake_weight), voxel_index.reshape(rows, LANES), oxygen],
            smem=(0,),
            scratch=[pltpu.VMEM((rows, LANES), f32)],
        )
        near_e = swap(message_even, near_even)
        near_o = swap(message_odd, near_odd)
        far_e = swap(listing, far_even)
        far_o = swap(listing, far_odd)

        step = grid_count // 2
        buffer, send = call(
            kernel(daughter_kernel, capacity=capacity, step=step),
            [((species, columns), f32), ((species, columns // 2), f32)],
            "daughters",
            [new_state, line(divider_ids), line(destinations)],
        )

        m = nz * cx
        field, strips, strip_even, strip_odd = call(
            kernel(deposit_kernel, grid_count=grid_count),
            [((2, nz, cx, cy), f32), ((4 * sweeps, 2 * m), f32), ((sweeps, 2 * m), f32), ((sweeps, 2 * m), f32)],
            "deposit",
            [oxygen, listing, near_e, near_o, far_e, far_o],
            scratch=[pltpu.VMEM((5, 3 * rows, LANES), f32), pltpu.VMEM((m, 2 * cy), f32)],
        )
        got_even = swap(strip_even, side_even)
        got_odd = swap(strip_odd, side_odd)

        while step:
            after = step // 2
            got = swap(send, lambda g, h: (g ^ step, h))
            outs = [((species, columns), f32)] + ([((species, columns // 2), f32)] if after else [])
            result = call(kernel(relay_kernel, capacity=capacity, step=step, after=after), outs, "relay", [buffer, got])
            buffer = result[0]
            send = result[-1]
            step = after

        (new_oxygen,) = call(
            kernel(sweep_kernel, grid_count=grid_count, row_count=row_count),
            [((nz, cx, cy), f32)],
            "sweeps",
            [field, strips, got_even, got_odd],
            scratch=[pltpu.VMEM((2, nz + 2, cx, cy), f32), pltpu.VMEM((2, nz + 2, cx, cy), f32)],
        )
        return new_state, buffer, new_oxygen

    return jax.shard_map(
        shards,
        mesh=mesh,
        in_specs=(
            P(None, GRID), P(), P(), P(), P(), P(), P(GRID), P(GRID), P(GRID, None), P(GRID), P(None, "gx", "gy"),
        ),
        out_specs=(P(None, GRID), P(None, GRID), P(None, "gx", "gy")),
        check_vma=False,
    )
```

time: 137 us -> 37.1 us (0.27)
  the two profiles are of different devices: /device:TPU:1 before, /device:TPU:0 now
where the time goes in v1:
time: 37.1 us; the launch traced here: 36.8 us
  Pallas kernels  13.9 us (37%)
  starting transfers between devices  12.8 us (35%)
  waiting for transfers between devices  4.46 us (12%)
  local copies, waits for them, and re-layouts  4.29 us (12%)
  between operations  1.41 us (4%)
    pallas_call x7, Pallas kernels, call(): pl.pallas_call(body, out_shape=tuple((jax.ShapeDtypeStruct(s, t) for s, t...  13.9 us
    ppermute x9, starting transfers between devices, swap(): return lax.ppermute(value, GRID, swap_pairs(grid_count, row_count, partner))  12.8 us
    ppermute x9, waiting for transfers between devices, swap(): return lax.ppermute(value, GRID, swap_pairs(grid_count, row_count, partner))  4.46 us
    unnamed x24, local copies, waits for them, and re-layouts  4.29 us
  transfers between devices with their start and end apart: 9, of which 3 were waited for; matrix products, arithmetic and copies ran while one was open for 0% of the time, Pallas kernels for 18%

profile of v1, /device:TPU:0, one launch (start us, length us, event | category | flops | bytes accessed | tf_op | source)
XLA Modules:
  0.0 36.8 jit_solution(3478811211923608839)
XLA Ops:
  0.6 0.0 copy-start.5
  1.3 0.0 copy-start.11
  1.3 0.0 copy-start.8
  1.3 0.0 copy-start.9
  1.3 0.0 copy-start.10
  1.3 0.0 copy-done.5
  1.4 0.6 %copy-done.11 = f32[39]{0:T(128)S(1)} copy-done((f32[39]{0:T(128)S(1)}, f32[39]{0:T(128)}, u32[]{:S(2)}) %copy-start.11) | copy-done | bytes 180
  2.0 0.0 copy-done.8
  2.0 0.0 copy-done.9
  2.0 0.0 copy-done.10
  2.0 0.0 copy-start
  2.0 0.9 %copy-done = f32[64,8,128]{2,1,0:T(8,128)S(1)} copy-done((f32[64,8,128]{2,1,0:T(8,128)S(1)}, f32[64,8,128]{2,1,0:T(8,128)}, u32[]{:S(2)}) %copy-start) | copy-done | bytes 262168
  3.0 0.0 copy-start.3
  3.0 1.0 %copy-done.3 = f32[39,2048]{1,0:T(8,128)S(1)} copy-done((f32[39,2048]{1,0:T(8,128)S(1)}, f32[39,2048]{1,0:T(8,128)}, u32[]{:S(2)}) %copy-start.3) | copy-done | bytes 319512
  3.9 0.0 copy-start.4
  3.9 0.7 %copy-done.4 = f32[39,39]{1,0:T(8,128)S(1)} copy-done((f32[39,39]{1,0:T(8,128)S(1)}, f32[39,39]{1,0:T(8,128)}, u32[]{:S(2)}) %copy-start.4) | copy-done | bytes 6108
  4.7 0.0 copy-start.6
  4.7 0.0 copy-start.7
  4.7 2.1 %advance.1 = (f32[39,2048]{1,0:T(8,128)}, bf16[304,128]{1,0:T(8,128)(2,1)S(1)}, bf16[304,128]{1,0:T(8,128)(2,1)S(1)}, bf16[48,128]{1,0:T(8,128)(2,1)S(1)}) custom-call(s32[1]{0:T(128)S(6)} %copy.14.refs_0_, f32[39,2048]{1,0:T(8,128)S(1)} %copy-done.3, f32[39,39]{1,0:T(8,128)S(1)} %copy-done.4, f32[1,39]{1,0:T(1,128)S(1)} %bitcast.10, f32[1,39]{1,0:T(1,128)S(1)} %bitcast.11, ...), custom_call_target="tpu_custom_call" | custom-call | tf_op jit(solution)/shard_map/advance/pallas_call | solution.py:27
  6.8 3.0 %collective-permute-start.3 = (bf16[304,128]{1,0:T(8,128)(2,1)S(1)}, bf16[304,128]{1,0:T(8,128)(2,1)S(1)}, u32[]{:S(2)}, u32[]{:S(2)}) collective-permute-start(bf16[304,128]{1,0:T(8,128)(2,1)S(1)} %get-tuple-element.25), channel_id=1, source_target_pairs={{0,4},{1,5},{2,6},{3,7},{4,0},{5,1},{6,2},{7,3},{8,12},{9,13},{10,... | collective-permute-start | bytes 233480 | tf_op jit(solution)/shard_map/ppermute | solution.py:365
  9.7 0.0 collective-permute-start.4
  9.7 0.0 copy-done.6
  9.7 0.0 copy-done.7
  9.7 0.0 copy-start.2
  9.7 1.0 %copy-done.2 = f32[39,2048]{1,0:T(8,128)S(1)} copy-done((f32[39,2048]{1,0:T(8,128)S(1)}, f32[39,2048]{1,0:T(8,128)}, u32[]{:S(2)}) %copy-start.2) | copy-done | bytes 319512
  10.7 0.6 %daughters.1 = (f32[39,256]{1,0:T(8,128)S(1)}, f32[39,128]{1,0:T(8,128)S(1)}) custom-call(f32[39,2048]{1,0:T(8,128)S(1)} %copy-done.2, s32[1,128]{1,0:T(1,128)S(1)} %bitcast.8, s32[1,128]{1,0:T(1,128)S(1)} %bitcast.9), custom_call_target="tpu_custom_call" | custom-call | tf_op jit(solution)/shard_map/daughters/pallas_call | solution.py:27
  11.3 3.0 %collective-permute-start = (f32[39,128]{1,0:T(8,128)S(1)}, f32[39,128]{1,0:T(8,128)S(1)}, u32[]{:S(2)}, u32[]{:S(2)}) collective-permute-start(f32[39,128]{1,0:T(8,128)S(1)} %get-tuple-element.19), channel_id=1, source_target_pairs={{0,16},{1,17},{2,18},{3,19},{4,20},{5,21},{6,22},{7,23},{8,24},{9,... | collective-permute-start | bytes 59912 | tf_op jit(solution)/shard_map/ppermute | solution.py:365
  14.3 1.8 %collective-permute-done.refs_1_ = f32[39,128]{1,0:T(8,128)S(1)} collective-permute-done((f32[39,128]{1,0:T(8,128)S(1)}, f32[39,128]{1,0:T(8,128)S(1)}, u32[]{:S(2)}, u32[]{:S(2)}) %collective-permute-start) | collective-permute-done | bytes 20000 | tf_op jit(solution)/shard_map/ppermute | solution.py:365
  16.1 0.1 relay.3
  16.2 1.6 %collective-permute-start.1 = (f32[39,128]{1,0:T(8,128)S(1)}, f32[39,128]{1,0:T(8,128)S(1)}, u32[]{:S(2)}, u32[]{:S(2)}) collective-permute-start(f32[39,128]{1,0:T(8,128)S(1)} %get-tuple-element.21), channel_id=1, source_target_pairs={{0,8},{1,9},{2,10},{3,11},{4,12},{5,13},{6,14},{7,15},{8,0},{9,1},... | collective-permute-start | bytes 59912 | tf_op jit(solution)/shard_map/ppermute | solution.py:365
  17.8 0.5 %collective-permute-start.5 = (bf16[48,128]{1,0:T(8,128)(2,1)S(1)}, bf16[48,128]{1,0:T(8,128)(2,1)S(1)}, u32[]{:S(2)}, u32[]{:S(2)}) collective-permute-start(bf16[48,128]{1,0:T(8,128)(2,1)S(1)} %get-tuple-element.24.refs_1_), channel_id=1, source_target_pairs={{0,8},{1,9},{2,10},{3,11},{4,12},{5,13},{6,14},{7,15},{8,0},{9,1},... | collective-permute-start | bytes 36872 | tf_op jit(solution)/shard_map/ppermute | solution.py:365
  18.2 0.0 collective-permute-start.6
  18.2 1.8 %collective-permute-done.1.refs_1_ = f32[39,128]{1,0:T(8,128)S(1)} collective-permute-done((f32[39,128]{1,0:T(8,128)S(1)}, f32[39,128]{1,0:T(8,128)S(1)}, u32[]{:S(2)}, u32[]{:S(2)}) %collective-permute-start.1) | collective-permute-done | bytes 20000 | tf_op jit(solution)/shard_map/ppermute | solution.py:365
  20.0 0.1 relay.4
  20.1 3.0 %collective-permute-start.2 = (f32[39,128]{1,0:T(8,128)S(1)}, f32[39,128]{1,0:T(8,128)S(1)}, u32[]{:S(2)}, u32[]{:S(2)}) collective-permute-start(f32[39,128]{1,0:T(8,128)S(1)} %get-tuple-element.23), channel_id=1, source_target_pairs={{0,4},{1,5},{2,6},{3,7},{4,0},{5,1},{6,2},{7,3},{8,12},{9,13},{10,... | collective-permute-start | bytes 59912 | tf_op jit(solution)/shard_map/ppermute | solution.py:365
  23.1 0.0 collective-permute-done.5.refs_4_
  23.1 0.0 collective-permute-done.6.refs_5_
  23.1 0.0 collective-permute-done.3.refs_2_
  23.1 0.0 collective-permute-done.4.refs_3_
  23.1 0.0 copy-done.1
  23.1 5.2 %deposit.1 = (f32[2,64,8,128]{3,2,1,0:T(8,128)S(1)}, f32[16,1024]{1,0:T(8,128)S(1)}, f32[4,1024]{1,0:T(4,128)S(1)}, f32[4,1024]{1,0:T(4,128)S(1)}) custom-call(f32[64,8,128]{2,1,0:T(8,128)S(1)} %copy-done.1, bf16[48,128]{1,0:T(8,128)(2,1)S(1)} %get-tuple-element.24.refs_1_, bf16[304,128]{1,0:T(8,128)(2,1)S(1)} %collective-permute-done.3.refs_2_, ...), custom_call_target="tpu_custom_call" | custom-call | tf_op jit(solution)/shard_map/deposit/pallas_call | solution.py:27
  28.4 0.1 collective-permute-start.7
  28.4 1.6 %collective-permute-start.8 = (f32[4,1024]{1,0:T(4,128)S(1)}, f32[4,1024]{1,0:T(4,128)S(1)}, u32[]{:S(2)}, u32[]{:S(2)}) collective-permute-start(f32[4,1024]{1,0:T(4,128)S(1)} %get-tuple-element.30), channel_id=1, source_target_pairs={{0,3},{1,2},{2,1},{3,0},{4,7},{5,6},{6,5},{7,4},{8,11},{9,10},{10,... | collective-permute-start | bytes 49160 | tf_op jit(solution)/shard_map/ppermute | solution.py:365
  30.1 0.0 collective-permute-done.2.refs_1_
  30.1 0.7 %relay.5 = f32[39,256]{1,0:T(8,128)} custom-call(f32[39,256]{1,0:T(8,128)S(1)} %get-tuple-element.22.refs_0_, f32[39,128]{1,0:T(8,128)S(1)} %collective-permute-done.2.refs_1_), custom_call_target="tpu_custom_call" | custom-call | tf_op jit(solution)/shard_map/relay/pallas_call | solution.py:27
  30.8 0.0 collective-permute-done.7.refs_2_
  30.8 0.9 %collective-permute-done.8.refs_3_ = f32[4,1024]{1,0:T(4,128)S(1)} collective-permute-done((f32[4,1024]{1,0:T(4,128)S(1)}, f32[4,1024]{1,0:T(4,128)S(1)}, u32[]{:S(2)}, u32[]{:S(2)}) %collective-permute-start.8) | collective-permute-done | bytes 16416 | tf_op jit(solution)/shard_map/ppermute | solution.py:365
  31.7 5.1 %sweeps.1 = f32[64,8,128]{2,1,0:T(8,128)} custom-call(f32[2,64,8,128]{3,2,1,0:T(8,128)S(1)} %get-tuple-element.27.refs_0_, f32[16,1024]{1,0:T(8,128)S(1)} %get-tuple-element.28.refs_1_, f32[4,1024]{1,0:T(4,128)S(1)} %collective-permute-done.7.refs_2_, f32[4,1024]{1,0:T(4,128)S(1)} %collective-permute-done.8.refs_3_), custom_call_target="tpu_custom_call" | custom-call | tf_op jit(solution)/shard_map/sweeps/pallas_call | solution.py:27
  (1 shorter events, 0.0 us)
Async XLA Ops:
  0.6 0.7 %copy-start.5 = (s32[2048]{0:T(1024)S(1)}, s32[2048]{0:T(1024)}, u32[]{:S(2)}) copy-start(s32[2048]{0:T(1024)} %param.20) | copy-start | bytes 24580
  1.3 0.7 %copy-start.11 = (f32[39]{0:T(128)S(1)}, f32[39]{0:T(128)}, u32[]{:S(2)}) copy-start(f32[39]{0:T(128)} %param.16) | copy-start | bytes 472
  1.3 0.7 %copy-start.8 = (f32[39]{0:T(128)S(1)}, f32[39]{0:T(128)}, u32[]{:S(2)}) copy-start(f32[39]{0:T(128)} %param.13) | copy-start | bytes 472
  1.3 0.7 %copy-start.9 = (f32[39]{0:T(128)S(1)}, f32[39]{0:T(128)}, u32[]{:S(2)}) copy-start(f32[39]{0:T(128)} %param.14) | copy-start | bytes 472
  1.3 0.7 %copy-start.10 = (f32[39]{0:T(128)S(1)}, f32[39]{0:T(128)}, u32[]{:S(2)}) copy-start(f32[39]{0:T(128)} %param.15) | copy-start | bytes 472
  2.0 0.9 %copy-start = (f32[64,8,128]{2,1,0:T(8,128)S(1)}, f32[64,8,128]{2,1,0:T(8,128)}, u32[]{:S(2)}) copy-start(f32[64,8,128]{2,1,0:T(8,128)} %refs_0_.2) | copy-start | bytes 786436
  3.0 1.0 %copy-start.3 = (f32[39,2048]{1,0:T(8,128)S(1)}, f32[39,2048]{1,0:T(8,128)}, u32[]{:S(2)}) copy-start(f32[39,2048]{1,0:T(8,128)} %refs_1_.1) | copy-start | bytes 958468
  3.9 0.7 %copy-start.4 = (f32[39,39]{1,0:T(8,128)S(1)}, f32[39,39]{1,0:T(8,128)}, u32[]{:S(2)}) copy-start(f32[39,39]{1,0:T(8,128)} %refs_2_.1) | copy-start | bytes 18256
  4.7 5.1 %copy-start.6 = (s32[128]{0:T(128)S(1)}, s32[128]{0:T(128)}, u32[]{:S(2)}) copy-start(s32[128]{0:T(128)} %param.18) | copy-start | bytes 1540
  4.7 5.1 %copy-start.7 = (s32[128,1]{0,1:T(1,128)S(1)}, s32[128,1]{0,1:T(1,128)}, u32[]{:S(2)}) copy-start(s32[128,1]{0,1:T(1,128)} %param.19) | copy-start | bytes 1540
  6.8 16.4 %copy-start.1 = (f32[64,8,128]{2,1,0:T(8,128)S(1)}, f32[64,8,128]{2,1,0:T(8,128)}, u32[]{:S(2)}) copy-start(f32[64,8,128]{2,1,0:T(8,128)} %refs_0_.2) | copy-start | bytes 786436
  6.8 16.4 %collective-permute-start.3 = (bf16[304,128]{1,0:T(8,128)(2,1)S(1)}, bf16[304,128]{1,0:T(8,128)(2,1)S(1)}, u32[]{:S(2)}, u32[]{:S(2)}) collective-permute-start(bf16[304,128]{1,0:T(8,128)(2,1)S(1)} %get-tuple-element.25), channel_id=1, source_target_pairs={{0,4},{1,5},{2,6},{3,7},{4,0},{5,1},{6,2},{7,3},{8,12},{9,13},{10,... | collective-permute-start | bytes 233480 | tf_op jit(solution)/shard_map/ppermute | solution.py:365
  9.7 13.4 %collective-permute-start.4 = (bf16[304,128]{1,0:T(8,128)(2,1)S(1)}, bf16[304,128]{1,0:T(8,128)(2,1)S(1)}, u32[]{:S(2)}, u32[]{:S(2)}) collective-permute-start(bf16[304,128]{1,0:T(8,128)(2,1)S(1)} %get-tuple-element.26), channel_id=1, source_target_pairs={{0,1},{1,0},{2,3},{3,2},{4,8},{5,9},{6,10},{7,11},{8,4},{9,5},{10,... | collective-permute-start | bytes 233480 | tf_op jit(solution)/shard_map/ppermute | solution.py:365
  9.7 1.0 %copy-start.2 = (f32[39,2048]{1,0:T(8,128)S(1)}, f32[39,2048]{1,0:T(8,128)}, u32[]{:S(2)}) copy-start(f32[39,2048]{1,0:T(8,128)} %get-tuple-element.14.refs_0_) | copy-start | bytes 958468
  11.3 4.8 %collective-permute-start = (f32[39,128]{1,0:T(8,128)S(1)}, f32[39,128]{1,0:T(8,128)S(1)}, u32[]{:S(2)}, u32[]{:S(2)}) collective-permute-start(f32[39,128]{1,0:T(8,128)S(1)} %get-tuple-element.19), channel_id=1, source_target_pairs={{0,16},{1,17},{2,18},{3,19},{4,20},{5,21},{6,22},{7,23},{8,24},{9,... | collective-permute-start | bytes 59912 | tf_op jit(solution)/shard_map/ppermute | solution.py:365
  16.2 3.8 %collective-permute-start.1 = (f32[39,128]{1,0:T(8,128)S(1)}, f32[39,128]{1,0:T(8,128)S(1)}, u32[]{:S(2)}, u32[]{:S(2)}) collective-permute-start(f32[39,128]{1,0:T(8,128)S(1)} %get-tuple-element.21), channel_id=1, source_target_pairs={{0,8},{1,9},{2,10},{3,11},{4,12},{5,13},{6,14},{7,15},{8,0},{9,1},... | collective-permute-start | bytes 59912 | tf_op jit(solution)/shard_map/ppermute | solution.py:365
  17.8 5.3 %collective-permute-start.5 = (bf16[48,128]{1,0:T(8,128)(2,1)S(1)}, bf16[48,128]{1,0:T(8,128)(2,1)S(1)}, u32[]{:S(2)}, u32[]{:S(2)}) collective-permute-start(bf16[48,128]{1,0:T(8,128)(2,1)S(1)} %get-tuple-element.24.refs_1_), channel_id=1, source_target_pairs={{0,8},{1,9},{2,10},{3,11},{4,12},{5,13},{6,14},{7,15},{8,0},{9,1},... | collective-permute-start | bytes 36872 | tf_op jit(solution)/shard_map/ppermute | solution.py:365
  18.2 4.9 %collective-permute-start.6 = (bf16[48,128]{1,0:T(8,128)(2,1)S(1)}, bf16[48,128]{1,0:T(8,128)(2,1)S(1)}, u32[]{:S(2)}, u32[]{:S(2)}) collective-permute-start(bf16[48,128]{1,0:T(8,128)(2,1)S(1)} %get-tuple-element.24.refs_1_), channel_id=1, source_target_pairs={{0,1},{1,0},{2,3},{3,2},{4,5},{5,4},{6,7},{7,6},{8,16},{9,17},{10,... | collective-permute-start | bytes 36872 | tf_op jit(solution)/shard_map/ppermute | solution.py:365
  20.1 10.0 %collective-permute-start.2 = (f32[39,128]{1,0:T(8,128)S(1)}, f32[39,128]{1,0:T(8,128)S(1)}, u32[]{:S(2)}, u32[]{:S(2)}) collective-permute-start(f32[39,128]{1,0:T(8,128)S(1)} %get-tuple-element.23), channel_id=1, source_target_pairs={{0,4},{1,5},{2,6},{3,7},{4,0},{5,1},{6,2},{7,3},{8,12},{9,13},{10,... | collective-permute-start | bytes 59912 | tf_op jit(solution)/shard_map/ppermute | solution.py:365
  28.4 2.4 %collective-permute-start.7 = (f32[4,1024]{1,0:T(4,128)S(1)}, f32[4,1024]{1,0:T(4,128)S(1)}, u32[]{:S(2)}, u32[]{:S(2)}) collective-permute-start(f32[4,1024]{1,0:T(4,128)S(1)} %get-tuple-element.29), channel_id=1, source_target_pairs={{0,1},{1,0},{2,3},{3,2},{4,5},{5,4},{6,7},{7,6},{8,9},{9,8},{10,11... | collective-permute-start | bytes 49160 | tf_op jit(solution)/shard_map/ppermute | solution.py:365
  28.4 3.2 %collective-permute-start.8 = (f32[4,1024]{1,0:T(4,128)S(1)}, f32[4,1024]{1,0:T(4,128)S(1)}, u32[]{:S(2)}, u32[]{:S(2)}) collective-permute-start(f32[4,1024]{1,0:T(4,128)S(1)} %get-tuple-element.30), channel_id=1, source_target_pairs={{0,3},{1,2},{2,1},{3,0},{4,7},{5,6},{6,5},{7,4},{8,11},{9,10},{10,... | collective-permute-start | bytes 49160 | tf_op jit(solution)/shard_map/ppermute | solution.py:365

commit v2 on v1

v2 whole, which is shorter than its diff:
```python
import jax
import jax.numpy as jnp
from jax import lax
from jax.experimental import pallas as pl
from jax.experimental.pallas import tpu as pltpu
from jax.sharding import PartitionSpec as P

time_step = 0.25
diffusion_number = 0.16
sweeps = 4
GRID = ("gx", "gy")
LANES = 128
EXACT = lax.Precision.HIGHEST
f32, bf16, i32 = jnp.float32, jnp.bfloat16, jnp.int32
VMEM_LIMIT = 48 << 20


def call(body, outs, name, inputs, smem=(), hbm=(), scratch=(), cost=None):
    def spec(at, shape):
        if at in smem:
            return pl.BlockSpec(memory_space=pltpu.SMEM)
        return pl.BlockSpec(memory_space=pltpu.HBM) if at in hbm else pl.BlockSpec(memory_space=pltpu.VMEM)

    count = len(inputs)
    inputs = [pltpu.with_memory_space_constraint(v, pltpu.HBM) if at in hbm else v for at, v in enumerate(inputs)]
    return pl.pallas_call(
        body,
        out_shape=tuple(jax.ShapeDtypeStruct(s, t) for s, t in outs),
        in_specs=[spec(at, value.shape) for at, value in enumerate(inputs)],
        out_specs=tuple(spec(count + at, s) for at, (s, t) in enumerate(outs)),
        scratch_shapes=scratch,
        compiler_params=pltpu.CompilerParams(vmem_limit_bytes=VMEM_LIMIT),
        name=name,
    )(*inputs)


def swap_pairs(grid_count, row_count, partner):
    pairs = []
    for g in range(grid_count):
        for h in range(row_count):
            p, q = partner(g, h)
            if not (0 <= p < grid_count and 0 <= q < row_count):
                p, q = g, h ^ 1
            pairs.append((g * row_count + h, p * row_count + q))
    return pairs


def near_even(g, h):
    return g ^ 1, h


def near_odd(g, h):
    return (g + 1 if g % 2 else g - 1), h


def far_even(g, h):
    return g ^ 2, h


def far_odd(g, h):
    return (g + 2 if g & 2 else g - 2), h


def side_even(g, h):
    return g, h ^ 1


def column(row, count):
    shape = (count, count)
    same = lax.broadcasted_iota(i32, shape, 0) == lax.broadcasted_iota(i32, shape, 1)
    return jnp.sum(jnp.where(same, jnp.broadcast_to(row, shape), 0), axis=1, keepdims=True)


def advance_kernel(
    count_ref, cell_hbm, coupling_hbm, basal_hbm, half_hbm, decay_hbm, weight_hbm, voxel_hbm, oxygen_hbm,
    new_state, message_even, message_odd, message_far,
    cell, coupling, basal, half, decay, weight, voxel, oxygen, drive, semaphores, *, cy, cx, nz,
):
    pairs = (
        (cell_hbm, cell), (coupling_hbm, coupling), (basal_hbm, basal), (half_hbm, half), (decay_hbm, decay),
        (weight_hbm, weight), (voxel_hbm, voxel), (oxygen_hbm, oxygen),
    )
    copies = [pltpu.make_async_copy(a, b, semaphores.at[i]) for i, (a, b) in enumerate(pairs)]
    for copy in copies:
        copy.start()
    for copy in copies:
        copy.wait()
    species, agents = cell.shape
    basal_c, half_c, decay_c, weight_c = (column(r[...], species) for r in (basal, half, decay, weight))
    half_square = half_c * half_c
    matrix = coupling[...]

    def rates(current):
        square = current * current
        occupancy = square / (half_square + square)
        product = jnp.dot(matrix, occupancy, precision=EXACT, preferred_element_type=f32)
        return basal_c + product - decay_c * current

    current = cell[...]
    for substep in range(2):
        middle = current + (0.5 * time_step) * rates(current)
        current = current + time_step * rates(middle)
    new_state[...] = current
    total = jnp.sum(weight_c * current, axis=0, keepdims=True)
    rows = agents // LANES
    for c in range(rows):
        drive[c : c + 1, :] = total[:, c * LANES : (c + 1) * LANES]
    x = drive[...]
    soft = jnp.maximum(x, 0.0) + jnp.log1p(jnp.exp(-jnp.abs(x)))
    slot = lax.broadcasted_iota(i32, (rows, LANES), 0) * LANES + lax.broadcasted_iota(i32, (rows, LANES), 1)
    uptake = jnp.where(slot < count_ref[0], soft, 0.0)
    code = voxel[...]
    at_y = code % cy
    at_x = (code // cy) % cx
    at_z = (code // (cy * cx)) % nz
    slab_x = (code // (cy * cx * nz)) * cx + at_x + cx // 2
    row = at_z * cx + slab_x % cx - nz * cx // 2
    col = (slab_x // cx) * cy + at_y - 2 * cy
    listing = jnp.concatenate([uptake, row.astype(f32), col.astype(f32)], axis=0).astype(bf16)
    own = oxygen[...] - 1.0
    turned = pltpu.roll(own, cx // 2, 1)
    low = lax.broadcasted_iota(i32, (nz // 2, cx, cy), 1) < cx // 2
    a, b = own[: nz // 2], own[nz // 2 :]
    ta, tb = turned[: nz // 2], turned[nz // 2 :]
    upper = jnp.where(low, ta, b)
    lower = jnp.where(low, a, tb)
    even = lax.axis_index("gx") % 2 == 0
    to_next = upper.reshape(nz // 2 * cx, cy)
    to_previous = lower.reshape(nz // 2 * cx, cy)
    head = nz // 2 * cx
    message_even[:head, :] = jnp.where(even, to_next, to_previous).astype(bf16)
    message_odd[:head, :] = jnp.where(even, to_previous, to_next).astype(bf16)
    message_even[head:, :] = listing
    message_odd[head:, :] = listing
    message_far[...] = listing


def one_hots(lists, which, base, width, m, left, right, slot):
    rows = lists.shape[1] // 3
    pack = 16
    row_at = (lax.broadcasted_iota(i32, (m, LANES), 0) - m // 2).astype(f32).astype(bf16).reshape(m // pack, pack, LANES)
    col_at = (lax.broadcasted_iota(i32, (width, LANES), 0) + base).astype(f32).astype(bf16)
    col_at = col_at.reshape(width // pack, pack, LANES)
    one, zero = jnp.ones((), bf16), jnp.zeros((), bf16)

    def line(at):
        return jnp.broadcast_to(lists[which, at : at + 1, :], (pack, LANES)).astype(bf16)[None]

    for at in range(rows):
        columns = slice((slot * rows + at) * LANES, (slot * rows + at + 1) * LANES)
        hit = jnp.where(row_at == line(rows + at), one, zero)
        left[:, columns] = hit.reshape(m, LANES)
        spread = jnp.where(col_at == line(2 * rows + at), jnp.broadcast_to(line(at), col_at.shape), zero)
        right[:width, columns] = spread.reshape(width, LANES)


def product(left, right):
    return lax.dot_general(left, right, (((1,), (1,)), ((), ())), preferred_element_type=f32)


def own_kernel(oxygen_hbm, own_list, base, lists, left, right, oxygen, semaphore):
    copy = pltpu.make_async_copy(oxygen_hbm, oxygen, semaphore)
    copy.start()
    nz, cx, cy = oxygen.shape
    lists[0] = own_list[...].astype(f32)
    one_hots(lists, 0, -cy, 2 * cy, nz * cx, left, right, 0)
    total = product(left[...], right[...])
    copy.wait()
    low = lax.broadcasted_iota(i32, (nz, cx, cy), 1) < cx // 2
    inner = pltpu.roll(oxygen[...], cx // 2, 1)
    base[:, :cx, :] = jnp.where(low, 0.0, inner) - total[:, :cy].reshape(nz, cx, cy)
    base[:, cx:, :] = jnp.where(low, inner, 0.0) - total[:, cy:].reshape(nz, cx, cy)


def deposit_kernel(
    base, near_e, near_o, far_e, far_o, field, strips, strip_even, strip_odd,
    lists, left, right, far_left, far_right, *, grid_count,
):
    nz, cx, cy = base.shape[0], base.shape[1] // 2, base.shape[2]
    half, zh = cx // 2, nz // 2
    head = zh * cx
    m = nz * cx
    rows = far_e.shape[0] // 3
    g = lax.axis_index("gx")
    even = g % 2 == 0
    low_pair = g % 4 < 2
    has_next, has_previous = g + 1 < grid_count, g >= 1
    has_next2, has_previous2 = g + 2 < grid_count, g >= 2

    def keep(listing, valid):
        index = lax.broadcasted_iota(i32, listing.shape, 0)
        return jnp.where((index < rows) & jnp.logical_not(valid), 0.0, listing)

    e, o = near_e[...].astype(f32), near_o[...].astype(f32)
    after, before = jnp.where(even, e, o), jnp.where(even, o, e)
    fe, fo = far_e[...].astype(f32), far_o[...].astype(f32)
    lists[0] = keep(after[head:], has_next)
    lists[1] = keep(before[head:], has_previous)
    lists[2] = keep(jnp.where(low_pair, fe, fo), has_next2)
    lists[3] = keep(jnp.where(low_pair, fo, fe), has_previous2)
    one_hots(lists, 0, -2 * cy, 2 * cy, m, left, right, 0)
    one_hots(lists, 1, 0, 2 * cy, m, left, right, 1)
    total = product(left[...], right[...])
    one_hots(lists, 2, -2 * cy, cy, m, far_left, far_right, 0)
    total1 = total[:, cy:] + product(far_left[...], far_right[...])
    one_hots(lists, 3, cy, cy, m, far_left, far_right, 0)
    total0 = total[:, :cy] + product(far_left[...], far_right[...])

    low = lax.broadcasted_iota(i32, (zh, cx, cy), 1) < half
    from_before = jnp.where(has_previous, before[:head] + 1.0, 0.0).reshape(zh, cx, cy)
    from_after = jnp.where(has_next, after[:head] + 1.0, 0.0).reshape(zh, cx, cy)
    before_b = pltpu.roll(from_before, half, 1)
    after_a = pltpu.roll(from_after, half, 1)
    shape = (zh, cx, cy)
    field[:zh, :cx] = base[:zh, :cx] + jnp.where(low, from_before, 0.0) - total0[:head].reshape(shape)
    field[zh:, :cx] = base[zh:, :cx] + jnp.where(low, before_b, 0.0) - total0[head:].reshape(shape)
    field[:zh, cx:] = base[:zh, cx:] + jnp.where(low, 0.0, after_a) - total1[:head].reshape(shape)
    field[zh:, cx:] = base[zh:, cx:] + jnp.where(low, 0.0, from_after) - total1[head:].reshape(shape)

    edge = 2 * sweeps
    picked = lax.broadcasted_iota(i32, (2 * edge, cy), 0)
    picked = jnp.where(picked < edge, picked, picked + cy - 2 * edge)
    picker = (picked == lax.broadcasted_iota(i32, (2 * edge, cy), 1)).astype(f32).astype(bf16)
    flat = field[...].reshape(2 * m, cy)
    rims = sum(product(picker, piece) for piece in pieces(flat))
    strips[...] = rims
    h_even = lax.axis_index("gy") % 2 == 0
    head_rows, tail_rows = rims[:sweeps], rims[2 * edge - sweeps :]
    strip_even[...] = jnp.where(h_even, tail_rows, head_rows)
    strip_odd[...] = jnp.where(h_even, head_rows, tail_rows)


def sweep_kernel(field, out, ping, pong, *, grid_count):
    nz, width, cy = field.shape
    cx = width // 2
    g = lax.axis_index("gx")
    top = width
    sub = lax.broadcasted_iota(i32, (cx, cy), 0)
    masks = (
        jnp.where((g == 0) & (sub < cx // 2), 0.0, diffusion_number),
        jnp.where((g == grid_count - 1) & (sub >= cx // 2), 0.0, diffusion_number),
    )
    centre = 1.0 / diffusion_number - 6.0
    zero = jnp.zeros((width, cy), f32)
    for buffer in (ping, pong):
        buffer[:top, :] = zero
        buffer[top + nz * width : top + nz * width + width, :] = zero
    ping[top : top + nz * width, :] = field[...].reshape(nz * width, cy)

    def one_sweep(source, target):
        def plane(z, carry):
            for tile in range(2):
                at = (z + 1) * width + tile * cx
                c = source[pl.ds(at, cx), :]
                total = source[pl.ds(at - width, cx), :] + source[pl.ds(at + width, cx), :]
                total = total + (source[pl.ds(at - 1, cx), :] + source[pl.ds(at + 1, cx), :])
                total = total + (pltpu.roll(c, 1, 1) + pltpu.roll(c, cy - 1, 1))
                target[pl.ds(at, cx), :] = (total + centre * c) * masks[tile]
            return carry

        lax.fori_loop(0, nz, plane, 0, unroll=8)

    for turn in range(sweeps):
        one_sweep(*((ping, pong) if turn % 2 == 0 else (pong, ping)))
    main = ping if sweeps % 2 == 0 else pong
    for z in range(nz):
        out[z] = main[pl.ds((z + 1) * width + cx // 2, cx), :]


def strip_kernel(inside, strips, got_even, got_odd, out, *, grid_count, row_count):
    nz, cx, cy = inside.shape
    m = strips.shape[1]
    width = m // nz
    g, h = lax.axis_index("gx"), lax.axis_index("gy")
    h_even = h % 2 == 0
    edge = 2 * sweeps
    has_right, has_left = h + 1 < row_count, h >= 1
    a, b = got_even[...], got_odd[...]
    right = jnp.where(has_right, jnp.where(h_even, a, b), 0.0)
    left = jnp.where(has_left, jnp.where(h_even, b, a), 0.0)
    band = jnp.concatenate([left, strips[...], right], axis=0)
    count = band.shape[0]
    lane = lax.broadcasted_iota(i32, (count, m), 1)
    line = lax.broadcasted_iota(i32, (count, m), 0)
    outside = (line < sweeps) & jnp.logical_not(has_left) | (line >= count - sweeps) & jnp.logical_not(has_right)
    at_x = lane % width
    outside = outside | (g == 0) & (at_x < cx // 2) | (g == grid_count - 1) & (at_x >= width - cx // 2)
    keep = jnp.where(outside, 0.0, diffusion_number)
    z_first, z_last = lane < width, lane >= m - width
    centre = 1.0 / diffusion_number - 6.0
    for turn in range(sweeps):
        total = jnp.where(z_first, 0.0, pltpu.roll(band, width, 1)) + jnp.where(z_last, 0.0, pltpu.roll(band, m - width, 1))
        total = total + (pltpu.roll(band, 1, 0) + pltpu.roll(band, count - 1, 0))
        total = total + (pltpu.roll(band, 1, 1) + pltpu.roll(band, m - 1, 1))
        band = (total + centre * band) * keep
    final = jnp.concatenate([band[sweeps : 2 * sweeps], band[count - 2 * sweeps : count - sweeps]], axis=0)
    placed = lax.broadcasted_iota(i32, (edge, cy), 0)
    placed = jnp.where(placed < sweeps, placed, placed + cy - edge)
    placer = (placed == lax.broadcasted_iota(i32, (edge, cy), 1)).astype(f32)
    edges = lax.dot_general(
        final, placer, (((0,), (0,)), ((), ())), precision=EXACT, preferred_element_type=f32
    ).reshape(nz, width, cy)
    low = lax.broadcasted_iota(i32, (nz, cx, cy), 1) < cx // 2
    mixed = pltpu.roll(jnp.where(low, edges[:, cx:], edges[:, :cx]), cx // 2, 1)
    at_y = lax.broadcasted_iota(i32, (nz, cx, cy), 2)
    out[...] = jnp.where((at_y < sweeps) | (at_y >= cy - sweeps), mixed, inside[...])


def pieces(value):
    high = value.astype(bf16)
    rest = value - high.astype(f32)
    middle = rest.astype(bf16)
    return high, middle, (rest - middle.astype(f32)).astype(bf16)


def first_send(buffer, mine, width):
    count = buffer.shape[1]
    half = count // 2
    left, right = buffer[:, :half], buffer[:, half:]
    if width == half:
        return jnp.where(mine, left, right)
    bit = (lax.broadcasted_iota(i32, left.shape, 1) // width) % 2 == 1
    moved = jnp.where(mine, pltpu.roll(right, width, 1), pltpu.roll(right, half - width, 1))
    return jnp.where(jnp.logical_xor(bit, mine), left, moved)


def take_in(buffer, got, mine, width):
    count = buffer.shape[1]
    half = count // 2
    left, right = buffer[:, :half], buffer[:, half:]
    if width == half:
        left, right = jnp.where(mine, got, left), jnp.where(mine, right, got)
    else:
        bit = (lax.broadcasted_iota(i32, left.shape, 1) // width) % 2 == 1
        other = jnp.logical_xor(bit, mine)
        moved = jnp.where(mine, pltpu.roll(got, half - width, 1), pltpu.roll(got, width, 1))
        left, right = jnp.where(other, moved, left), jnp.where(other, got, right)
    return jnp.concatenate([left, right], axis=1)


def daughter_kernel(state, ids, targets, new_state, buffer, send, semaphore, *, capacity, step):
    copy = pltpu.make_async_copy(state, new_state, semaphore)
    copy.start()
    species, agents = state.shape
    picks = ids.shape[1]
    columns = buffer.shape[1]
    target = targets[...]
    square = (picks, picks)
    across = jnp.broadcast_to(target, square)
    down = jnp.broadcast_to(column(target, picks), square)
    earlier = lax.broadcasted_iota(i32, square, 0) < lax.broadcasted_iota(i32, square, 1)
    rank = jnp.sum(jnp.where((across == down) & earlier, 1, 0), axis=0, keepdims=True)
    position = target * capacity + rank
    chosen = (lax.broadcasted_iota(i32, (agents, picks), 0) == ids[...]).astype(f32).astype(bf16)
    mothers = sum(jnp.dot(p, chosen, preferred_element_type=f32) for p in pieces(state[...]))
    placing = (lax.broadcasted_iota(i32, (columns, picks), 0) == position).astype(f32).astype(bf16)
    placed = sum(
        lax.dot_general(p, placing, (((1,), (1,)), ((), ())), preferred_element_type=f32)
        for p in pieces(mothers)
    )
    buffer[...] = placed
    mine = (lax.axis_index("gx") // step) % 2 == 1
    send[...] = first_send(placed, mine, capacity * step)
    copy.wait()


def relay_kernel(buffer, got, merged, *send, capacity, step, after):
    g = lax.axis_index("gx")
    value = take_in(buffer[...], got[...], (g // step) % 2 == 1, capacity * step)
    merged[...] = value
    if after:
        send[0][...] = first_send(value, (g // after) % 2 == 1, capacity * after)


def solution(mesh):
    grid_count, row_count = mesh.shape["gx"], mesh.shape["gy"]

    def swap(value, partner):
        return lax.ppermute(value, GRID, swap_pairs(grid_count, row_count, partner))

    def side_odd(g, h):
        p = h + 1 if h % 2 else h - 1
        return (g, p) if 0 <= p < row_count else (g, h ^ (row_count - 1))

    def shards(
        cell_state, coupling, basal_rate, half_sat, decay_rate, uptake_weight,
        agent_counts, divider_ids, destinations, voxel_index, oxygen,
    ):
        species, agents = cell_state.shape
        nz, cx, cy = oxygen.shape
        picks = divider_ids.shape[0]
        rows = agents // LANES
        head = nz // 2 * cx
        capacity = max(2, 2 * picks // grid_count)
        columns = grid_count * capacity

        def line(value):
            return value.reshape(1, -1)

        def kernel(body, **sizes):
            def run(*refs):
                return body(*refs, **sizes)

            return run

        m = nz * cx
        state, message_even, message_odd, listing = call(
            kernel(advance_kernel, cy=cy, cx=cx, nz=nz),
            [((species, agents), f32), ((head + 3 * rows, LANES), bf16), ((head + 3 * rows, LANES), bf16),
             ((3 * rows, LANES), bf16)],
            "advance",
            [agent_counts, cell_state, coupling, line(basal_rate), line(half_sat), line(decay_rate),
             line(uptake_weight), voxel_index.reshape(rows, LANES), oxygen],
            smem=(0,),
            hbm=range(1, 9),
            scratch=[pltpu.VMEM((species, agents), f32), pltpu.VMEM((species, species), f32)]
            + [pltpu.VMEM((1, species), f32)] * 4
            + [pltpu.VMEM((rows, LANES), i32), pltpu.VMEM((nz, cx, cy), f32), pltpu.VMEM((rows, LANES), f32),
               pltpu.SemaphoreType.DMA((8,))],
        )
        near_e = swap(message_even, near_even)
        near_o = swap(message_odd, near_odd)
        far_e = swap(listing, far_even)
        far_o = swap(listing, far_odd)

        step = grid_count // 2
        new_state, buffer, send = call(
            kernel(daughter_kernel, capacity=capacity, step=step),
            [((species, agents), f32), ((species, columns), f32), ((species, columns // 2), f32)],
            "daughters",
            [state, line(divider_ids), line(destinations)],
            hbm=(3,),
            scratch=[pltpu.SemaphoreType.DMA],
        )
        (base,) = call(
            own_kernel,
            [((nz, 2 * cx, cy), f32)],
            "own",
            [oxygen, listing],
            hbm=(0,),
            scratch=[pltpu.VMEM((1, 3 * rows, LANES), f32), pltpu.VMEM((m, agents), bf16), pltpu.VMEM((2 * cy, agents), bf16),
                     pltpu.VMEM((nz, cx, cy), f32), pltpu.SemaphoreType.DMA],
        )
        field, strips, strip_even, strip_odd = call(
            kernel(deposit_kernel, grid_count=grid_count),
            [((nz, 2 * cx, cy), f32), ((4 * sweeps, 2 * m), f32), ((sweeps, 2 * m), f32), ((sweeps, 2 * m), f32)],
            "deposit",
            [base, near_e, near_o, far_e, far_o],
            scratch=[pltpu.VMEM((4, 3 * rows, LANES), f32), pltpu.VMEM((m, 2 * agents), bf16),
                     pltpu.VMEM((2 * cy, 2 * agents), bf16), pltpu.VMEM((m, agents), bf16), pltpu.VMEM((cy, agents), bf16)],
        )
        got_even = swap(strip_even, side_even)
        got_odd = swap(strip_odd, side_odd)
        reach = (nz + 2) * 2 * cx
        (inside,) = call(
            kernel(sweep_kernel, grid_count=grid_count),
            [((nz, cx, cy), f32)],
            "sweeps",
            [field],
            scratch=[pltpu.VMEM((reach, cy), f32), pltpu.VMEM((reach, cy), f32)],
        )
        (new_oxygen,) = call(
            kernel(strip_kernel, grid_count=grid_count, row_count=row_count),
            [((nz, cx, cy), f32)],
            "strips",
            [inside, strips, got_even, got_odd],
        )
        stages = [strips, inside]
        while step:
            after = step // 2
            got = swap(send, lambda g, h: (g ^ step, h))
            if stages:
                got, _ = lax.optimization_barrier((got, stages.pop(0)))
            outs = [((species, columns), f32)] + ([((species, columns // 2), f32)] if after else [])
            result = call(kernel(relay_kernel, capacity=capacity, step=step, after=after), outs, "relay", [buffer, got])
            buffer = result[0]
            send = result[-1]
            step = after
        return new_state, buffer, new_oxygen

    return jax.shard_map(
        shards,
        mesh=mesh,
        in_specs=(
            P(None, GRID), P(), P(), P(), P(), P(), P(GRID), P(GRID), P(GRID, None), P(GRID), P(None, "gx", "gy"),
        ),
        out_specs=(P(None, GRID), P(None, GRID), P(None, "gx", "gy")),
        check_vma=False,
    )
```

time: 37.1 us -> 33.3 us (0.90)
  local copies, waits for them, and re-layouts: 4.29 us -> 0.67 us
  waiting for transfers between devices: 4.46 us -> 2.65 us
  starting transfers between devices: 12.8 us -> 14 us
  Pallas kernels: 13.9 us -> 14.5 us
    unnamed x24 -> x4, local copies, waits for them, and re-layouts: 4.29 us -> 0.67 us
    ppermute x9, waiting for transfers between devices: 4.46 us -> 2.65 us  [swap(): return lax.ppermute(value, GRID, swap_pairs(grid_count, row_count, partner))]
    ppermute x9, starting transfers between devices: 12.8 us -> 14 us  [swap(): return lax.ppermute(value, GRID, swap_pairs(grid_count, row_count, partner))]
    pallas_call x7 -> x9, Pallas kernels: 13.9 us -> 14.5 us  [call(): pl.pallas_call(body, out_shape=tuple((jax.ShapeDtypeStruct(s, t) for s, t...]
  transfers between devices with their start and end apart: 9 -> 9, of which waited for: 3 -> 2; matrix products, arithmetic and copies ran while one was open for 0% -> 0% of each run, Pallas kernels for 18% -> 33%
where the time goes in v2:
time: 33.3 us; the launch traced here: 33.1 us
  Pallas kernels  14.5 us (44%)
  starting transfers between devices  14 us (42%)
  waiting for transfers between devices  2.65 us (8%)
  between operations  1.34 us (4%)
  local copies, waits for them, and re-layouts  0.67 us (2%)
    pallas_call x9, Pallas kernels, call(): pl.pallas_call(body, out_shape=tuple((jax.ShapeDtypeStruct(s, t) for s, t...  14.5 us
    ppermute x9, starting transfers between devices, swap(): return lax.ppermute(value, GRID, swap_pairs(grid_count, row_count, partner))  14 us
    ppermute x9, waiting for transfers between devices, swap(): return lax.ppermute(value, GRID, swap_pairs(grid_count, row_count, partner))  2.65 us
    unnamed x4, local copies, waits for them, and re-layouts  0.67 us
  transfers between devices with their start and end apart: 9, of which 2 were waited for; matrix products, arithmetic and copies ran while one was open for 0% of the time, Pallas kernels for 33%

profile of v2, /device:TPU:0, one launch (start us, length us, event | category | flops | bytes accessed | tf_op | source)
XLA Modules:
  0.0 33.1 jit_solution(15203366788544261421)
XLA Ops:
  1.3 2.6 %advance.1 = (f32[39,2048]{1,0:T(8,128)S(1)}, bf16[304,128]{1,0:T(8,128)(2,1)S(1)}, bf16[304,128]{1,0:T(8,128)(2,1)S(1)}, bf16[48,128]{1,0:T(8,128)(2,1)S(1)}) custom-call(s32[1]{0:T(128)S(6)} %copy.14.refs_0_, f32[39,2048]{1,0:T(8,128)} %refs_1_.1, f32[39,39]{1,0:T(8,128)} %refs_2_.1, f32[1,39]{1,0:T(1,128)} %bitcast.10, f32[1,39]{1,0:T(1,128)} %bitcast.11, ...), custom_call_target="tpu_custom_call" | custom-call | tf_op jit(solution)/shard_map/advance/pallas_call | solution.py:26
  3.9 3.0 %collective-permute-start.1 = (bf16[304,128]{1,0:T(8,128)(2,1)S(1)}, bf16[304,128]{1,0:T(8,128)(2,1)S(1)}, u32[]{:S(2)}, u32[]{:S(2)}) collective-permute-start(bf16[304,128]{1,0:T(8,128)(2,1)S(1)} %get-tuple-element.25), channel_id=1, source_target_pairs={{0,4},{1,5},{2,6},{3,7},{4,0},{5,1},{6,2},{7,3},{8,12},{9,13},{10,... | collective-permute-start | bytes 233480 | tf_op jit(solution)/shard_map/ppermute | solution.py:379
  7.0 0.0 collective-permute-start.2
  7.0 0.0 copy-start
  7.0 0.0 copy-start.1
  7.0 0.7 %copy-done = s32[128]{0:T(128)S(1)} copy-done((s32[128]{0:T(128)S(1)}, s32[128]{0:T(128)}, u32[]{:S(2)}) %copy-start) | copy-done | bytes 536
  7.6 0.0 copy-done.1
  7.6 0.7 %daughters.1 = (f32[39,2048]{1,0:T(8,128)}, f32[39,256]{1,0:T(8,128)S(1)}, f32[39,128]{1,0:T(8,128)S(1)}) custom-call(f32[39,2048]{1,0:T(8,128)S(1)} %get-tuple-element.20.refs_0_, s32[1,128]{1,0:T(1,128)S(1)} %bitcast.7, s32[1,128]{1,0:T(1,128)S(1)} %bitcast.8), custom_call_target="tpu_custom_call" | custom-call | tf_op jit(solution)/shard_map/daughters/pallas_call | solution.py:26
  8.4 3.0 %collective-permute-start = (f32[39,128]{1,0:T(8,128)S(1)}, f32[39,128]{1,0:T(8,128)S(1)}, u32[]{:S(2)}, u32[]{:S(2)}) collective-permute-start(f32[39,128]{1,0:T(8,128)S(1)} %get-tuple-element.23), channel_id=1, source_target_pairs={{0,16},{1,17},{2,18},{3,19},{4,20},{5,21},{6,22},{7,23},{8,24},{9,... | collective-permute-start | bytes 59912 | tf_op jit(solution)/shard_map/ppermute | solution.py:379
  11.4 1.6 %collective-permute-start.3 = (bf16[48,128]{1,0:T(8,128)(2,1)S(1)}, bf16[48,128]{1,0:T(8,128)(2,1)S(1)}, u32[]{:S(2)}, u32[]{:S(2)}) collective-permute-start(bf16[48,128]{1,0:T(8,128)(2,1)S(1)} %get-tuple-element.24.own_list), channel_id=1, source_target_pairs={{0,8},{1,9},{2,10},{3,11},{4,12},{5,13},{6,14},{7,15},{8,0},{9,1},... | collective-permute-start | bytes 36872 | tf_op jit(solution)/shard_map/ppermute | solution.py:379
  13.0 0.0 collective-permute-start.4
  13.0 1.0 %own.1.refs_0_ = f32[64,16,128]{2,1,0:T(8,128)S(1)} custom-call(f32[64,8,128]{2,1,0:T(8,128)} %oxygen_hbm.1, bf16[48,128]{1,0:T(8,128)(2,1)S(1)} %get-tuple-element.24.own_list), custom_call_target="tpu_custom_call" | custom-call | tf_op jit(solution)/shard_map/own/pallas_call | solution.py:26
  14.0 1.1 %collective-permute-done.3.refs_3_ = bf16[48,128]{1,0:T(8,128)(2,1)S(1)} collective-permute-done((bf16[48,128]{1,0:T(8,128)(2,1)S(1)}, bf16[48,128]{1,0:T(8,128)(2,1)S(1)}, u32[]{:S(2)}, u32[]{:S(2)}) %collective-permute-start.3) | collective-permute-done | bytes 12320 | tf_op jit(solution)/shard_map/ppermute | solution.py:379
  15.1 0.0 collective-permute-done.4.refs_4_
  15.1 0.0 collective-permute-done.1.refs_1_
  15.1 0.0 collective-permute-done.2.refs_2_
  15.1 3.8 %deposit.1 = (f32[64,16,128]{2,1,0:T(8,128)S(1)}, f32[16,1024]{1,0:T(8,128)S(1)}, f32[4,1024]{1,0:T(4,128)S(1)}, f32[4,1024]{1,0:T(4,128)S(1)}) custom-call(f32[64,16,128]{2,1,0:T(8,128)S(1)} %own.1.refs_0_, bf16[304,128]{1,0:T(8,128)(2,1)S(1)} %collective-permute-done.1.refs_1_, bf16[304,128]{1,0:T(8,128)(2,1)S(1)} %collective-permute-done.2.refs_2_, ...), custom_call_target="tpu_custom_call" | custom-call | tf_op jit(solution)/shard_map/deposit/pallas_call | solution.py:26
  18.9 0.0 collective-permute-done.refs_1_
  18.9 0.1 relay.3
  19.1 2.0 %collective-permute-start.5 = (f32[39,128]{1,0:T(8,128)S(1)}, f32[39,128]{1,0:T(8,128)S(1)}, u32[]{:S(2)}, u32[]{:S(2)}) collective-permute-start(f32[39,128]{1,0:T(8,128)S(1)} %get-tuple-element.30), channel_id=1, source_target_pairs={{0,8},{1,9},{2,10},{3,11},{4,12},{5,13},{6,14},{7,15},{8,0},{9,1},... | collective-permute-start | bytes 59912 | tf_op jit(solution)/shard_map/ppermute | solution.py:379
  21.1 3.4 %sweeps.1.refs_0_ = f32[64,8,128]{2,1,0:T(8,128)S(1)} custom-call(f32[64,16,128]{2,1,0:T(8,128)S(1)} %get-tuple-element.31.refs_0_), custom_call_target="tpu_custom_call" | custom-call | tf_op jit(solution)/shard_map/sweeps/pallas_call | solution.py:26
  24.5 0.0 collective-permute-done.5.refs_1_
  24.5 0.1 relay.4
  24.6 2.7 %collective-permute-start.6 = (f32[39,128]{1,0:T(8,128)S(1)}, f32[39,128]{1,0:T(8,128)S(1)}, u32[]{:S(2)}, u32[]{:S(2)}) collective-permute-start(f32[39,128]{1,0:T(8,128)S(1)} %get-tuple-element.34), channel_id=1, source_target_pairs={{0,4},{1,5},{2,6},{3,7},{4,0},{5,1},{6,2},{7,3},{8,12},{9,13},{10,... | collective-permute-start | bytes 59912 | tf_op jit(solution)/shard_map/ppermute | solution.py:379
  27.3 0.0 collective-permute-start.7
  27.3 1.6 %collective-permute-start.8 = (f32[4,1024]{1,0:T(4,128)S(1)}, f32[4,1024]{1,0:T(4,128)S(1)}, u32[]{:S(2)}, u32[]{:S(2)}) collective-permute-start(f32[4,1024]{1,0:T(4,128)S(1)} %get-tuple-element.36), channel_id=1, source_target_pairs={{0,3},{1,2},{2,1},{3,0},{4,7},{5,6},{6,5},{7,4},{8,11},{9,10},{10,... | collective-permute-start | bytes 49160 | tf_op jit(solution)/shard_map/ppermute | solution.py:379
  28.9 0.0 collective-permute-done.7.refs_2_
  28.9 1.6 %collective-permute-done.8.refs_3_ = f32[4,1024]{1,0:T(4,128)S(1)} collective-permute-done((f32[4,1024]{1,0:T(4,128)S(1)}, f32[4,1024]{1,0:T(4,128)S(1)}, u32[]{:S(2)}, u32[]{:S(2)}) %collective-permute-start.8) | collective-permute-done | bytes 16416 | tf_op jit(solution)/shard_map/ppermute | solution.py:379
  30.4 2.0 %strips.1 = f32[64,8,128]{2,1,0:T(8,128)} custom-call(f32[64,8,128]{2,1,0:T(8,128)S(1)} %sweeps.1.refs_0_, f32[16,1024]{1,0:T(8,128)S(1)} %get-tuple-element.27.refs_1_, f32[4,1024]{1,0:T(4,128)S(1)} %collective-permute-done.7.refs_2_, f32[4,1024]{1,0:T(4,128)S(1)} %collective-permute-done.8.refs_3_), custom_call_target="tpu_custom_call" | custom-call | tf_op jit(solution)/shard_map/strips/pallas_call | solution.py:26
  32.4 0.0 collective-permute-done.6.refs_1_
  32.4 0.7 %relay.5 = f32[39,256]{1,0:T(8,128)} custom-call(f32[39,256]{1,0:T(8,128)S(1)} %get-tuple-element.33.refs_0_, f32[39,128]{1,0:T(8,128)S(1)} %collective-permute-done.6.refs_1_), custom_call_target="tpu_custom_call" | custom-call | tf_op jit(solution)/shard_map/relay/pallas_call | solution.py:26
Async XLA Ops:
  3.9 11.2 %collective-permute-start.1 = (bf16[304,128]{1,0:T(8,128)(2,1)S(1)}, bf16[304,128]{1,0:T(8,128)(2,1)S(1)}, u32[]{:S(2)}, u32[]{:S(2)}) collective-permute-start(bf16[304,128]{1,0:T(8,128)(2,1)S(1)} %get-tuple-element.25), channel_id=1, source_target_pairs={{0,4},{1,5},{2,6},{3,7},{4,0},{5,1},{6,2},{7,3},{8,12},{9,13},{10,... | collective-permute-start | bytes 233480 | tf_op jit(solution)/shard_map/ppermute | solution.py:379
  7.0 8.2 %collective-permute-start.2 = (bf16[304,128]{1,0:T(8,128)(2,1)S(1)}, bf16[304,128]{1,0:T(8,128)(2,1)S(1)}, u32[]{:S(2)}, u32[]{:S(2)}) collective-permute-start(bf16[304,128]{1,0:T(8,128)(2,1)S(1)} %get-tuple-element.26), channel_id=1, source_target_pairs={{0,1},{1,0},{2,3},{3,2},{4,8},{5,9},{6,10},{7,11},{8,4},{9,5},{10,... | collective-permute-start | bytes 233480 | tf_op jit(solution)/shard_map/ppermute | solution.py:379
  7.0 0.7 %copy-start = (s32[128]{0:T(128)S(1)}, s32[128]{0:T(128)}, u32[]{:S(2)}) copy-start(s32[128]{0:T(128)} %param.18) | copy-start | bytes 1540
  7.0 0.7 %copy-start.1 = (s32[128,1]{0,1:T(1,128)S(1)}, s32[128,1]{0,1:T(1,128)}, u32[]{:S(2)}) copy-start(s32[128,1]{0,1:T(1,128)} %param.19) | copy-start | bytes 1540
  8.4 10.5 %collective-permute-start = (f32[39,128]{1,0:T(8,128)S(1)}, f32[39,128]{1,0:T(8,128)S(1)}, u32[]{:S(2)}, u32[]{:S(2)}) collective-permute-start(f32[39,128]{1,0:T(8,128)S(1)} %get-tuple-element.23), channel_id=1, source_target_pairs={{0,16},{1,17},{2,18},{3,19},{4,20},{5,21},{6,22},{7,23},{8,24},{9,... | collective-permute-start | bytes 59912 | tf_op jit(solution)/shard_map/ppermute | solution.py:379
  11.4 3.7 %collective-permute-start.3 = (bf16[48,128]{1,0:T(8,128)(2,1)S(1)}, bf16[48,128]{1,0:T(8,128)(2,1)S(1)}, u32[]{:S(2)}, u32[]{:S(2)}) collective-permute-start(bf16[48,128]{1,0:T(8,128)(2,1)S(1)} %get-tuple-element.24.own_list), channel_id=1, source_target_pairs={{0,8},{1,9},{2,10},{3,11},{4,12},{5,13},{6,14},{7,15},{8,0},{9,1},... | collective-permute-start | bytes 36872 | tf_op jit(solution)/shard_map/ppermute | solution.py:379
  13.0 2.1 %collective-permute-start.4 = (bf16[48,128]{1,0:T(8,128)(2,1)S(1)}, bf16[48,128]{1,0:T(8,128)(2,1)S(1)}, u32[]{:S(2)}, u32[]{:S(2)}) collective-permute-start(bf16[48,128]{1,0:T(8,128)(2,1)S(1)} %get-tuple-element.24.own_list), channel_id=1, source_target_pairs={{0,1},{1,0},{2,3},{3,2},{4,5},{5,4},{6,7},{7,6},{8,16},{9,17},{10,... | collective-permute-start | bytes 36872 | tf_op jit(solution)/shard_map/ppermute | solution.py:379
  19.1 5.4 %collective-permute-start.5 = (f32[39,128]{1,0:T(8,128)S(1)}, f32[39,128]{1,0:T(8,128)S(1)}, u32[]{:S(2)}, u32[]{:S(2)}) collective-permute-start(f32[39,128]{1,0:T(8,128)S(1)} %get-tuple-element.30), channel_id=1, source_target_pairs={{0,8},{1,9},{2,10},{3,11},{4,12},{5,13},{6,14},{7,15},{8,0},{9,1},... | collective-permute-start | bytes 59912 | tf_op jit(solution)/shard_map/ppermute | solution.py:379
  24.6 7.8 %collective-permute-start.6 = (f32[39,128]{1,0:T(8,128)S(1)}, f32[39,128]{1,0:T(8,128)S(1)}, u32[]{:S(2)}, u32[]{:S(2)}) collective-permute-start(f32[39,128]{1,0:T(8,128)S(1)} %get-tuple-element.34), channel_id=1, source_target_pairs={{0,4},{1,5},{2,6},{3,7},{4,0},{5,1},{6,2},{7,3},{8,12},{9,13},{10,... | collective-permute-start | bytes 59912 | tf_op jit(solution)/shard_map/ppermute | solution.py:379
  27.3 1.6 %collective-permute-start.7 = (f32[4,1024]{1,0:T(4,128)S(1)}, f32[4,1024]{1,0:T(4,128)S(1)}, u32[]{:S(2)}, u32[]{:S(2)}) collective-permute-start(f32[4,1024]{1,0:T(4,128)S(1)} %get-tuple-element.35), channel_id=1, source_target_pairs={{0,1},{1,0},{2,3},{3,2},{4,5},{5,4},{6,7},{7,6},{8,9},{9,8},{10,11... | collective-permute-start | bytes 49160 | tf_op jit(solution)/shard_map/ppermute | solution.py:379
  27.3 3.2 %collective-permute-start.8 = (f32[4,1024]{1,0:T(4,128)S(1)}, f32[4,1024]{1,0:T(4,128)S(1)}, u32[]{:S(2)}, u32[]{:S(2)}) collective-permute-start(f32[4,1024]{1,0:T(4,128)S(1)} %get-tuple-element.36), channel_id=1, source_target_pairs={{0,3},{1,2},{2,1},{3,0},{4,7},{5,6},{6,5},{7,4},{8,11},{9,10},{10,... | collective-permute-start | bytes 49160 | tf_op jit(solution)/shard_map/ppermute | solution.py:379

commit v3 on v2

--- a/solution.py
+++ b/solution.py
@@ -72,13 +72,13 @@
 
 
 def advance_kernel(
-    count_ref, cell_hbm, coupling_hbm, basal_hbm, half_hbm, decay_hbm, weight_hbm, voxel_hbm, oxygen_hbm,
-    new_state, message_even, message_odd, message_far,
-    cell, coupling, basal, half, decay, weight, voxel, oxygen, drive, semaphores, *, cy, cx, nz,
+    count_ref, cell_hbm, coupling_hbm, basal_hbm, half_hbm, decay_hbm, weight_hbm, voxel_hbm, oxygen_hbm, ids_hbm,
+    targets_hbm, new_state, message_even, message_odd, message_far, buffer,
+    cell, coupling, basal, half, decay, weight, voxel, oxygen, ids, targets, drive, semaphores, *, cy, cx, nz, capacity,
 ):
     pairs = (
         (cell_hbm, cell), (coupling_hbm, coupling), (basal_hbm, basal), (half_hbm, half), (decay_hbm, decay),
-        (weight_hbm, weight), (voxel_hbm, voxel), (oxygen_hbm, oxygen),
+        (weight_hbm, weight), (voxel_hbm, voxel), (oxygen_hbm, oxygen), (ids_hbm, ids), (targets_hbm, targets),
     )
     copies = [pltpu.make_async_copy(a, b, semaphores.at[i]) for i, (a, b) in enumerate(pairs)]
     for copy in copies:
@@ -130,15 +130,19 @@
     head = nz // 2 * cx
     message_even[:head, :] = jnp.where(even, to_next, to_previous).astype(bf16)
     message_odd[:head, :] = jnp.where(even, to_previous, to_next).astype(bf16)
-    message_even[head:, :] = listing
+    tail = head + 3 * rows
+    message_even[head:tail, :] = listing
     message_odd[head:, :] = listing
     message_far[...] = listing
-
-
-def one_hots(lists, which, base, width, m, left, right, slot):
+    placed = place_daughters(current, ids[...], targets[...], capacity, buffer.shape[1])
+    buffer[...] = placed
+    put_pieces(message_even, tail, first_send(placed, lax.axis_index("gx") % 2 == 1, capacity))
+
+
+def one_hots(lists, which, first, m, base, width, left, right, slot):
     rows = lists.shape[1] // 3
     pack = 16
-    row_at = (lax.broadcasted_iota(i32, (m, LANES), 0) - m // 2).astype(f32).astype(bf16).reshape(m // pack, pack, LANES)
+    row_at = (lax.broadcasted_iota(i32, (m, LANES), 0) + first).astype(f32).astype(bf16).reshape(m // pack, pack, LANES)
     col_at = (lax.broadcasted_iota(i32, (width, LANES), 0) + base).astype(f32).astype(bf16)
     col_at = col_at.reshape(width // pack, pack, LANES)
     one, zero = jnp.ones((), bf16), jnp.zeros((), bf16)
@@ -158,64 +162,94 @@
     return lax.dot_general(left, right, (((1,), (1,)), ((), ())), preferred_element_type=f32)
 
 
-def own_kernel(oxygen_hbm, own_list, base, lists, left, right, oxygen, semaphore):
-    copy = pltpu.make_async_copy(oxygen_hbm, oxygen, semaphore)
+def own_kernel(oxygen_hbm, own_list, state, base, new_state, lists, left, right, oxygen, semaphores):
+    copy = pltpu.make_async_copy(oxygen_hbm, oxygen, semaphores.at[0])
     copy.start()
+    store = pltpu.make_async_copy(state, new_state, semaphores.at[1])
+    store.start()
     nz, cx, cy = oxygen.shape
+    m = nz * cx
     lists[0] = own_list[...].astype(f32)
-    one_hots(lists, 0, -cy, 2 * cy, nz * cx, left, right, 0)
+    one_hots(lists, 0, -m // 2, m, -cy, 2 * cy, left, right, 0)
     total = product(left[...], right[...])
     copy.wait()
     low = lax.broadcasted_iota(i32, (nz, cx, cy), 1) < cx // 2
     inner = pltpu.roll(oxygen[...], cx // 2, 1)
     base[:, :cx, :] = jnp.where(low, 0.0, inner) - total[:, :cy].reshape(nz, cx, cy)
     base[:, cx:, :] = jnp.where(low, inner, 0.0) - total[:, cy:].reshape(nz, cx, cy)
-
-
-def deposit_kernel(
-    base, near_e, near_o, far_e, far_o, field, strips, strip_even, strip_odd,
-    lists, left, right, far_left, far_right, *, grid_count,
+    store.wait()
+
+
+def keep(listing, rows, valid):
+    index = lax.broadcasted_iota(i32, listing.shape, 0)
+    return jnp.where((index < rows) & jnp.logical_not(valid), 0.0, listing)
+
+
+def relay_first_kernel(buffer, got, listing, merged, message, *, capacity, head):
+    g = lax.axis_index("gx")
+    species = buffer.shape[0]
+    count = listing.shape[0]
+    value = take_in(buffer[...], get_pieces(got, head + count, species), g % 2 == 1, capacity)
+    merged[...] = value
+    message[:count, :] = listing[...]
+    put_pieces(message, count, first_send(value, (g // 2) % 2 == 1, 2 * capacity))
+
+
+def near_kernel(base, listing, near_e, near_o, field, lists, left, right, *, grid_count):
+    nz, cx, cy = base.shape[0], base.shape[1] // 2, base.shape[2]
+    m, head = nz * cx, nz // 2 * cx
+    count = listing.shape[0]
+    rows = count // 3
+    g = lax.axis_index("gx")
+    even = g % 2 == 0
+    e, o = near_e[head : head + count, :].astype(f32), near_o[head : head + count, :].astype(f32)
+    lists[0] = keep(jnp.where(even, e, o), rows, g + 1 < grid_count)
+    lists[1] = keep(jnp.where(even, o, e), rows, g >= 1)
+    one_hots(lists, 0, -m // 2, m, -2 * cy, 2 * cy, left, right, 0)
+    one_hots(lists, 1, -m // 2, m, 0, 2 * cy, left, right, 1)
+    total = product(left[...], right[...])
+    field[:, :cx, :] = base[:, :cx, :] - total[:, :cy].reshape(nz, cx, cy)
+    field[:, cx:, :] = base[:, cx:, :] - total[:, cy:].reshape(nz, cx, cy)
+
+
+def far_kernel(
+    base, buffer, near_e, near_o, far_e, far_o, field, strips, strip_even, strip_odd, merged, send,
+    lists, left, right, *, grid_count, capacity, after,
 ):
     nz, cx, cy = base.shape[0], base.shape[1] // 2, base.shape[2]
     half, zh = cx // 2, nz // 2
-    head = zh * cx
-    m = nz * cx
-    rows = far_e.shape[0] // 3
+    head, m = zh * cx, nz * cx
+    count = far_o.shape[0]
+    rows = count // 3
+    agents = rows * LANES
     g = lax.axis_index("gx")
     even = g % 2 == 0
     low_pair = g % 4 < 2
-    has_next, has_previous = g + 1 < grid_count, g >= 1
-    has_next2, has_previous2 = g + 2 < grid_count, g >= 2
-
-    def keep(listing, valid):
-        index = lax.broadcasted_iota(i32, listing.shape, 0)
-        return jnp.where((index < rows) & jnp.logical_not(valid), 0.0, listing)
-
-    e, o = near_e[...].astype(f32), near_o[...].astype(f32)
-    after, before = jnp.where(even, e, o), jnp.where(even, o, e)
-    fe, fo = far_e[...].astype(f32), far_o[...].astype(f32)
-    lists[0] = keep(after[head:], has_next)
-    lists[1] = keep(before[head:], has_previous)
-    lists[2] = keep(jnp.where(low_pair, fe, fo), has_next2)
-    lists[3] = keep(jnp.where(low_pair, fo, fe), has_previous2)
-    one_hots(lists, 0, -2 * cy, 2 * cy, m, left, right, 0)
-    one_hots(lists, 1, 0, 2 * cy, m, left, right, 1)
-    total = product(left[...], right[...])
-    one_hots(lists, 2, -2 * cy, cy, m, far_left, far_right, 0)
-    total1 = total[:, cy:] + product(far_left[...], far_right[...])
-    one_hots(lists, 3, cy, cy, m, far_left, far_right, 0)
-    total0 = total[:, :cy] + product(far_left[...], far_right[...])
-
-    low = lax.broadcasted_iota(i32, (zh, cx, cy), 1) < half
-    from_before = jnp.where(has_previous, before[:head] + 1.0, 0.0).reshape(zh, cx, cy)
-    from_after = jnp.where(has_next, after[:head] + 1.0, 0.0).reshape(zh, cx, cy)
-    before_b = pltpu.roll(from_before, half, 1)
-    after_a = pltpu.roll(from_after, half, 1)
+    fe, fo = far_e[:count, :].astype(f32), far_o[...].astype(f32)
+    for which, listing, valid in (
+        (0, jnp.where(low_pair, fe, fo), g + 2 < grid_count),
+        (1, jnp.where(low_pair, fo, fe), g >= 2),
+    ):
+        code = listing[rows : 2 * rows].astype(i32) + m // 2
+        at_z = code // cx
+        code = (at_z % zh) * cx + (at_z // zh) * half + code % half
+        lists[which, :rows] = jnp.where(valid, listing[:rows], 0.0)
+        lists[which, rows : 2 * rows] = code.astype(f32)
+        lists[which, 2 * rows :] = listing[2 * rows :]
+    one_hots(lists, 0, 0, head, -2 * cy, cy, left, right, 0)
+    one_hots(lists, 1, 0, head, cy, cy, left, right, 1)
+    past_after = product(left[:, :agents], right[:, :agents])
+    past_before = product(left[:, agents:], right[:, agents:])
+
+    e, o = near_e[:head, :].astype(f32), near_o[:head, :].astype(f32)
     shape = (zh, cx, cy)
-    field[:zh, :cx] = base[:zh, :cx] + jnp.where(low, from_before, 0.0) - total0[:head].reshape(shape)
-    field[zh:, :cx] = base[zh:, :cx] + jnp.where(low, before_b, 0.0) - total0[head:].reshape(shape)
-    field[:zh, cx:] = base[:zh, cx:] + jnp.where(low, 0.0, after_a) - total1[:head].reshape(shape)
-    field[zh:, cx:] = base[zh:, cx:] + jnp.where(low, 0.0, from_after) - total1[head:].reshape(shape)
+    from_before = (jnp.where(g >= 1, jnp.where(even, o, e) + 1.0, 0.0) - past_before).reshape(shape)
+    from_after = (jnp.where(g + 1 < grid_count, jnp.where(even, e, o) + 1.0, 0.0) - past_after).reshape(shape)
+    low = lax.broadcasted_iota(i32, shape, 1) < half
+    field[:zh, :cx] = base[:zh, :cx] + jnp.where(low, from_before, 0.0)
+    field[zh:, :cx] = base[zh:, :cx] + jnp.where(low, pltpu.roll(from_before, half, 1), 0.0)
+    field[:zh, cx:] = base[:zh, cx:] + jnp.where(low, 0.0, pltpu.roll(from_after, half, 1))
+    field[zh:, cx:] = base[zh:, cx:] + jnp.where(low, 0.0, from_after)
 
     edge = 2 * sweeps
     picked = lax.broadcasted_iota(i32, (2 * edge, cy), 0)
@@ -228,46 +262,36 @@
     head_rows, tail_rows = rims[:sweeps], rims[2 * edge - sweeps :]
     strip_even[...] = jnp.where(h_even, tail_rows, head_rows)
     strip_odd[...] = jnp.where(h_even, head_rows, tail_rows)
-
-
-def sweep_kernel(field, out, ping, pong, *, grid_count):
+    value = take_in(buffer[...], get_pieces(far_e, count, buffer.shape[0]), (g // 2) % 2 == 1, 2 * capacity)
+    merged[...] = value
+    send[...] = first_send(value, (g // after) % 2 == 1, after * capacity)
+
+
+def sweep_kernel(field, out, *, grid_count):
     nz, width, cy = field.shape
-    cx = width // 2
+    half = width // 4
     g = lax.axis_index("gx")
-    top = width
-    sub = lax.broadcasted_iota(i32, (cx, cy), 0)
-    masks = (
-        jnp.where((g == 0) & (sub < cx // 2), 0.0, diffusion_number),
-        jnp.where((g == grid_count - 1) & (sub >= cx // 2), 0.0, diffusion_number),
+    at_x = lax.broadcasted_iota(i32, (nz, width, cy), 1)
+    outside = (g == 0) & (at_x < half) | (g == grid_count - 1) & (at_x >= width - half)
+    scale = jnp.where(outside, 0.0, diffusion_number)
+    centre = 1.0 / diffusion_number - 6.0
+    plane = jnp.zeros((1, width, cy), f32)
+    value = field[...]
+    for turn in range(sweeps):
+        total = jnp.concatenate([plane, value[:-1]], axis=0) + jnp.concatenate([value[1:], plane], axis=0)
+        total = total + (pltpu.roll(value, 1, 1) + pltpu.roll(value, width - 1, 1))
+        total = total + (pltpu.roll(value, 1, 2) + pltpu.roll(value, cy - 1, 2))
+        value = (total + centre * value) * scale
+    low = lax.broadcasted_iota(i32, (nz, width // 2, cy), 1) < half
+    out[...] = pltpu.roll(jnp.where(low, value[:, width // 2 :], value[:, : width // 2]), half, 1)
+
+
+def strip_kernel(
+    inside, strips, got_even, got_odd, buffer, got, out, daughters, *, grid_count, row_count, capacity, step,
+):
+    daughters[...] = take_in(
+        buffer[...], got[...], (lax.axis_index("gx") // step) % 2 == 1, capacity * step
     )
-    centre = 1.0 / diffusion_number - 6.0
-    zero = jnp.zeros((width, cy), f32)
-    for buffer in (ping, pong):
-        buffer[:top, :] = zero
-        buffer[top + nz * width : top + nz * width + width, :] = zero
-    ping[top : top + nz * width, :] = field[...].reshape(nz * width, cy)
-
-    def one_sweep(source, target):
-        def plane(z, carry):
-            for tile in range(2):
-                at = (z + 1) * width + tile * cx
-                c = source[pl.ds(at, cx), :]
-                total = source[pl.ds(at - width, cx), :] + source[pl.ds(at + width, cx), :]
-                total = total + (source[pl.ds(at - 1, cx), :] + source[pl.ds(at + 1, cx), :])
-                total = total + (pltpu.roll(c, 1, 1) + pltpu.roll(c, cy - 1, 1))
-                target[pl.ds(at, cx), :] = (total + centre * c) * masks[tile]
-            return carry
-
-        lax.fori_loop(0, nz, plane, 0, unroll=8)
-
-    for turn in range(sweeps):
-        one_sweep(*((ping, pong) if turn % 2 == 0 else (pong, ping)))
-    main = ping if sweeps % 2 == 0 else pong
-    for z in range(nz):
-        out[z] = main[pl.ds((z + 1) * width + cx // 2, cx), :]
-
-
-def strip_kernel(inside, strips, got_even, got_odd, out, *, grid_count, row_count):
     nz, cx, cy = inside.shape
     m = strips.shape[1]
     width = m // nz
@@ -313,6 +337,20 @@
     return high, middle, (rest - middle.astype(f32)).astype(bf16)
 
 
+PIECE_ROWS = 48
+
+
+def put_pieces(message, at, value):
+    for number, piece in enumerate(pieces(value)):
+        start = at + number * PIECE_ROWS
+        message[start : start + value.shape[0], :] = piece
+
+
+def get_pieces(message, at, count):
+    starts = [at + number * PIECE_ROWS for number in range(3)]
+    return sum(message[start : start + count, :].astype(f32) for start in starts)
+
+
 def first_send(buffer, mine, width):
     count = buffer.shape[1]
     half = count // 2
@@ -338,38 +376,26 @@
     return jnp.concatenate([left, right], axis=1)
 
 
-def daughter_kernel(state, ids, targets, new_state, buffer, send, semaphore, *, capacity, step):
-    copy = pltpu.make_async_copy(state, new_state, semaphore)
-    copy.start()
+def place_daughters(state, ids, target, capacity, columns):
     species, agents = state.shape
     picks = ids.shape[1]
-    columns = buffer.shape[1]
-    target = targets[...]
     square = (picks, picks)
     across = jnp.broadcast_to(target, square)
     down = jnp.broadcast_to(column(target, picks), square)
     earlier = lax.broadcasted_iota(i32, square, 0) < lax.broadcasted_iota(i32, square, 1)
     rank = jnp.sum(jnp.where((across == down) & earlier, 1, 0), axis=0, keepdims=True)
     position = target * capacity + rank
-    chosen = (lax.broadcasted_iota(i32, (agents, picks), 0) == ids[...]).astype(f32).astype(bf16)
-    mothers = sum(jnp.dot(p, chosen, preferred_element_type=f32) for p in pieces(state[...]))
+    chosen = (lax.broadcasted_iota(i32, (agents, picks), 0) == ids).astype(f32).astype(bf16)
+    mothers = sum(jnp.dot(p, chosen, preferred_element_type=f32) for p in pieces(state))
     placing = (lax.broadcasted_iota(i32, (columns, picks), 0) == position).astype(f32).astype(bf16)
-    placed = sum(
-        lax.dot_general(p, placing, (((1,), (1,)), ((), ())), preferred_element_type=f32)
-        for p in pieces(mothers)
-    )
-    buffer[...] = placed
-    mine = (lax.axis_index("gx") // step) % 2 == 1
-    send[...] = first_send(placed, mine, capacity * step)
-    copy.wait()
-
-
-def relay_kernel(buffer, got, merged, *send, capacity, step, after):
+    return sum(product(p, placing) for p in pieces(mothers))
+
+
+def relay_kernel(buffer, got, merged, send, *, capacity, step, after):
     g = lax.axis_index("gx")
     value = take_in(buffer[...], got[...], (g // step) % 2 == 1, capacity * step)
     merged[...] = value
-    if after:
-        send[0][...] = first_send(value, (g // after) % 2 == 1, capacity * after)
+    send[...] = first_send(value, (g // after) % 2 == 1, capacity * after)
 
 
 def solution(mesh):
@@ -404,79 +430,90 @@
             return run
 
         m = nz * cx
-        state, message_even, message_odd, listing = call(
-            kernel(advance_kernel, cy=cy, cx=cx, nz=nz),
-            [((species, agents), f32), ((head + 3 * rows, LANES), bf16), ((head + 3 * rows, LANES), bf16),
-             ((3 * rows, LANES), bf16)],
+        count = 3 * rows
+        pieces_rows = 3 * PIECE_ROWS
+        one_field = (nz, 2 * cx, cy)
+        listed = (count, LANES)
+        half_buffer = ((species, columns // 2), f32)
+        assert species <= PIECE_ROWS and columns == 2 * LANES and grid_count >= 8
+
+        state, message_even, message_odd, listing, buffer = call(
+            kernel(advance_kernel, cy=cy, cx=cx, nz=nz, capacity=capacity),
+            [((species, agents), f32), ((head + count + pieces_rows, LANES), bf16), ((head + count, LANES), bf16),
+             (listed, bf16), ((species, columns), f32)],
             "advance",
             [agent_counts, cell_state, coupling, line(basal_rate), line(half_sat), line(decay_rate),
-             line(uptake_weight), voxel_index.reshape(rows, LANES), oxygen],
+             line(uptake_weight), voxel_index.reshape(rows, LANES), oxygen, line(divider_ids), line(destinations)],
             smem=(0,),
-            hbm=range(1, 9),
+            hbm=range(1, 11),
             scratch=[pltpu.VMEM((species, agents), f32), pltpu.VMEM((species, species), f32)]
             + [pltpu.VMEM((1, species), f32)] * 4
-            + [pltpu.VMEM((rows, LANES), i32), pltpu.VMEM((nz, cx, cy), f32), pltpu.VMEM((rows, LANES), f32),
-               pltpu.SemaphoreType.DMA((8,))],
+            + [pltpu.VMEM((rows, LANES), i32), pltpu.VMEM((nz, cx, cy), f32)]
+            + [pltpu.VMEM((1, picks), i32)] * 2
+            + [pltpu.VMEM((rows, LANES), f32), pltpu.SemaphoreType.DMA((10,))],
         )
         near_e = swap(message_even, near_even)
         near_o = swap(message_odd, near_odd)
-        far_e = swap(listing, far_even)
+        base, new_state = call(
+            own_kernel,
+            [(one_field, f32), ((species, agents), f32)],
+            "own",
+            [oxygen, listing, state],
+            hbm=(0, 4),
+            scratch=[pltpu.VMEM((1,) + listed, f32), pltpu.VMEM((m, agents), bf16), pltpu.VMEM((2 * cy, agents), bf16),
+                     pltpu.VMEM((nz, cx, cy), f32), pltpu.SemaphoreType.DMA((2,))],
+        )
+        buffer, base = lax.optimization_barrier((buffer, base))
+        buffer, message_far = call(
+            kernel(relay_first_kernel, capacity=capacity, head=head),
+            [((species, columns), f32), ((count + pieces_rows, LANES), bf16)],
+            "relay",
+            [buffer, near_e, listing],
+        )
+        far_e = swap(message_far, far_even)
         far_o = swap(listing, far_odd)
-
-        step = grid_count // 2
-        new_state, buffer, send = call(
-            kernel(daughter_kernel, capacity=capacity, step=step),
-            [((species, agents), f32), ((species, columns), f32), ((species, columns // 2), f32)],
-            "daughters",
-            [state, line(divider_ids), line(destinations)],
-            hbm=(3,),
-            scratch=[pltpu.SemaphoreType.DMA],
-        )
-        (base,) = call(
-            own_kernel,
-            [((nz, 2 * cx, cy), f32)],
-            "own",
-            [oxygen, listing],
-            hbm=(0,),
-            scratch=[pltpu.VMEM((1, 3 * rows, LANES), f32), pltpu.VMEM((m, agents), bf16), pltpu.VMEM((2 * cy, agents), bf16),
-                     pltpu.VMEM((nz, cx, cy), f32), pltpu.SemaphoreType.DMA],
-        )
-        field, strips, strip_even, strip_odd = call(
-            kernel(deposit_kernel, grid_count=grid_count),
-            [((nz, 2 * cx, cy), f32), ((4 * sweeps, 2 * m), f32), ((sweeps, 2 * m), f32), ((sweeps, 2 * m), f32)],
-            "deposit",
-            [base, near_e, near_o, far_e, far_o],
-            scratch=[pltpu.VMEM((4, 3 * rows, LANES), f32), pltpu.VMEM((m, 2 * agents), bf16),
-                     pltpu.VMEM((2 * cy, 2 * agents), bf16), pltpu.VMEM((m, agents), bf16), pltpu.VMEM((cy, agents), bf16)],
+        base, _ = lax.optimization_barrier((base, message_far))
+        (field,) = call(
+            kernel(near_kernel, grid_count=grid_count),
+            [(one_field, f32)],
+            "near",
+            [base, listing, near_e, near_o],
+            scratch=[pltpu.VMEM((2,) + listed, f32), pltpu.VMEM((m, 2 * agents), bf16),
+                     pltpu.VMEM((2 * cy, 2 * agents), bf16)],
+        )
+        step = 4
+        field, strips, strip_even, strip_odd, buffer, send = call(
+            kernel(far_kernel, grid_count=grid_count, capacity=capacity, after=step),
+            [(one_field, f32), ((4 * sweeps, 2 * m), f32), ((sweeps, 2 * m), f32), ((sweeps, 2 * m), f32),
+             ((species, columns), f32)] + [half_buffer],
+            "far",
+            [field, buffer, near_e, near_o, far_e, far_o],
+            scratch=[pltpu.VMEM((2,) + listed, f32), pltpu.VMEM((head, 2 * agents), bf16),
+                     pltpu.VMEM((cy, 2 * agents), bf16)],
         )
         got_even = swap(strip_even, side_even)
         got_odd = swap(strip_odd, side_odd)
-        reach = (nz + 2) * 2 * cx
+        got = swap(send, lambda g, h: (g ^ step, h))
         (inside,) = call(
-            kernel(sweep_kernel, grid_count=grid_count),
-            [((nz, cx, cy), f32)],
-            "sweeps",
-            [field],
-            scratch=[pltpu.VMEM((reach, cy), f32), pltpu.VMEM((reach, cy), f32)],
-        )
-        (new_oxygen,) = call(
-            kernel(strip_kernel, grid_count=grid_count, row_count=row_count),
-            [((nz, cx, cy), f32)],
+            kernel(sweep_kernel, grid_count=grid_count), [((nz, cx, cy), f32)], "sweeps", [field]
+        )
+        while step < grid_count // 2:
+            after = 2 * step
+            buffer, sent = call(
+                kernel(relay_kernel, capacity=capacity, step=step, after=after),
+                [((species, columns), f32), half_buffer],
+                "relay",
+                [buffer, got],
+            )
+            step = after
+            got = swap(sent, lambda g, h: (g ^ step, h))
+        new_oxygen, daughter_state = call(
+            kernel(strip_kernel, grid_count=grid_count, row_count=row_count, capacity=capacity, step=step),
+            [((nz, cx, cy), f32), ((species, columns), f32)],
             "strips",
-            [inside, strips, got_even, got_odd],
-        )
-        stages = [strips, inside]
-        while step:
-            after = step // 2
-            got = swap(send, lambda g, h: (g ^ step, h))
-            if stages:
-                got, _ = lax.optimization_barrier((got, stages.pop(0)))
-            outs = [((species, columns), f32)] + ([((species, columns // 2), f32)] if after else [])
-            result = call(kernel(relay_kernel, capacity=capacity, step=step, after=after), outs, "relay", [buffer, got])
-            buffer = result[0]
-            send = result[-1]
-            step = after
-        return new_state, buffer, new_oxygen
+            [inside, strips, got_even, got_odd, buffer, got],
+        )
+        return new_state, daughter_state, new_oxygen
 
     return jax.shard_map(
         shards,

time: 33.3 us -> 26.5 us (0.80)
  Pallas kernels: 14.5 us -> 10.6 us
  starting transfers between devices: 14 us -> 10.4 us
  waiting for transfers between devices: 2.65 us -> 3.97 us
  local copies, waits for them, and re-layouts: 0.67 us -> 0 us
    pallas_call x9 -> x7, Pallas kernels: 14.5 us -> 10.6 us  [call(): pl.pallas_call(body, out_shape=tuple((jax.ShapeDtypeStruct(s, t) for s, t...]
    ppermute x9 -> x7, starting transfers between devices: 14 us -> 10.4 us  [swap(): return lax.ppermute(value, GRID, swap_pairs(grid_count, row_count, partner))]
    ppermute x9 -> x7, waiting for transfers between devices: 2.65 us -> 3.97 us  [swap(): return lax.ppermute(value, GRID, swap_pairs(grid_count, row_count, partner))]
    unnamed x4 -> x0, local copies, waits for them, and re-layouts: 0.67 us -> none
  transfers between devices with their start and end apart: 9 -> 7, of which waited for: 2 -> 3; matrix products, arithmetic and copies ran while one was open for 0% -> 0% of each run, Pallas kernels for 33% -> 16%
where the time goes in v3:
time: 26.5 us; the launch traced here: 26.3 us
  Pallas kernels  10.6 us (40%)
  starting transfers between devices  10.4 us (39%)
  waiting for transfers between devices  3.97 us (15%)
  between operations  1.34 us (5%)
    pallas_call x7, Pallas kernels, call(): pl.pallas_call(body, out_shape=tuple((jax.ShapeDtypeStruct(s, t) for s, t...  10.6 us
    ppermute x7, starting transfers between devices, swap(): return lax.ppermute(value, GRID, swap_pairs(grid_count, row_count, partner))  10.4 us
    ppermute x7, waiting for transfers between devices, swap(): return lax.ppermute(value, GRID, swap_pairs(grid_count, row_count, partner))  3.97 us
  transfers between devices with their start and end apart: 7, of which 3 were waited for; matrix products, arithmetic and copies ran while one was open for 0% of the time, Pallas kernels for 16%

profile of v3, /device:TPU:0, one launch (start us, length us, event | category | flops | bytes accessed | tf_op | source)
XLA Modules:
  0.0 26.3 jit_solution(17924778793323352478)
XLA Ops:
  1.3 3.2 %advance.1 = (f32[39,2048]{1,0:T(8,128)S(1)}, bf16[448,128]{1,0:T(8,128)(2,1)S(1)}, bf16[304,128]{1,0:T(8,128)(2,1)S(1)}, bf16[48,128]{1,0:T(8,128)(2,1)S(1)}, f32[39,256]{1,0:T(8,128)S(1)}) custom-call(s32[1]{0:T(128)S(6)} %copy.14.refs_0_, f32[39,2048]{1,0:T(8,128)} %refs_1_.1, f32[39,39]{1,0:T(8,128)} %refs_2_.1, f32[1,39]{1,0:T(1,128)} %bitcast.8, ...), custom_call_target="tpu_custom_call" | custom-call | tf_op jit(solution)/shard_map/advance/pallas_call | solution.py:26
  4.5 3.0 %collective-permute-start = (bf16[448,128]{1,0:T(8,128)(2,1)S(1)}, bf16[448,128]{1,0:T(8,128)(2,1)S(1)}, u32[]{:S(2)}, u32[]{:S(2)}) collective-permute-start(bf16[448,128]{1,0:T(8,128)(2,1)S(1)} %get-tuple-element.30), channel_id=1, source_target_pairs={{0,4},{1,5},{2,6},{3,7},{4,0},{5,1},{6,2},{7,3},{8,12},{9,13},{10,... | collective-permute-start | bytes 344072 | tf_op jit(solution)/shard_map/ppermute | solution.py:405
  7.5 0.0 collective-permute-start.1
  7.5 1.1 %own.1 = (f32[64,16,128]{2,1,0:T(8,128)S(1)}, f32[39,2048]{1,0:T(8,128)}) custom-call(f32[64,8,128]{2,1,0:T(8,128)} %oxygen_hbm.1, bf16[48,128]{1,0:T(8,128)(2,1)S(1)} %get-tuple-element.23.own_list.refs_2_.refs_1_, f32[39,2048]{1,0:T(8,128)S(1)} %get-tuple-element.24.state), custom_call_target="tpu_custom_call" | custom-call | tf_op jit(solution)/shard_map/own/pallas_call | solution.py:26
  8.6 2.9 %collective-permute-done.refs_1_.refs_2_ = bf16[448,128]{1,0:T(8,128)(2,1)S(1)} collective-permute-done((bf16[448,128]{1,0:T(8,128)(2,1)S(1)}, bf16[448,128]{1,0:T(8,128)(2,1)S(1)}, u32[]{:S(2)}, u32[]{:S(2)}) %collective-permute-start) | collective-permute-done | bytes 114720 | tf_op jit(solution)/shard_map/ppermute | solution.py:405
  11.6 0.1 relay.1
  11.7 1.8 %collective-permute-start.2 = (bf16[192,128]{1,0:T(8,128)(2,1)S(1)}, bf16[192,128]{1,0:T(8,128)(2,1)S(1)}, u32[]{:S(2)}, u32[]{:S(2)}) collective-permute-start(bf16[192,128]{1,0:T(8,128)(2,1)S(1)} %get-tuple-element.31), channel_id=1, source_target_pairs={{0,8},{1,9},{2,10},{3,11},{4,12},{5,13},{6,14},{7,15},{8,0},{9,1},... | collective-permute-start | bytes 147464 | tf_op jit(solution)/shard_map/ppermute | solution.py:405
  13.4 0.0 collective-permute-start.3
  13.4 0.0 collective-permute-done.1.refs_3_
  13.4 1.7 %near.1.refs_0_ = f32[64,16,128]{2,1,0:T(8,128)S(1)} custom-call(f32[64,16,128]{2,1,0:T(8,128)S(1)} %get-tuple-element.32.refs_0_, bf16[48,128]{1,0:T(8,128)(2,1)S(1)} %get-tuple-element.23.own_list.refs_2_.refs_1_, bf16[448,128]{1,0:T(8,128)(2,1)S(1)} %collective-permute-done.refs_1_.refs_2_, bf16[304,128]{1,0:T(8,128)(2,1)S(1)} %collective-permute-done.1.refs_3_), custom_call_target="tpu_custom_call" | custom-call | tf_op jit(solution)/shard_map/near/pallas_call | solution.py:26
  15.1 0.0 collective-permute-done.3.refs_5_
  15.1 0.7 %collective-permute-done.2.refs_4_ = bf16[192,128]{1,0:T(8,128)(2,1)S(1)} collective-permute-done((bf16[192,128]{1,0:T(8,128)(2,1)S(1)}, bf16[192,128]{1,0:T(8,128)(2,1)S(1)}, u32[]{:S(2)}, u32[]{:S(2)}) %collective-permute-start.2) | collective-permute-done | bytes 49184 | tf_op jit(solution)/shard_map/ppermute | solution.py:405
  15.8 1.3 %far.1 = (f32[64,16,128]{2,1,0:T(8,128)S(1)}, f32[16,1024]{1,0:T(8,128)S(1)}, f32[4,1024]{1,0:T(4,128)S(1)}, f32[4,1024]{1,0:T(4,128)S(1)}, f32[39,256]{1,0:T(8,128)S(1)}, /*index=5*/f32[39,128]{1,0:T(8,128)S(1)}) custom-call(f32[64,16,128]{2,1,0:T(8,128)S(1)} %near.1.refs_0_, f32[39,256]{1,0:T(8,128)S(1)} %get-tuple-element.34.refs_1_, ...), custom_call_target="tpu_custom_call" | custom-call | tf_op jit(solution)/shard_map/far/pallas_call | solution.py:26
  17.2 4.0 %collective-permute-start.6 = (f32[39,128]{1,0:T(8,128)S(1)}, f32[39,128]{1,0:T(8,128)S(1)}, u32[]{:S(2)}, u32[]{:S(2)}) collective-permute-start(f32[39,128]{1,0:T(8,128)S(1)} %get-tuple-element.40), channel_id=1, source_target_pairs={{0,16},{1,17},{2,18},{3,19},{4,20},{5,21},{6,22},{7,23},{8,24},{9,... | collective-permute-start | bytes 59912 | tf_op jit(solution)/shard_map/ppermute | solution.py:405
  21.1 0.0 collective-permute-start.4
  21.1 1.6 %collective-permute-start.5 = (f32[4,1024]{1,0:T(4,128)S(1)}, f32[4,1024]{1,0:T(4,128)S(1)}, u32[]{:S(2)}, u32[]{:S(2)}) collective-permute-start(f32[4,1024]{1,0:T(4,128)S(1)} %get-tuple-element.38), channel_id=1, source_target_pairs={{0,3},{1,2},{2,1},{3,0},{4,7},{5,6},{6,5},{7,4},{8,11},{9,10},{10,... | collective-permute-start | bytes 49160 | tf_op jit(solution)/shard_map/ppermute | solution.py:405
  22.7 1.2 %sweeps.1.refs_0_ = f32[64,8,128]{2,1,0:T(8,128)S(1)} custom-call(f32[64,16,128]{2,1,0:T(8,128)S(1)} %get-tuple-element.35.refs_0_), custom_call_target="tpu_custom_call" | custom-call | tf_op jit(solution)/shard_map/sweeps/pallas_call | solution.py:26
  23.9 0.0 collective-permute-done.4.refs_2_
  23.9 0.4 %collective-permute-done.5.refs_3_ = f32[4,1024]{1,0:T(4,128)S(1)} collective-permute-done((f32[4,1024]{1,0:T(4,128)S(1)}, f32[4,1024]{1,0:T(4,128)S(1)}, u32[]{:S(2)}, u32[]{:S(2)}) %collective-permute-start.5) | collective-permute-done | bytes 16416 | tf_op jit(solution)/shard_map/ppermute | solution.py:405
  24.3 0.0 collective-permute-done.6.refs_5_
  24.3 2.0 %strips.1 = (f32[64,8,128]{2,1,0:T(8,128)}, f32[39,256]{1,0:T(8,128)}) custom-call(f32[64,8,128]{2,1,0:T(8,128)S(1)} %sweeps.1.refs_0_, f32[16,1024]{1,0:T(8,128)S(1)} %get-tuple-element.36.refs_1_, f32[4,1024]{1,0:T(4,128)S(1)} %collective-permute-done.4.refs_2_, f32[4,1024]{1,0:T(4,128)S(1)} %collective-permute-done.5.refs_3_, ...), custom_call_target="tpu_custom_call" | custom-call | tf_op jit(solution)/shard_map/strips/pallas_call | solution.py:26
Async XLA Ops:
  4.5 7.1 %collective-permute-start = (bf16[448,128]{1,0:T(8,128)(2,1)S(1)}, bf16[448,128]{1,0:T(8,128)(2,1)S(1)}, u32[]{:S(2)}, u32[]{:S(2)}) collective-permute-start(bf16[448,128]{1,0:T(8,128)(2,1)S(1)} %get-tuple-element.30), channel_id=1, source_target_pairs={{0,4},{1,5},{2,6},{3,7},{4,0},{5,1},{6,2},{7,3},{8,12},{9,13},{10,... | collective-permute-start | bytes 344072 | tf_op jit(solution)/shard_map/ppermute | solution.py:405
  7.5 6.0 %collective-permute-start.1 = (bf16[304,128]{1,0:T(8,128)(2,1)S(1)}, bf16[304,128]{1,0:T(8,128)(2,1)S(1)}, u32[]{:S(2)}, u32[]{:S(2)}) collective-permute-start(bf16[304,128]{1,0:T(8,128)(2,1)S(1)} %get-tuple-element.33), channel_id=1, source_target_pairs={{0,1},{1,0},{2,3},{3,2},{4,8},{5,9},{6,10},{7,11},{8,4},{9,5},{10,... | collective-permute-start | bytes 233480 | tf_op jit(solution)/shard_map/ppermute | solution.py:405
  11.7 4.2 %collective-permute-start.2 = (bf16[192,128]{1,0:T(8,128)(2,1)S(1)}, bf16[192,128]{1,0:T(8,128)(2,1)S(1)}, u32[]{:S(2)}, u32[]{:S(2)}) collective-permute-start(bf16[192,128]{1,0:T(8,128)(2,1)S(1)} %get-tuple-element.31), channel_id=1, source_target_pairs={{0,8},{1,9},{2,10},{3,11},{4,12},{5,13},{6,14},{7,15},{8,0},{9,1},... | collective-permute-start | bytes 147464 | tf_op jit(solution)/shard_map/ppermute | solution.py:405
  13.4 1.7 %collective-permute-start.3 = (bf16[48,128]{1,0:T(8,128)(2,1)S(1)}, bf16[48,128]{1,0:T(8,128)(2,1)S(1)}, u32[]{:S(2)}, u32[]{:S(2)}) collective-permute-start(bf16[48,128]{1,0:T(8,128)(2,1)S(1)} %get-tuple-element.23.own_list.refs_2_.refs_1_), channel_id=1, source_target_pairs={{0,1},{1,0},{2,3},{3,2},{4,5},{5,4},{6,7},{7,6},{8,16},{9,17},{10,... | collective-permute-start | bytes 36872 | tf_op jit(solution)/shard_map/ppermute | solution.py:405
  17.2 7.1 %collective-permute-start.6 = (f32[39,128]{1,0:T(8,128)S(1)}, f32[39,128]{1,0:T(8,128)S(1)}, u32[]{:S(2)}, u32[]{:S(2)}) collective-permute-start(f32[39,128]{1,0:T(8,128)S(1)} %get-tuple-element.40), channel_id=1, source_target_pairs={{0,16},{1,17},{2,18},{3,19},{4,20},{5,21},{6,22},{7,23},{8,24},{9,... | collective-permute-start | bytes 59912 | tf_op jit(solution)/shard_map/ppermute | solution.py:405
  21.1 2.8 %collective-permute-start.4 = (f32[4,1024]{1,0:T(4,128)S(1)}, f32[4,1024]{1,0:T(4,128)S(1)}, u32[]{:S(2)}, u32[]{:S(2)}) collective-permute-start(f32[4,1024]{1,0:T(4,128)S(1)} %get-tuple-element.37), channel_id=1, source_target_pairs={{0,1},{1,0},{2,3},{3,2},{4,5},{5,4},{6,7},{7,6},{8,9},{9,8},{10,11... | collective-permute-start | bytes 49160 | tf_op jit(solution)/shard_map/ppermute | solution.py:405
  21.1 3.2 %collective-permute-start.5 = (f32[4,1024]{1,0:T(4,128)S(1)}, f32[4,1024]{1,0:T(4,128)S(1)}, u32[]{:S(2)}, u32[]{:S(2)}) collective-permute-start(f32[4,1024]{1,0:T(4,128)S(1)} %get-tuple-element.38), channel_id=1, source_target_pairs={{0,3},{1,2},{2,1},{3,0},{4,7},{5,6},{6,5},{7,4},{8,11},{9,10},{10,... | collective-permute-start | bytes 49160 | tf_op jit(solution)/shard_map/ppermute | solution.py:405

commit v4 on v3

--- a/solution.py
+++ b/solution.py
@@ -10,6 +10,7 @@
 sweeps = 4
 GRID = ("gx", "gy")
 LANES = 128
+AGENT_PART = 2048
 EXACT = lax.Precision.HIGHEST
 f32, bf16, i32 = jnp.float32, jnp.bfloat16, jnp.int32
 VMEM_LIMIT = 48 << 20
@@ -74,37 +75,64 @@
 def advance_kernel(
     count_ref, cell_hbm, coupling_hbm, basal_hbm, half_hbm, decay_hbm, weight_hbm, voxel_hbm, oxygen_hbm, ids_hbm,
     targets_hbm, new_state, message_even, message_odd, message_far, buffer,
-    cell, coupling, basal, half, decay, weight, voxel, oxygen, ids, targets, drive, semaphores, *, cy, cx, nz, capacity,
+    cell, coupling, basal, half, decay, weight, voxel, oxygen, ids, targets, drive, matrices, stack, semaphores,
+    *, cy, cx, nz, capacity,
 ):
     pairs = (
-        (cell_hbm, cell), (coupling_hbm, coupling), (basal_hbm, basal), (half_hbm, half), (decay_hbm, decay),
-        (weight_hbm, weight), (voxel_hbm, voxel), (oxygen_hbm, oxygen), (ids_hbm, ids), (targets_hbm, targets),
+        (coupling_hbm, coupling), (basal_hbm, basal), (half_hbm, half), (decay_hbm, decay), (weight_hbm, weight),
+        (voxel_hbm, voxel), (ids_hbm, ids), (targets_hbm, targets), (oxygen_hbm, oxygen),
     )
+    species, agents = cell.shape
+    parts = [slice(at, at + AGENT_PART) for at in range(0, agents, AGENT_PART)]
     copies = [pltpu.make_async_copy(a, b, semaphores.at[i]) for i, (a, b) in enumerate(pairs)]
-    for copy in copies:
+    waves = [
+        pltpu.make_async_copy(cell_hbm.at[:, part], cell.at[:, part], semaphores.at[len(pairs) + i])
+        for i, part in enumerate(parts)
+    ]
+    waves[0].start()
+    stack[...] = jnp.zeros_like(stack)
+    for copy in copies[:-1]:
         copy.start()
-    for copy in copies:
+    for copy in waves[1:] + copies[-1:]:
+        copy.start()
+    for copy in copies[:-1]:
         copy.wait()
-    species, agents = cell.shape
     basal_c, half_c, decay_c, weight_c = (column(r[...], species) for r in (basal, half, decay, weight))
     half_square = half_c * half_c
-    matrix = coupling[...]
+    matrix_high, matrix_low, _ = pieces(coupling[...])
+    matrices[...] = jnp.zeros_like(matrices)
+    for number, piece in enumerate((matrix_high, matrix_high, matrix_low)):
+        matrices[:, number * PIECE_ROWS : number * PIECE_ROWS + species] = piece
+    matrix = matrices[...]
 
     def rates(current):
         square = current * current
         occupancy = square / (half_square + square)
-        product = jnp.dot(matrix, occupancy, precision=EXACT, preferred_element_type=f32)
-        return basal_c + product - decay_c * current
-
-    current = cell[...]
-    for substep in range(2):
-        middle = current + (0.5 * time_step) * rates(current)
-        current = current + time_step * rates(middle)
-    new_state[...] = current
-    total = jnp.sum(weight_c * current, axis=0, keepdims=True)
+        high = occupancy.astype(bf16)
+        low = (occupancy - high.astype(f32)).astype(bf16)
+        for number, piece in enumerate((high, low, high)):
+            stack[number * PIECE_ROWS : number * PIECE_ROWS + species, :] = piece
+        drive_sum = jnp.dot(matrix, stack[...], preferred_element_type=f32)
+        return basal_c + drive_sum - decay_c * current
+
     rows = agents // LANES
-    for c in range(rows):
-        drive[c : c + 1, :] = total[:, c * LANES : (c + 1) * LANES]
+    picks = ids.shape[1]
+    mothers = jnp.zeros((species, picks), f32)
+    for part, wave in zip(parts, waves):
+        wave.wait()
+        current = cell[:, part]
+        for substep in range(2):
+            middle = current + (0.5 * time_step) * rates(current)
+            current = current + time_step * rates(middle)
+        new_state[:, part] = current
+        total = jnp.sum(weight_c * current, axis=0, keepdims=True)
+        for at in range(0, AGENT_PART, LANES):
+            c = (part.start + at) // LANES
+            drive[c : c + 1, :] = total[:, at : at + LANES]
+        slots = lax.broadcasted_iota(i32, (AGENT_PART, picks), 0) + part.start
+        chosen = (slots == ids[...]).astype(f32).astype(bf16)
+        mothers += sum(jnp.dot(p, chosen, preferred_element_type=f32) for p in pieces(current)[:2])
+    copies[-1].wait()
     x = drive[...]
     soft = jnp.maximum(x, 0.0) + jnp.log1p(jnp.exp(-jnp.abs(x)))
     slot = lax.broadcasted_iota(i32, (rows, LANES), 0) * LANES + lax.broadcasted_iota(i32, (rows, LANES), 1)
@@ -134,7 +162,7 @@
     message_even[head:tail, :] = listing
     message_odd[head:, :] = listing
     message_far[...] = listing
-    placed = place_daughters(current, ids[...], targets[...], capacity, buffer.shape[1])
+    placed = place_daughters(mothers, targets[...], capacity, buffer.shape[1])
     buffer[...] = placed
     put_pieces(message_even, tail, first_send(placed, lax.axis_index("gx") % 2 == 1, capacity))
 
@@ -256,7 +284,7 @@
     picked = jnp.where(picked < edge, picked, picked + cy - 2 * edge)
     picker = (picked == lax.broadcasted_iota(i32, (2 * edge, cy), 1)).astype(f32).astype(bf16)
     flat = field[...].reshape(2 * m, cy)
-    rims = sum(product(picker, piece) for piece in pieces(flat))
+    rims = sum(product(picker, piece) for piece in pieces(flat)[:2])
     strips[...] = rims
     h_even = lax.axis_index("gy") % 2 == 0
     head_rows, tail_rows = rims[:sweeps], rims[2 * edge - sweeps :]
@@ -321,8 +349,11 @@
     placed = lax.broadcasted_iota(i32, (edge, cy), 0)
     placed = jnp.where(placed < sweeps, placed, placed + cy - edge)
     placer = (placed == lax.broadcasted_iota(i32, (edge, cy), 1)).astype(f32)
+    high = final.astype(bf16).astype(f32)
+    stacked = jnp.concatenate([high, final - high], axis=0).astype(bf16)
+    placers = jnp.concatenate([placer, placer], axis=0).astype(bf16)
     edges = lax.dot_general(
-        final, placer, (((0,), (0,)), ((), ())), precision=EXACT, preferred_element_type=f32
+        stacked, placers, (((0,), (0,)), ((), ())), preferred_element_type=f32
     ).reshape(nz, width, cy)
     low = lax.broadcasted_iota(i32, (nz, cx, cy), 1) < cx // 2
     mixed = pltpu.roll(jnp.where(low, edges[:, cx:], edges[:, :cx]), cx // 2, 1)
@@ -341,13 +372,13 @@
 
 
 def put_pieces(message, at, value):
-    for number, piece in enumerate(pieces(value)):
+    for number, piece in enumerate(pieces(value)[:2]):
         start = at + number * PIECE_ROWS
         message[start : start + value.shape[0], :] = piece
 
 
 def get_pieces(message, at, count):
-    starts = [at + number * PIECE_ROWS for number in range(3)]
+    starts = [at + number * PIECE_ROWS for number in range(2)]
     return sum(message[start : start + count, :].astype(f32) for start in starts)
 
 
@@ -376,19 +407,16 @@
     return jnp.concatenate([left, right], axis=1)
 
 
-def place_daughters(state, ids, target, capacity, columns):
-    species, agents = state.shape
-    picks = ids.shape[1]
+def place_daughters(mothers, target, capacity, columns):
+    picks = target.shape[1]
     square = (picks, picks)
     across = jnp.broadcast_to(target, square)
     down = jnp.broadcast_to(column(target, picks), square)
     earlier = lax.broadcasted_iota(i32, square, 0) < lax.broadcasted_iota(i32, square, 1)
     rank = jnp.sum(jnp.where((across == down) & earlier, 1, 0), axis=0, keepdims=True)
     position = target * capacity + rank
-    chosen = (lax.broadcasted_iota(i32, (agents, picks), 0) == ids).astype(f32).astype(bf16)
-    mothers = sum(jnp.dot(p, chosen, preferred_element_type=f32) for p in pieces(state))
     placing = (lax.broadcasted_iota(i32, (columns, picks), 0) == position).astype(f32).astype(bf16)
-    return sum(product(p, placing) for p in pieces(mothers))
+    return sum(product(p, placing) for p in pieces(mothers)[:2])
 
 
 def relay_kernel(buffer, got, merged, send, *, capacity, step, after):
@@ -431,7 +459,7 @@
 
         m = nz * cx
         count = 3 * rows
-        pieces_rows = 3 * PIECE_ROWS
+        pieces_rows = 2 * PIECE_ROWS
         one_field = (nz, 2 * cx, cy)
         listed = (count, LANES)
         half_buffer = ((species, columns // 2), f32)
@@ -450,7 +478,8 @@
             + [pltpu.VMEM((1, species), f32)] * 4
             + [pltpu.VMEM((rows, LANES), i32), pltpu.VMEM((nz, cx, cy), f32)]
             + [pltpu.VMEM((1, picks), i32)] * 2
-            + [pltpu.VMEM((rows, LANES), f32), pltpu.SemaphoreType.DMA((10,))],
+            + [pltpu.VMEM((rows, LANES), f32), pltpu.VMEM((species, 3 * PIECE_ROWS), bf16),
+               pltpu.VMEM((3 * PIECE_ROWS, AGENT_PART), bf16), pltpu.SemaphoreType.DMA((9 + agents // AGENT_PART,))],
         )
         near_e = swap(message_even, near_even)
         near_o = swap(message_odd, near_odd)
@@ -491,9 +520,9 @@
             scratch=[pltpu.VMEM((2,) + listed, f32), pltpu.VMEM((head, 2 * agents), bf16),
                      pltpu.VMEM((cy, 2 * agents), bf16)],
         )
+        got = swap(send, lambda g, h: (g ^ step, h))
+        got_odd = swap(strip_odd, side_odd)
         got_even = swap(strip_even, side_even)
-        got_odd = swap(strip_odd, side_odd)
-        got = swap(send, lambda g, h: (g ^ step, h))
         (inside,) = call(
             kernel(sweep_kernel, grid_count=grid_count), [((nz, cx, cy), f32)], "sweeps", [field]
         )

time: 26.5 us -> 24.5 us (0.925)
  Pallas kernels: 10.6 us -> 9.64 us
  starting transfers between devices: 10.4 us -> 9.65 us
  waiting for transfers between devices: 3.97 us -> 3.63 us
    pallas_call x7, Pallas kernels: 10.6 us -> 9.64 us  [call(): pl.pallas_call(body, out_shape=tuple((jax.ShapeDtypeStruct(s, t) for s, t...]
    ppermute x7, starting transfers between devices: 10.4 us -> 9.65 us  [swap(): return lax.ppermute(value, GRID, swap_pairs(grid_count, row_count, partner))]
    ppermute x7, waiting for transfers between devices: 3.97 us -> 3.63 us  [swap(): return lax.ppermute(value, GRID, swap_pairs(grid_count, row_count, partner))]
  transfers between devices with their start and end apart: 7 -> 7, of which waited for: 3 -> 3; matrix products, arithmetic and copies ran while one was open for 0% -> 0% of each run, Pallas kernels for 16% -> 17%
where the time goes in v4:
time: 24.5 us; the launch traced here: 24.3 us
  starting transfers between devices  9.65 us (39%)
  Pallas kernels  9.64 us (39%)
  waiting for transfers between devices  3.63 us (15%)
  between operations  1.33 us (5%)
    ppermute x7, starting transfers between devices, swap(): return lax.ppermute(value, GRID, swap_pairs(grid_count, row_count, partner))  9.65 us
    pallas_call x7, Pallas kernels, call(): pl.pallas_call(body, out_shape=tuple((jax.ShapeDtypeStruct(s, t) for s, t...  9.64 us
    ppermute x7, waiting for transfers between devices, swap(): return lax.ppermute(value, GRID, swap_pairs(grid_count, row_count, partner))  3.63 us
  transfers between devices with their start and end apart: 7, of which 3 were waited for; matrix products, arithmetic and copies ran while one was open for 0% of the time, Pallas kernels for 17%

profile of v4, /device:TPU:0, one launch (start us, length us, event | category | flops | bytes accessed | tf_op | source)
XLA Modules:
  0.0 24.3 jit_solution(3542545626460596039)
XLA Ops:
  1.3 2.7 %advance.1 = (f32[39,2048]{1,0:T(8,128)S(1)}, bf16[400,128]{1,0:T(8,128)(2,1)S(1)}, bf16[304,128]{1,0:T(8,128)(2,1)S(1)}, bf16[48,128]{1,0:T(8,128)(2,1)S(1)}, f32[39,256]{1,0:T(8,128)S(1)}) custom-call(s32[1]{0:T(128)S(6)} %copy.14.refs_0_, f32[39,2048]{1,0:T(8,128)} %refs_1_.1, f32[39,39]{1,0:T(8,128)} %refs_2_.1, f32[1,39]{1,0:T(1,128)} %bitcast.8, ...), custom_call_target="tpu_custom_call" | custom-call | tf_op jit(solution)/shard_map/advance/pallas_call | solution.py:27
  4.0 3.0 %collective-permute-start = (bf16[400,128]{1,0:T(8,128)(2,1)S(1)}, bf16[400,128]{1,0:T(8,128)(2,1)S(1)}, u32[]{:S(2)}, u32[]{:S(2)}) collective-permute-start(bf16[400,128]{1,0:T(8,128)(2,1)S(1)} %get-tuple-element.30), channel_id=1, source_target_pairs={{0,4},{1,5},{2,6},{3,7},{4,0},{5,1},{6,2},{7,3},{8,12},{9,13},{10,... | collective-permute-start | bytes 307208 | tf_op jit(solution)/shard_map/ppermute | solution.py:433
  7.1 0.0 collective-permute-start.1
  7.1 1.1 %own.1 = (f32[64,16,128]{2,1,0:T(8,128)S(1)}, f32[39,2048]{1,0:T(8,128)}) custom-call(f32[64,8,128]{2,1,0:T(8,128)} %oxygen_hbm.1, bf16[48,128]{1,0:T(8,128)(2,1)S(1)} %get-tuple-element.23.own_list.refs_2_.refs_1_, f32[39,2048]{1,0:T(8,128)S(1)} %get-tuple-element.24.state), custom_call_target="tpu_custom_call" | custom-call | tf_op jit(solution)/shard_map/own/pallas_call | solution.py:27
  8.2 2.7 %collective-permute-done.refs_1_.refs_2_ = bf16[400,128]{1,0:T(8,128)(2,1)S(1)} collective-permute-done((bf16[400,128]{1,0:T(8,128)(2,1)S(1)}, bf16[400,128]{1,0:T(8,128)(2,1)S(1)}, u32[]{:S(2)}, u32[]{:S(2)}) %collective-permute-start) | collective-permute-done | bytes 102432 | tf_op jit(solution)/shard_map/ppermute | solution.py:433
  10.9 0.1 relay.1
  11.0 1.7 %collective-permute-start.2 = (bf16[144,128]{1,0:T(8,128)(2,1)S(1)}, bf16[144,128]{1,0:T(8,128)(2,1)S(1)}, u32[]{:S(2)}, u32[]{:S(2)}) collective-permute-start(bf16[144,128]{1,0:T(8,128)(2,1)S(1)} %get-tuple-element.31), channel_id=1, source_target_pairs={{0,8},{1,9},{2,10},{3,11},{4,12},{5,13},{6,14},{7,15},{8,0},{9,1},... | collective-permute-start | bytes 110600 | tf_op jit(solution)/shard_map/ppermute | solution.py:433
  12.7 0.0 collective-permute-start.3
  12.7 0.0 collective-permute-done.1.refs_3_
  12.7 1.7 %near.1.refs_0_ = f32[64,16,128]{2,1,0:T(8,128)S(1)} custom-call(f32[64,16,128]{2,1,0:T(8,128)S(1)} %get-tuple-element.32.refs_0_, bf16[48,128]{1,0:T(8,128)(2,1)S(1)} %get-tuple-element.23.own_list.refs_2_.refs_1_, bf16[400,128]{1,0:T(8,128)(2,1)S(1)} %collective-permute-done.refs_1_.refs_2_, bf16[304,128]{1,0:T(8,128)(2,1)S(1)} %collective-permute-done.1.refs_3_), custom_call_target="tpu_custom_call" | custom-call | tf_op jit(solution)/shard_map/near/pallas_call | solution.py:27
  14.3 0.0 collective-permute-done.3.refs_5_
  14.3 0.6 %collective-permute-done.2.refs_4_ = bf16[144,128]{1,0:T(8,128)(2,1)S(1)} collective-permute-done((bf16[144,128]{1,0:T(8,128)(2,1)S(1)}, bf16[144,128]{1,0:T(8,128)(2,1)S(1)}, u32[]{:S(2)}, u32[]{:S(2)}) %collective-permute-start.2) | collective-permute-done | bytes 36896 | tf_op jit(solution)/shard_map/ppermute | solution.py:433
  15.0 1.3 %far.1 = (f32[64,16,128]{2,1,0:T(8,128)S(1)}, f32[16,1024]{1,0:T(8,128)S(1)}, f32[4,1024]{1,0:T(4,128)S(1)}, f32[4,1024]{1,0:T(4,128)S(1)}, f32[39,256]{1,0:T(8,128)S(1)}, /*index=5*/f32[39,128]{1,0:T(8,128)S(1)}) custom-call(f32[64,16,128]{2,1,0:T(8,128)S(1)} %near.1.refs_0_, f32[39,256]{1,0:T(8,128)S(1)} %get-tuple-element.34.refs_1_, ...), custom_call_target="tpu_custom_call" | custom-call | tf_op jit(solution)/shard_map/far/pallas_call | solution.py:27
  16.2 3.3 %collective-permute-start.6 = (f32[39,128]{1,0:T(8,128)S(1)}, f32[39,128]{1,0:T(8,128)S(1)}, u32[]{:S(2)}, u32[]{:S(2)}) collective-permute-start(f32[39,128]{1,0:T(8,128)S(1)} %get-tuple-element.40), channel_id=1, source_target_pairs={{0,16},{1,17},{2,18},{3,19},{4,20},{5,21},{6,22},{7,23},{8,24},{9,... | collective-permute-start | bytes 59912 | tf_op jit(solution)/shard_map/ppermute | solution.py:433
  19.5 0.0 collective-permute-start.4
  19.6 1.6 %collective-permute-start.5 = (f32[4,1024]{1,0:T(4,128)S(1)}, f32[4,1024]{1,0:T(4,128)S(1)}, u32[]{:S(2)}, u32[]{:S(2)}) collective-permute-start(f32[4,1024]{1,0:T(4,128)S(1)} %get-tuple-element.38), channel_id=1, source_target_pairs={{0,3},{1,2},{2,1},{3,0},{4,7},{5,6},{6,5},{7,4},{8,11},{9,10},{10,... | collective-permute-start | bytes 49160 | tf_op jit(solution)/shard_map/ppermute | solution.py:433
  21.2 1.2 %sweeps.1.refs_0_ = f32[64,8,128]{2,1,0:T(8,128)S(1)} custom-call(f32[64,16,128]{2,1,0:T(8,128)S(1)} %get-tuple-element.35.refs_0_), custom_call_target="tpu_custom_call" | custom-call | tf_op jit(solution)/shard_map/sweeps/pallas_call | solution.py:27
  22.4 0.0 collective-permute-done.4.refs_2_
  22.4 0.3 %collective-permute-done.5.refs_3_ = f32[4,1024]{1,0:T(4,128)S(1)} collective-permute-done((f32[4,1024]{1,0:T(4,128)S(1)}, f32[4,1024]{1,0:T(4,128)S(1)}, u32[]{:S(2)}, u32[]{:S(2)}) %collective-permute-start.5) | collective-permute-done | bytes 16416 | tf_op jit(solution)/shard_map/ppermute | solution.py:433
  22.7 0.0 collective-permute-done.6.refs_5_
  22.7 1.5 %strips.1 = (f32[64,8,128]{2,1,0:T(8,128)}, f32[39,256]{1,0:T(8,128)}) custom-call(f32[64,8,128]{2,1,0:T(8,128)S(1)} %sweeps.1.refs_0_, f32[16,1024]{1,0:T(8,128)S(1)} %get-tuple-element.36.refs_1_, f32[4,1024]{1,0:T(4,128)S(1)} %collective-permute-done.4.refs_2_, f32[4,1024]{1,0:T(4,128)S(1)} %collective-permute-done.5.refs_3_, ...), custom_call_target="tpu_custom_call" | custom-call | tf_op jit(solution)/shard_map/strips/pallas_call | solution.py:27
Async XLA Ops:
  4.0 6.8 %collective-permute-start = (bf16[400,128]{1,0:T(8,128)(2,1)S(1)}, bf16[400,128]{1,0:T(8,128)(2,1)S(1)}, u32[]{:S(2)}, u32[]{:S(2)}) collective-permute-start(bf16[400,128]{1,0:T(8,128)(2,1)S(1)} %get-tuple-element.30), channel_id=1, source_target_pairs={{0,4},{1,5},{2,6},{3,7},{4,0},{5,1},{6,2},{7,3},{8,12},{9,13},{10,... | collective-permute-start | bytes 307208 | tf_op jit(solution)/shard_map/ppermute | solution.py:433
  7.1 5.6 %collective-permute-start.1 = (bf16[304,128]{1,0:T(8,128)(2,1)S(1)}, bf16[304,128]{1,0:T(8,128)(2,1)S(1)}, u32[]{:S(2)}, u32[]{:S(2)}) collective-permute-start(bf16[304,128]{1,0:T(8,128)(2,1)S(1)} %get-tuple-element.33), channel_id=1, source_target_pairs={{0,1},{1,0},{2,3},{3,2},{4,8},{5,9},{6,10},{7,11},{8,4},{9,5},{10,... | collective-permute-start | bytes 233480 | tf_op jit(solution)/shard_map/ppermute | solution.py:433
  11.0 4.0 %collective-permute-start.2 = (bf16[144,128]{1,0:T(8,128)(2,1)S(1)}, bf16[144,128]{1,0:T(8,128)(2,1)S(1)}, u32[]{:S(2)}, u32[]{:S(2)}) collective-permute-start(bf16[144,128]{1,0:T(8,128)(2,1)S(1)} %get-tuple-element.31), channel_id=1, source_target_pairs={{0,8},{1,9},{2,10},{3,11},{4,12},{5,13},{6,14},{7,15},{8,0},{9,1},... | collective-permute-start | bytes 110600 | tf_op jit(solution)/shard_map/ppermute | solution.py:433
  12.7 1.7 %collective-permute-start.3 = (bf16[48,128]{1,0:T(8,128)(2,1)S(1)}, bf16[48,128]{1,0:T(8,128)(2,1)S(1)}, u32[]{:S(2)}, u32[]{:S(2)}) collective-permute-start(bf16[48,128]{1,0:T(8,128)(2,1)S(1)} %get-tuple-element.23.own_list.refs_2_.refs_1_), channel_id=1, source_target_pairs={{0,1},{1,0},{2,3},{3,2},{4,5},{5,4},{6,7},{7,6},{8,16},{9,17},{10,... | collective-permute-start | bytes 36872 | tf_op jit(solution)/shard_map/ppermute | solution.py:433
  16.2 6.5 %collective-permute-start.6 = (f32[39,128]{1,0:T(8,128)S(1)}, f32[39,128]{1,0:T(8,128)S(1)}, u32[]{:S(2)}, u32[]{:S(2)}) collective-permute-start(f32[39,128]{1,0:T(8,128)S(1)} %get-tuple-element.40), channel_id=1, source_target_pairs={{0,16},{1,17},{2,18},{3,19},{4,20},{5,21},{6,22},{7,23},{8,24},{9,... | collective-permute-start | bytes 59912 | tf_op jit(solution)/shard_map/ppermute | solution.py:433
  19.5 2.8 %collective-permute-start.4 = (f32[4,1024]{1,0:T(4,128)S(1)}, f32[4,1024]{1,0:T(4,128)S(1)}, u32[]{:S(2)}, u32[]{:S(2)}) collective-permute-start(f32[4,1024]{1,0:T(4,128)S(1)} %get-tuple-element.37), channel_id=1, source_target_pairs={{0,1},{1,0},{2,3},{3,2},{4,5},{5,4},{6,7},{7,6},{8,9},{9,8},{10,11... | collective-permute-start | bytes 49160 | tf_op jit(solution)/shard_map/ppermute | solution.py:433
  19.6 3.2 %collective-permute-start.5 = (f32[4,1024]{1,0:T(4,128)S(1)}, f32[4,1024]{1,0:T(4,128)S(1)}, u32[]{:S(2)}, u32[]{:S(2)}) collective-permute-start(f32[4,1024]{1,0:T(4,128)S(1)} %get-tuple-element.38), channel_id=1, source_target_pairs={{0,3},{1,2},{2,1},{3,0},{4,7},{5,6},{6,5},{7,4},{8,11},{9,10},{10,... | collective-permute-start | bytes 49160 | tf_op jit(solution)/shard_map/ppermute | solution.py:433

commit v5 on v3

--- a/solution.py
+++ b/solution.py
@@ -74,49 +74,65 @@
 def advance_kernel(
     count_ref, cell_hbm, coupling_hbm, basal_hbm, half_hbm, decay_hbm, weight_hbm, voxel_hbm, oxygen_hbm, ids_hbm,
     targets_hbm, new_state, message_even, message_odd, message_far, buffer,
-    cell, coupling, basal, half, decay, weight, voxel, oxygen, ids, targets, drive, semaphores, *, cy, cx, nz, capacity,
+    cell, coupling, basal, half, decay, weight, voxel, oxygen, ids, targets, drive, matrices, stack, chosen, codes, semaphores,
+    *, cy, cx, nz, capacity,
 ):
     pairs = (
-        (cell_hbm, cell), (coupling_hbm, coupling), (basal_hbm, basal), (half_hbm, half), (decay_hbm, decay),
-        (weight_hbm, weight), (voxel_hbm, voxel), (oxygen_hbm, oxygen), (ids_hbm, ids), (targets_hbm, targets),
+        (ids_hbm, ids), (voxel_hbm, voxel), (targets_hbm, targets), (coupling_hbm, coupling), (basal_hbm, basal),
+        (half_hbm, half), (decay_hbm, decay), (weight_hbm, weight), (cell_hbm, cell), (oxygen_hbm, oxygen),
     )
+    species, agents = cell.shape
     copies = [pltpu.make_async_copy(a, b, semaphores.at[i]) for i, (a, b) in enumerate(pairs)]
     for copy in copies:
         copy.start()
-    for copy in copies:
+    stack[...] = jnp.zeros_like(stack)
+    for copy in copies[:-2]:
         copy.wait()
-    species, agents = cell.shape
+    rows = agents // LANES
+    picks = ids.shape[1]
+    chosen[...] = (lax.broadcasted_iota(i32, (agents, picks), 0) == ids[...]).astype(f32).astype(bf16)
+    code = voxel[...]
+    at_y = code % cy
+    at_x = (code // cy) % cx
+    at_z = (code // (cy * cx)) % nz
+    slab_x = (code // (cy * cx * nz)) * cx + at_x + cx // 2
+    codes[:rows, :] = (at_z * cx + slab_x % cx - nz * cx // 2).astype(f32)
+    codes[rows:, :] = ((slab_x // cx) * cy + at_y - 2 * cy).astype(f32)
     basal_c, half_c, decay_c, weight_c = (column(r[...], species) for r in (basal, half, decay, weight))
     half_square = half_c * half_c
-    matrix = coupling[...]
+    matrix_high, matrix_low, _ = pieces(coupling[...])
+    matrices[...] = jnp.zeros_like(matrices)
+    for number, piece in enumerate((matrix_high, matrix_high, matrix_low)):
+        matrices[:, number * PIECE_ROWS : number * PIECE_ROWS + species] = piece
+    matrix = matrices[...]
 
     def rates(current):
         square = current * current
         occupancy = square / (half_square + square)
-        product = jnp.dot(matrix, occupancy, precision=EXACT, preferred_element_type=f32)
-        return basal_c + product - decay_c * current
-
+        high = occupancy.astype(bf16)
+        low = (occupancy - high.astype(f32)).astype(bf16)
+        for number, piece in enumerate((high, low, high)):
+            stack[number * PIECE_ROWS : number * PIECE_ROWS + species, :] = piece
+        drive_sum = jnp.dot(matrix, stack[...], preferred_element_type=f32)
+        return basal_c + drive_sum - decay_c * current
+
+    placing = place_columns(targets[...], capacity, buffer.shape[1])
+    copies[-2].wait()
     current = cell[...]
     for substep in range(2):
         middle = current + (0.5 * time_step) * rates(current)
         current = current + time_step * rates(middle)
     new_state[...] = current
     total = jnp.sum(weight_c * current, axis=0, keepdims=True)
-    rows = agents // LANES
     for c in range(rows):
         drive[c : c + 1, :] = total[:, c * LANES : (c + 1) * LANES]
+    mothers = sum(jnp.dot(p, chosen[...], preferred_element_type=f32) for p in pieces(current)[:2])
+    copies[-1].wait()
     x = drive[...]
     soft = jnp.maximum(x, 0.0) + jnp.log1p(jnp.exp(-jnp.abs(x)))
     slot = lax.broadcasted_iota(i32, (rows, LANES), 0) * LANES + lax.broadcasted_iota(i32, (rows, LANES), 1)
     uptake = jnp.where(slot < count_ref[0], soft, 0.0)
-    code = voxel[...]
-    at_y = code % cy
-    at_x = (code // cy) % cx
-    at_z = (code // (cy * cx)) % nz
-    slab_x = (code // (cy * cx * nz)) * cx + at_x + cx // 2
-    row = at_z * cx + slab_x % cx - nz * cx // 2
-    col = (slab_x // cx) * cy + at_y - 2 * cy
-    listing = jnp.concatenate([uptake, row.astype(f32), col.astype(f32)], axis=0).astype(bf16)
+    listing = jnp.concatenate([uptake, codes[...]], axis=0).astype(bf16)
     own = oxygen[...] - 1.0
     turned = pltpu.roll(own, cx // 2, 1)
     low = lax.broadcasted_iota(i32, (nz // 2, cx, cy), 1) < cx // 2
@@ -134,7 +150,7 @@
     message_even[head:tail, :] = listing
     message_odd[head:, :] = listing
     message_far[...] = listing
-    placed = place_daughters(current, ids[...], targets[...], capacity, buffer.shape[1])
+    placed = sum(product(p, placing) for p in pieces(mothers)[:2])
     buffer[...] = placed
     put_pieces(message_even, tail, first_send(placed, lax.axis_index("gx") % 2 == 1, capacity))
 
@@ -226,25 +242,39 @@
     even = g % 2 == 0
     low_pair = g % 4 < 2
     fe, fo = far_e[:count, :].astype(f32), far_o[...].astype(f32)
-    for which, listing, valid in (
-        (0, jnp.where(low_pair, fe, fo), g + 2 < grid_count),
-        (1, jnp.where(low_pair, fo, fe), g >= 2),
+    quarter = zh // 2
+    for which, listing, base_code, valid in (
+        (0, jnp.where(low_pair, fe, fo), -2 * cy, g + 2 < grid_count),
+        (1, jnp.where(low_pair, fo, fe), cy, g >= 2),
     ):
         code = listing[rows : 2 * rows].astype(i32) + m // 2
-        at_z = code // cx
-        code = (at_z % zh) * cx + (at_z // zh) * half + code % half
+        at_z, at_y = code // cx, listing[2 * rows :].astype(i32) - base_code
+        inner_z = at_z % zh
+        code = (inner_z % quarter) * cx + (inner_z // quarter) * half + code % half
         lists[which, :rows] = jnp.where(valid, listing[:rows], 0.0)
         lists[which, rows : 2 * rows] = code.astype(f32)
-        lists[which, 2 * rows :] = listing[2 * rows :]
-    one_hots(lists, 0, 0, head, -2 * cy, cy, left, right, 0)
-    one_hots(lists, 1, 0, head, cy, cy, left, right, 1)
-    past_after = product(left[:, :agents], right[:, :agents])
-    past_before = product(left[:, agents:], right[:, agents:])
+        lists[which, 2 * rows :] = jnp.where((at_y >= 0) & (at_y < cy), (at_z // zh) * cy + at_y, -1).astype(f32)
+    one_hots(lists, 0, 0, head // 2, 0, 2 * cy, left, right, 0)
+    one_hots(lists, 1, 0, head // 2, 0, 2 * cy, left, right, 1)
+    low_quarter = lax.broadcasted_iota(i32, (quarter, cx, cy), 1) < half
+
+    def unfold(total):
+        lower, upper = (total[:, t * cy : (t + 1) * cy].reshape(quarter, cx, cy) for t in range(2))
+        return jnp.concatenate(
+            [
+                jnp.where(low_quarter, lower, pltpu.roll(upper, half, 1)),
+                jnp.where(low_quarter, pltpu.roll(lower, half, 1), upper),
+            ],
+            axis=0,
+        )
+
+    past_after = unfold(product(left[:, :agents], right[:, :agents]))
+    past_before = unfold(product(left[:, agents:], right[:, agents:]))
 
     e, o = near_e[:head, :].astype(f32), near_o[:head, :].astype(f32)
     shape = (zh, cx, cy)
-    from_before = (jnp.where(g >= 1, jnp.where(even, o, e) + 1.0, 0.0) - past_before).reshape(shape)
-    from_after = (jnp.where(g + 1 < grid_count, jnp.where(even, e, o) + 1.0, 0.0) - past_after).reshape(shape)
+    from_before = jnp.where(g >= 1, jnp.where(even, o, e) + 1.0, 0.0).reshape(shape) - past_before
+    from_after = jnp.where(g + 1 < grid_count, jnp.where(even, e, o) + 1.0, 0.0).reshape(shape) - past_after
     low = lax.broadcasted_iota(i32, shape, 1) < half
     field[:zh, :cx] = base[:zh, :cx] + jnp.where(low, from_before, 0.0)
     field[zh:, :cx] = base[zh:, :cx] + jnp.where(low, pltpu.roll(from_before, half, 1), 0.0)
@@ -255,8 +285,10 @@
     picked = lax.broadcasted_iota(i32, (2 * edge, cy), 0)
     picked = jnp.where(picked < edge, picked, picked + cy - 2 * edge)
     picker = (picked == lax.broadcasted_iota(i32, (2 * edge, cy), 1)).astype(f32).astype(bf16)
-    flat = field[...].reshape(2 * m, cy)
-    rims = sum(product(picker, piece) for piece in pieces(flat))
+    tiles = 2 * m // LANES
+    value = field[...].reshape(nz // tiles, tiles, 2 * cx, cy)
+    flat = jnp.concatenate([value[:, k].reshape(LANES, cy) for k in range(tiles)], axis=0)
+    rims = product(jnp.concatenate([picker, picker], axis=1), jnp.concatenate(pieces(flat)[:2], axis=1))
     strips[...] = rims
     h_even = lax.axis_index("gy") % 2 == 0
     head_rows, tail_rows = rims[:sweeps], rims[2 * edge - sweeps :]
@@ -287,11 +319,14 @@
 
 
 def strip_kernel(
-    inside, strips, got_even, got_odd, buffer, got, out, daughters, *, grid_count, row_count, capacity, step,
+    inside, strips, got_even, got_odd, buffer, got, out, daughters, merged, taken, semaphores,
+    *, grid_count, row_count, capacity, step,
 ):
-    daughters[...] = take_in(
+    taken[...] = take_in(
         buffer[...], got[...], (lax.axis_index("gx") // step) % 2 == 1, capacity * step
     )
+    copies = [pltpu.make_async_copy(taken, daughters, semaphores.at[0])]
+    copies[0].start()
     nz, cx, cy = inside.shape
     m = strips.shape[1]
     width = m // nz
@@ -302,32 +337,57 @@
     a, b = got_even[...], got_odd[...]
     right = jnp.where(has_right, jnp.where(h_even, a, b), 0.0)
     left = jnp.where(has_left, jnp.where(h_even, b, a), 0.0)
-    band = jnp.concatenate([left, strips[...], right], axis=0)
-    count = band.shape[0]
-    lane = lax.broadcasted_iota(i32, (count, m), 1)
-    line = lax.broadcasted_iota(i32, (count, m), 0)
+    own = strips[...]
+    tiles = m // LANES
+    bands = [
+        jnp.concatenate([rows[:, k * LANES : (k + 1) * LANES] for rows in (left, own, right)], axis=0) for k in range(tiles)
+    ]
+    shape = bands[0].shape
+    count = shape[0]
+    lane = lax.broadcasted_iota(i32, shape, 1)
+    line = lax.broadcasted_iota(i32, shape, 0)
     outside = (line < sweeps) & jnp.logical_not(has_left) | (line >= count - sweeps) & jnp.logical_not(has_right)
     at_x = lane % width
     outside = outside | (g == 0) & (at_x < cx // 2) | (g == grid_count - 1) & (at_x >= width - cx // 2)
-    keep = jnp.where(outside, 0.0, diffusion_number)
-    z_first, z_last = lane < width, lane >= m - width
+    scale = jnp.where(outside, 0.0, diffusion_number)
+    z_first, z_last = lane < width, lane >= LANES - width
     centre = 1.0 / diffusion_number - 6.0
     for turn in range(sweeps):
-        total = jnp.where(z_first, 0.0, pltpu.roll(band, width, 1)) + jnp.where(z_last, 0.0, pltpu.roll(band, m - width, 1))
-        total = total + (pltpu.roll(band, 1, 0) + pltpu.roll(band, count - 1, 0))
-        total = total + (pltpu.roll(band, 1, 1) + pltpu.roll(band, m - 1, 1))
-        band = (total + centre * band) * keep
-    final = jnp.concatenate([band[sweeps : 2 * sweeps], band[count - 2 * sweeps : count - sweeps]], axis=0)
+        wrapped = jnp.where(z_first, 0.0, pltpu.roll(bands[-1], width, 1))
+        onward = jnp.where(z_last, 0.0, pltpu.roll(bands[0], LANES - width, 1))
+        around = [wrapped] + bands + [onward]
+        bands = [
+            (
+                (around[k] + around[k + 2])
+                + (pltpu.roll(b, 1, 0) + pltpu.roll(b, count - 1, 0))
+                + (pltpu.roll(b, 1, 1) + pltpu.roll(b, LANES - 1, 1))
+                + centre * b
+            ) * scale
+            for k, b in enumerate(bands)
+        ]
     placed = lax.broadcasted_iota(i32, (edge, cy), 0)
     placed = jnp.where(placed < sweeps, placed, placed + cy - edge)
     placer = (placed == lax.broadcasted_iota(i32, (edge, cy), 1)).astype(f32)
-    edges = lax.dot_general(
-        final, placer, (((0,), (0,)), ((), ())), precision=EXACT, preferred_element_type=f32
-    ).reshape(nz, width, cy)
-    low = lax.broadcasted_iota(i32, (nz, cx, cy), 1) < cx // 2
-    mixed = pltpu.roll(jnp.where(low, edges[:, cx:], edges[:, :cx]), cx // 2, 1)
-    at_y = lax.broadcasted_iota(i32, (nz, cx, cy), 2)
-    out[...] = jnp.where((at_y < sweeps) | (at_y >= cy - sweeps), mixed, inside[...])
+    placers = jnp.concatenate([placer, placer], axis=0).astype(bf16)
+    planes = nz // tiles
+    low = lax.broadcasted_iota(i32, (planes, cx, cy), 1) < cx // 2
+    at_y = lax.broadcasted_iota(i32, (planes, cx, cy), 2)
+    rim = (at_y < sweeps) | (at_y >= cy - sweeps)
+    for k, b in enumerate(bands):
+        final = jnp.concatenate([b[sweeps : 2 * sweeps], b[count - 2 * sweeps : count - sweeps]], axis=0)
+        high = final.astype(bf16).astype(f32)
+        stacked = jnp.concatenate([high, final - high], axis=0).astype(bf16)
+        edges = lax.dot_general(
+            stacked, placers, (((0,), (0,)), ((), ())), preferred_element_type=f32
+        ).reshape(planes, width, cy)
+        mixed = pltpu.roll(jnp.where(low, edges[:, cx:], edges[:, :cx]), cx // 2, 1)
+        for at in range(planes):
+            z = at * tiles + k
+            merged[k, at] = jnp.where(rim[at], mixed[at], inside[z])
+        copies.append(pltpu.make_async_copy(merged.at[k], out.at[:, k], semaphores.at[k + 1]))
+        copies[-1].start()
+    for copy in copies:
+        copy.wait()
 
 
 def pieces(value):
@@ -341,13 +401,13 @@
 
 
 def put_pieces(message, at, value):
-    for number, piece in enumerate(pieces(value)):
+    for number, piece in enumerate(pieces(value)[:2]):
         start = at + number * PIECE_ROWS
         message[start : start + value.shape[0], :] = piece
 
 
 def get_pieces(message, at, count):
-    starts = [at + number * PIECE_ROWS for number in range(3)]
+    starts = [at + number * PIECE_ROWS for number in range(2)]
     return sum(message[start : start + count, :].astype(f32) for start in starts)
 
 
@@ -376,19 +436,15 @@
     return jnp.concatenate([left, right], axis=1)
 
 
-def place_daughters(state, ids, target, capacity, columns):
-    species, agents = state.shape
-    picks = ids.shape[1]
+def place_columns(target, capacity, columns):
+    picks = target.shape[1]
     square = (picks, picks)
     across = jnp.broadcast_to(target, square)
     down = jnp.broadcast_to(column(target, picks), square)
     earlier = lax.broadcasted_iota(i32, square, 0) < lax.broadcasted_iota(i32, square, 1)
     rank = jnp.sum(jnp.where((across == down) & earlier, 1, 0), axis=0, keepdims=True)
     position = target * capacity + rank
-    chosen = (lax.broadcasted_iota(i32, (agents, picks), 0) == ids).astype(f32).astype(bf16)
-    mothers = sum(jnp.dot(p, chosen, preferred_element_type=f32) for p in pieces(state))
-    placing = (lax.broadcasted_iota(i32, (columns, picks), 0) == position).astype(f32).astype(bf16)
-    return sum(product(p, placing) for p in pieces(mothers))
+    return (lax.broadcasted_iota(i32, (columns, picks), 0) == position).astype(f32).astype(bf16)
 
 
 def relay_kernel(buffer, got, merged, send, *, capacity, step, after):
@@ -431,7 +487,7 @@
 
         m = nz * cx
         count = 3 * rows
-        pieces_rows = 3 * PIECE_ROWS
+        pieces_rows = 2 * PIECE_ROWS
         one_field = (nz, 2 * cx, cy)
         listed = (count, LANES)
         half_buffer = ((species, columns // 2), f32)
@@ -450,7 +506,9 @@
             + [pltpu.VMEM((1, species), f32)] * 4
             + [pltpu.VMEM((rows, LANES), i32), pltpu.VMEM((nz, cx, cy), f32)]
             + [pltpu.VMEM((1, picks), i32)] * 2
-            + [pltpu.VMEM((rows, LANES), f32), pltpu.SemaphoreType.DMA((10,))],
+            + [pltpu.VMEM((rows, LANES), f32), pltpu.VMEM((species, 3 * PIECE_ROWS), bf16),
+               pltpu.VMEM((3 * PIECE_ROWS, agents), bf16), pltpu.VMEM((agents, picks), bf16),
+               pltpu.VMEM((2 * rows, LANES), f32), pltpu.SemaphoreType.DMA((10,))],
         )
         near_e = swap(message_even, near_even)
         near_o = swap(message_odd, near_odd)
@@ -488,12 +546,12 @@
              ((species, columns), f32)] + [half_buffer],
             "far",
             [field, buffer, near_e, near_o, far_e, far_o],
-            scratch=[pltpu.VMEM((2,) + listed, f32), pltpu.VMEM((head, 2 * agents), bf16),
-                     pltpu.VMEM((cy, 2 * agents), bf16)],
-        )
+            scratch=[pltpu.VMEM((2,) + listed, f32), pltpu.VMEM((head // 2, 2 * agents), bf16),
+                     pltpu.VMEM((2 * cy, 2 * agents), bf16)],
+        )
+        got = swap(send, lambda g, h: (g ^ step, h))
+        got_odd = swap(strip_odd, side_odd)
         got_even = swap(strip_even, side_even)
-        got_odd = swap(strip_odd, side_odd)
-        got = swap(send, lambda g, h: (g ^ step, h))
         (inside,) = call(
             kernel(sweep_kernel, grid_count=grid_count), [((nz, cx, cy), f32)], "sweeps", [field]
         )
@@ -507,13 +565,17 @@
             )
             step = after
             got = swap(sent, lambda g, h: (g ^ step, h))
+        tiles = 2 * m // LANES
         new_oxygen, daughter_state = call(
             kernel(strip_kernel, grid_count=grid_count, row_count=row_count, capacity=capacity, step=step),
-            [((nz, cx, cy), f32), ((species, columns), f32)],
+            [((nz // tiles, tiles, cx, cy), f32), ((species, columns), f32)],
             "strips",
             [inside, strips, got_even, got_odd, buffer, got],
-        )
-        return new_state, daughter_state, new_oxygen
+            hbm=(6, 7),
+            scratch=[pltpu.VMEM((tiles, nz // tiles, cx, cy), f32), pltpu.VMEM((species, columns), f32),
+                     pltpu.SemaphoreType.DMA((tiles + 1,))],
+        )
+        return new_state, daughter_state, new_oxygen.reshape(nz, cx, cy)
 
     return jax.shard_map(
         shards,

time: 26.5 us -> 24.3 us (0.917)
  Pallas kernels: 10.6 us -> 9.47 us
  starting transfers between devices: 10.4 us -> 9.61 us
  waiting for transfers between devices: 3.97 us -> 3.63 us
    pallas_call x7, Pallas kernels: 10.6 us -> 9.47 us  [call(): pl.pallas_call(body, out_shape=tuple((jax.ShapeDtypeStruct(s, t) for s, t...]
    ppermute x7, starting transfers between devices: 10.4 us -> 9.61 us  [swap(): return lax.ppermute(value, GRID, swap_pairs(grid_count, row_count, partner))]
    ppermute x7, waiting for transfers between devices: 3.97 us -> 3.63 us  [swap(): return lax.ppermute(value, GRID, swap_pairs(grid_count, row_count, partner))]
  transfers between devices with their start and end apart: 7 -> 7, of which waited for: 3 -> 3; matrix products, arithmetic and copies ran while one was open for 0% -> 0% of each run, Pallas kernels for 16% -> 17%
where the time goes in v5:
time: 24.3 us; the launch traced here: 24 us
  starting transfers between devices  9.61 us (40%)
  Pallas kernels  9.47 us (39%)
  waiting for transfers between devices  3.63 us (15%)
  between operations  1.33 us (5%)
    ppermute x7, starting transfers between devices, swap(): return lax.ppermute(value, GRID, swap_pairs(grid_count, row_count, partner))  9.61 us
    pallas_call x7, Pallas kernels, call(): pl.pallas_call(body, out_shape=tuple((jax.ShapeDtypeStruct(s, t) for s, t...  9.47 us
    ppermute x7, waiting for transfers between devices, swap(): return lax.ppermute(value, GRID, swap_pairs(grid_count, row_count, partner))  3.63 us
  transfers between devices with their start and end apart: 7, of which 3 were waited for; matrix products, arithmetic and copies ran while one was open for 0% of the time, Pallas kernels for 17%

profile of v5, /device:TPU:0, one launch (start us, length us, event | category | flops | bytes accessed | tf_op | source)
XLA Modules:
  0.0 24.0 jit_solution(10111443595767506564)
XLA Ops:
  1.3 2.6 %advance.1 = (f32[39,2048]{1,0:T(8,128)S(1)}, bf16[400,128]{1,0:T(8,128)(2,1)S(1)}, bf16[304,128]{1,0:T(8,128)(2,1)S(1)}, bf16[48,128]{1,0:T(8,128)(2,1)S(1)}, f32[39,256]{1,0:T(8,128)S(1)}) custom-call(s32[1]{0:T(128)S(6)} %copy.14.refs_0_, f32[39,2048]{1,0:T(8,128)} %refs_1_.1, f32[39,39]{1,0:T(8,128)} %refs_2_.1, f32[1,39]{1,0:T(1,128)} %bitcast.9, ...), custom_call_target="tpu_custom_call" | custom-call | tf_op jit(solution)/shard_map/advance/pallas_call | solution.py:26
  3.9 3.0 %collective-permute-start = (bf16[400,128]{1,0:T(8,128)(2,1)S(1)}, bf16[400,128]{1,0:T(8,128)(2,1)S(1)}, u32[]{:S(2)}, u32[]{:S(2)}) collective-permute-start(bf16[400,128]{1,0:T(8,128)(2,1)S(1)} %get-tuple-element.30), channel_id=1, source_target_pairs={{0,4},{1,5},{2,6},{3,7},{4,0},{5,1},{6,2},{7,3},{8,12},{9,13},{10,... | collective-permute-start | bytes 307208 | tf_op jit(solution)/shard_map/ppermute | solution.py:461
  6.9 0.0 collective-permute-start.1
  6.9 1.1 %own.1 = (f32[64,16,128]{2,1,0:T(8,128)S(1)}, f32[39,2048]{1,0:T(8,128)}) custom-call(f32[64,8,128]{2,1,0:T(8,128)} %oxygen_hbm.1, bf16[48,128]{1,0:T(8,128)(2,1)S(1)} %get-tuple-element.23.own_list.refs_2_.refs_1_, f32[39,2048]{1,0:T(8,128)S(1)} %get-tuple-element.24.state), custom_call_target="tpu_custom_call" | custom-call | tf_op jit(solution)/shard_map/own/pallas_call | solution.py:26
  8.1 2.7 %collective-permute-done.refs_1_.refs_2_ = bf16[400,128]{1,0:T(8,128)(2,1)S(1)} collective-permute-done((bf16[400,128]{1,0:T(8,128)(2,1)S(1)}, bf16[400,128]{1,0:T(8,128)(2,1)S(1)}, u32[]{:S(2)}, u32[]{:S(2)}) %collective-permute-start) | collective-permute-done | bytes 102432 | tf_op jit(solution)/shard_map/ppermute | solution.py:461
  10.7 0.1 relay.1
  10.8 1.7 %collective-permute-start.2 = (bf16[144,128]{1,0:T(8,128)(2,1)S(1)}, bf16[144,128]{1,0:T(8,128)(2,1)S(1)}, u32[]{:S(2)}, u32[]{:S(2)}) collective-permute-start(bf16[144,128]{1,0:T(8,128)(2,1)S(1)} %get-tuple-element.31), channel_id=1, source_target_pairs={{0,8},{1,9},{2,10},{3,11},{4,12},{5,13},{6,14},{7,15},{8,0},{9,1},... | collective-permute-start | bytes 110600 | tf_op jit(solution)/shard_map/ppermute | solution.py:461
  12.5 0.0 collective-permute-start.3
  12.5 0.0 collective-permute-done.1.refs_3_
  12.5 1.7 %near.1.refs_0_ = f32[64,16,128]{2,1,0:T(8,128)S(1)} custom-call(f32[64,16,128]{2,1,0:T(8,128)S(1)} %get-tuple-element.32.refs_0_, bf16[48,128]{1,0:T(8,128)(2,1)S(1)} %get-tuple-element.23.own_list.refs_2_.refs_1_, bf16[400,128]{1,0:T(8,128)(2,1)S(1)} %collective-permute-done.refs_1_.refs_2_, bf16[304,128]{1,0:T(8,128)(2,1)S(1)} %collective-permute-done.1.refs_3_), custom_call_target="tpu_custom_call" | custom-call | tf_op jit(solution)/shard_map/near/pallas_call | solution.py:26
  14.2 0.0 collective-permute-done.3.refs_5_
  14.2 0.6 %collective-permute-done.2.refs_4_ = bf16[144,128]{1,0:T(8,128)(2,1)S(1)} collective-permute-done((bf16[144,128]{1,0:T(8,128)(2,1)S(1)}, bf16[144,128]{1,0:T(8,128)(2,1)S(1)}, u32[]{:S(2)}, u32[]{:S(2)}) %collective-permute-start.2) | collective-permute-done | bytes 36896 | tf_op jit(solution)/shard_map/ppermute | solution.py:461
  14.9 1.3 %far.1 = (f32[64,16,128]{2,1,0:T(8,128)S(1)}, f32[16,1024]{1,0:T(8,128)S(1)}, f32[4,1024]{1,0:T(4,128)S(1)}, f32[4,1024]{1,0:T(4,128)S(1)}, f32[39,256]{1,0:T(8,128)S(1)}, /*index=5*/f32[39,128]{1,0:T(8,128)S(1)}) custom-call(f32[64,16,128]{2,1,0:T(8,128)S(1)} %near.1.refs_0_, f32[39,256]{1,0:T(8,128)S(1)} %get-tuple-element.34.refs_1_, ...), custom_call_target="tpu_custom_call" | custom-call | tf_op jit(solution)/shard_map/far/pallas_call | solution.py:26
  16.2 3.3 %collective-permute-start.6 = (f32[39,128]{1,0:T(8,128)S(1)}, f32[39,128]{1,0:T(8,128)S(1)}, u32[]{:S(2)}, u32[]{:S(2)}) collective-permute-start(f32[39,128]{1,0:T(8,128)S(1)} %get-tuple-element.40), channel_id=1, source_target_pairs={{0,16},{1,17},{2,18},{3,19},{4,20},{5,21},{6,22},{7,23},{8,24},{9,... | collective-permute-start | bytes 59912 | tf_op jit(solution)/shard_map/ppermute | solution.py:461
  19.5 0.0 collective-permute-start.4
  19.5 1.6 %collective-permute-start.5 = (f32[4,1024]{1,0:T(4,128)S(1)}, f32[4,1024]{1,0:T(4,128)S(1)}, u32[]{:S(2)}, u32[]{:S(2)}) collective-permute-start(f32[4,1024]{1,0:T(4,128)S(1)} %get-tuple-element.38), channel_id=1, source_target_pairs={{0,3},{1,2},{2,1},{3,0},{4,7},{5,6},{6,5},{7,4},{8,11},{9,10},{10,... | collective-permute-start | bytes 49160 | tf_op jit(solution)/shard_map/ppermute | solution.py:461
  21.1 1.2 %sweeps.1.refs_0_ = f32[64,8,128]{2,1,0:T(8,128)S(1)} custom-call(f32[64,16,128]{2,1,0:T(8,128)S(1)} %get-tuple-element.35.refs_0_), custom_call_target="tpu_custom_call" | custom-call | tf_op jit(solution)/shard_map/sweeps/pallas_call | solution.py:26
  22.3 0.0 collective-permute-done.4.refs_2_
  22.3 0.3 %collective-permute-done.5.refs_3_ = f32[4,1024]{1,0:T(4,128)S(1)} collective-permute-done((f32[4,1024]{1,0:T(4,128)S(1)}, f32[4,1024]{1,0:T(4,128)S(1)}, u32[]{:S(2)}, u32[]{:S(2)}) %collective-permute-start.5) | collective-permute-done | bytes 16416 | tf_op jit(solution)/shard_map/ppermute | solution.py:461
  22.6 0.0 collective-permute-done.6.refs_5_
  22.6 1.4 %strips.1 = (f32[8,8,8,128]{3,2,1,0:T(8,128)}, f32[39,256]{1,0:T(8,128)}) custom-call(f32[64,8,128]{2,1,0:T(8,128)S(1)} %sweeps.1.refs_0_, f32[16,1024]{1,0:T(8,128)S(1)} %get-tuple-element.36.refs_1_, f32[4,1024]{1,0:T(4,128)S(1)} %collective-permute-done.4.refs_2_, f32[4,1024]{1,0:T(4,128)S(1)} %collective-permute-done.5.refs_3_, ...), custom_call_target="tpu_custom_call" | custom-call | tf_op jit(solution)/shard_map/strips/pallas_call | solution.py:26
Async XLA Ops:
  3.9 6.8 %collective-permute-start = (bf16[400,128]{1,0:T(8,128)(2,1)S(1)}, bf16[400,128]{1,0:T(8,128)(2,1)S(1)}, u32[]{:S(2)}, u32[]{:S(2)}) collective-permute-start(bf16[400,128]{1,0:T(8,128)(2,1)S(1)} %get-tuple-element.30), channel_id=1, source_target_pairs={{0,4},{1,5},{2,6},{3,7},{4,0},{5,1},{6,2},{7,3},{8,12},{9,13},{10,... | collective-permute-start | bytes 307208 | tf_op jit(solution)/shard_map/ppermute | solution.py:461
  6.9 5.6 %collective-permute-start.1 = (bf16[304,128]{1,0:T(8,128)(2,1)S(1)}, bf16[304,128]{1,0:T(8,128)(2,1)S(1)}, u32[]{:S(2)}, u32[]{:S(2)}) collective-permute-start(bf16[304,128]{1,0:T(8,128)(2,1)S(1)} %get-tuple-element.33), channel_id=1, source_target_pairs={{0,1},{1,0},{2,3},{3,2},{4,8},{5,9},{6,10},{7,11},{8,4},{9,5},{10,... | collective-permute-start | bytes 233480 | tf_op jit(solution)/shard_map/ppermute | solution.py:461
  10.8 4.0 %collective-permute-start.2 = (bf16[144,128]{1,0:T(8,128)(2,1)S(1)}, bf16[144,128]{1,0:T(8,128)(2,1)S(1)}, u32[]{:S(2)}, u32[]{:S(2)}) collective-permute-start(bf16[144,128]{1,0:T(8,128)(2,1)S(1)} %get-tuple-element.31), channel_id=1, source_target_pairs={{0,8},{1,9},{2,10},{3,11},{4,12},{5,13},{6,14},{7,15},{8,0},{9,1},... | collective-permute-start | bytes 110600 | tf_op jit(solution)/shard_map/ppermute | solution.py:461
  12.5 1.7 %collective-permute-start.3 = (bf16[48,128]{1,0:T(8,128)(2,1)S(1)}, bf16[48,128]{1,0:T(8,128)(2,1)S(1)}, u32[]{:S(2)}, u32[]{:S(2)}) collective-permute-start(bf16[48,128]{1,0:T(8,128)(2,1)S(1)} %get-tuple-element.23.own_list.refs_2_.refs_1_), channel_id=1, source_target_pairs={{0,1},{1,0},{2,3},{3,2},{4,5},{5,4},{6,7},{7,6},{8,16},{9,17},{10,... | collective-permute-start | bytes 36872 | tf_op jit(solution)/shard_map/ppermute | solution.py:461
  16.2 6.4 %collective-permute-start.6 = (f32[39,128]{1,0:T(8,128)S(1)}, f32[39,128]{1,0:T(8,128)S(1)}, u32[]{:S(2)}, u32[]{:S(2)}) collective-permute-start(f32[39,128]{1,0:T(8,128)S(1)} %get-tuple-element.40), channel_id=1, source_target_pairs={{0,16},{1,17},{2,18},{3,19},{4,20},{5,21},{6,22},{7,23},{8,24},{9,... | collective-permute-start | bytes 59912 | tf_op jit(solution)/shard_map/ppermute | solution.py:461
  19.5 2.8 %collective-permute-start.4 = (f32[4,1024]{1,0:T(4,128)S(1)}, f32[4,1024]{1,0:T(4,128)S(1)}, u32[]{:S(2)}, u32[]{:S(2)}) collective-permute-start(f32[4,1024]{1,0:T(4,128)S(1)} %get-tuple-element.37), channel_id=1, source_target_pairs={{0,1},{1,0},{2,3},{3,2},{4,5},{5,4},{6,7},{7,6},{8,9},{9,8},{10,11... | collective-permute-start | bytes 49160 | tf_op jit(solution)/shard_map/ppermute | solution.py:461
  19.5 3.2 %collective-permute-start.5 = (f32[4,1024]{1,0:T(4,128)S(1)}, f32[4,1024]{1,0:T(4,128)S(1)}, u32[]{:S(2)}, u32[]{:S(2)}) collective-permute-start(f32[4,1024]{1,0:T(4,128)S(1)} %get-tuple-element.38), channel_id=1, source_target_pairs={{0,3},{1,2},{2,1},{3,0},{4,7},{5,6},{6,5},{7,4},{8,11},{9,10},{10,... | collective-permute-start | bytes 49160 | tf_op jit(solution)/shard_map/ppermute | solution.py:461

commit v6 on v5

--- a/solution.py
+++ b/solution.py
@@ -293,7 +293,8 @@
     h_even = lax.axis_index("gy") % 2 == 0
     head_rows, tail_rows = rims[:sweeps], rims[2 * edge - sweeps :]
     strip_even[...] = jnp.where(h_even, tail_rows, head_rows)
-    strip_odd[...] = jnp.where(h_even, head_rows, tail_rows)
+    strip_odd[:sweeps, :] = jnp.where(h_even, head_rows, tail_rows)
+    strip_odd[sweeps:, :] = head_rows
     value = take_in(buffer[...], get_pieces(far_e, count, buffer.shape[0]), (g // 2) % 2 == 1, 2 * capacity)
     merged[...] = value
     send[...] = first_send(value, (g // after) % 2 == 1, after * capacity)
@@ -334,7 +335,7 @@
     h_even = h % 2 == 0
     edge = 2 * sweeps
     has_right, has_left = h + 1 < row_count, h >= 1
-    a, b = got_even[...], got_odd[...]
+    a, b = got_even[...], got_odd[:sweeps, :]
     right = jnp.where(has_right, jnp.where(h_even, a, b), 0.0)
     left = jnp.where(has_left, jnp.where(h_even, b, a), 0.0)
     own = strips[...]
@@ -542,7 +543,7 @@
         step = 4
         field, strips, strip_even, strip_odd, buffer, send = call(
             kernel(far_kernel, grid_count=grid_count, capacity=capacity, after=step),
-            [(one_field, f32), ((4 * sweeps, 2 * m), f32), ((sweeps, 2 * m), f32), ((sweeps, 2 * m), f32),
+            [(one_field, f32), ((4 * sweeps, 2 * m), f32), ((sweeps, 2 * m), f32), ((2 * sweeps, 2 * m), f32),
              ((species, columns), f32)] + [half_buffer],
             "far",
             [field, buffer, near_e, near_o, far_e, far_o],

time: 24.3 us -> 23.6 us (0.971)
  waiting for transfers between devices: 3.63 us -> 3.3 us
  starting transfers between devices: 9.61 us -> 9.33 us
    ppermute x7, waiting for transfers between devices: 3.63 us -> 3.3 us  [swap(): return lax.ppermute(value, GRID, swap_pairs(grid_count, row_count, partner))]
    ppermute x7, starting transfers between devices: 9.61 us -> 9.33 us  [swap(): return lax.ppermute(value, GRID, swap_pairs(grid_count, row_count, partner))]
  transfers between devices with their start and end apart: 7 -> 7, of which waited for: 3 -> 2; matrix products, arithmetic and copies ran while one was open for 0% -> 0% of each run, Pallas kernels for 17% -> 17%
where the time goes in v6:
time: 23.6 us; the launch traced here: 23.5 us
  Pallas kernels  9.48 us (40%)
  starting transfers between devices  9.33 us (40%)
  waiting for transfers between devices  3.3 us (14%)
  between operations  1.35 us (6%)
    pallas_call x7, Pallas kernels, call(): pl.pallas_call(body, out_shape=tuple((jax.ShapeDtypeStruct(s, t) for s, t...  9.48 us
    ppermute x7, starting transfers between devices, swap(): return lax.ppermute(value, GRID, swap_pairs(grid_count, row_count, partner))  9.33 us
    ppermute x7, waiting for transfers between devices, swap(): return lax.ppermute(value, GRID, swap_pairs(grid_count, row_count, partner))  3.3 us
  transfers between devices with their start and end apart: 7, of which 2 were waited for; matrix products, arithmetic and copies ran while one was open for 0% of the time, Pallas kernels for 17%

profile of v6, /device:TPU:0, one launch (start us, length us, event | category | flops | bytes accessed | tf_op | source)
XLA Modules:
  0.0 23.5 jit_solution(6389795009494470892)
XLA Ops:
  1.3 2.6 %advance.1 = (f32[39,2048]{1,0:T(8,128)S(1)}, bf16[400,128]{1,0:T(8,128)(2,1)S(1)}, bf16[304,128]{1,0:T(8,128)(2,1)S(1)}, bf16[48,128]{1,0:T(8,128)(2,1)S(1)}, f32[39,256]{1,0:T(8,128)S(1)}) custom-call(s32[1]{0:T(128)S(6)} %copy.14.refs_0_, f32[39,2048]{1,0:T(8,128)} %refs_1_.1, f32[39,39]{1,0:T(8,128)} %refs_2_.1, f32[1,39]{1,0:T(1,128)} %bitcast.9, ...), custom_call_target="tpu_custom_call" | custom-call | tf_op jit(solution)/shard_map/advance/pallas_call | solution.py:26
  3.9 3.0 %collective-permute-start = (bf16[400,128]{1,0:T(8,128)(2,1)S(1)}, bf16[400,128]{1,0:T(8,128)(2,1)S(1)}, u32[]{:S(2)}, u32[]{:S(2)}) collective-permute-start(bf16[400,128]{1,0:T(8,128)(2,1)S(1)} %get-tuple-element.30), channel_id=1, source_target_pairs={{0,4},{1,5},{2,6},{3,7},{4,0},{5,1},{6,2},{7,3},{8,12},{9,13},{10,... | collective-permute-start | bytes 307208 | tf_op jit(solution)/shard_map/ppermute | solution.py:462
  6.9 0.0 collective-permute-start.1
  6.9 1.1 %own.1 = (f32[64,16,128]{2,1,0:T(8,128)S(1)}, f32[39,2048]{1,0:T(8,128)}) custom-call(f32[64,8,128]{2,1,0:T(8,128)} %oxygen_hbm.1, bf16[48,128]{1,0:T(8,128)(2,1)S(1)} %get-tuple-element.23.own_list.refs_2_.refs_1_, f32[39,2048]{1,0:T(8,128)S(1)} %get-tuple-element.24.state), custom_call_target="tpu_custom_call" | custom-call | tf_op jit(solution)/shard_map/own/pallas_call | solution.py:26
  8.1 2.7 %collective-permute-done.refs_1_.refs_2_ = bf16[400,128]{1,0:T(8,128)(2,1)S(1)} collective-permute-done((bf16[400,128]{1,0:T(8,128)(2,1)S(1)}, bf16[400,128]{1,0:T(8,128)(2,1)S(1)}, u32[]{:S(2)}, u32[]{:S(2)}) %collective-permute-start) | collective-permute-done | bytes 102432 | tf_op jit(solution)/shard_map/ppermute | solution.py:462
  10.7 0.1 relay.1
  10.8 1.7 %collective-permute-start.2 = (bf16[144,128]{1,0:T(8,128)(2,1)S(1)}, bf16[144,128]{1,0:T(8,128)(2,1)S(1)}, u32[]{:S(2)}, u32[]{:S(2)}) collective-permute-start(bf16[144,128]{1,0:T(8,128)(2,1)S(1)} %get-tuple-element.31), channel_id=1, source_target_pairs={{0,8},{1,9},{2,10},{3,11},{4,12},{5,13},{6,14},{7,15},{8,0},{9,1},... | collective-permute-start | bytes 110600 | tf_op jit(solution)/shard_map/ppermute | solution.py:462
  12.5 0.0 collective-permute-start.3
  12.5 0.0 collective-permute-done.1.refs_3_
  12.5 1.7 %near.1.refs_0_ = f32[64,16,128]{2,1,0:T(8,128)S(1)} custom-call(f32[64,16,128]{2,1,0:T(8,128)S(1)} %get-tuple-element.32.refs_0_, bf16[48,128]{1,0:T(8,128)(2,1)S(1)} %get-tuple-element.23.own_list.refs_2_.refs_1_, bf16[400,128]{1,0:T(8,128)(2,1)S(1)} %collective-permute-done.refs_1_.refs_2_, bf16[304,128]{1,0:T(8,128)(2,1)S(1)} %collective-permute-done.1.refs_3_), custom_call_target="tpu_custom_call" | custom-call | tf_op jit(solution)/shard_map/near/pallas_call | solution.py:26
  14.2 0.0 collective-permute-done.3.refs_5_
  14.2 0.6 %collective-permute-done.2.refs_4_ = bf16[144,128]{1,0:T(8,128)(2,1)S(1)} collective-permute-done((bf16[144,128]{1,0:T(8,128)(2,1)S(1)}, bf16[144,128]{1,0:T(8,128)(2,1)S(1)}, u32[]{:S(2)}, u32[]{:S(2)}) %collective-permute-start.2) | collective-permute-done | bytes 36896 | tf_op jit(solution)/shard_map/ppermute | solution.py:462
  14.9 1.3 %far.1 = (f32[64,16,128]{2,1,0:T(8,128)S(1)}, f32[16,1024]{1,0:T(8,128)S(1)}, f32[4,1024]{1,0:T(4,128)S(1)}, f32[8,1024]{1,0:T(8,128)S(1)}, f32[39,256]{1,0:T(8,128)S(1)}, /*index=5*/f32[39,128]{1,0:T(8,128)S(1)}) custom-call(f32[64,16,128]{2,1,0:T(8,128)S(1)} %near.1.refs_0_, f32[39,256]{1,0:T(8,128)S(1)} %get-tuple-element.34.refs_1_, ...), custom_call_target="tpu_custom_call" | custom-call | tf_op jit(solution)/shard_map/far/pallas_call | solution.py:26
  16.2 1.0 %collective-permute-start.5 = (f32[8,1024]{1,0:T(8,128)S(1)}, f32[8,1024]{1,0:T(8,128)S(1)}, u32[]{:S(2)}, u32[]{:S(2)}) collective-permute-start(f32[8,1024]{1,0:T(8,128)S(1)} %get-tuple-element.38), channel_id=1, source_target_pairs={{0,3},{1,2},{2,1},{3,0},{4,7},{5,6},{6,5},{7,4},{8,11},{9,10},{10,... | collective-permute-start | bytes 98312 | tf_op jit(solution)/shard_map/ppermute | solution.py:462
  17.2 2.3 %collective-permute-start.6 = (f32[39,128]{1,0:T(8,128)S(1)}, f32[39,128]{1,0:T(8,128)S(1)}, u32[]{:S(2)}, u32[]{:S(2)}) collective-permute-start(f32[39,128]{1,0:T(8,128)S(1)} %get-tuple-element.40), channel_id=1, source_target_pairs={{0,16},{1,17},{2,18},{3,19},{4,20},{5,21},{6,22},{7,23},{8,24},{9,... | collective-permute-start | bytes 59912 | tf_op jit(solution)/shard_map/ppermute | solution.py:462
  19.5 1.3 %collective-permute-start.4 = (f32[4,1024]{1,0:T(4,128)S(1)}, f32[4,1024]{1,0:T(4,128)S(1)}, u32[]{:S(2)}, u32[]{:S(2)}) collective-permute-start(f32[4,1024]{1,0:T(4,128)S(1)} %get-tuple-element.37), channel_id=1, source_target_pairs={{0,1},{1,0},{2,3},{3,2},{4,5},{5,4},{6,7},{7,6},{8,9},{9,8},{10,11... | collective-permute-start | bytes 49160 | tf_op jit(solution)/shard_map/ppermute | solution.py:462
  20.8 1.2 %sweeps.1.refs_0_ = f32[64,8,128]{2,1,0:T(8,128)S(1)} custom-call(f32[64,16,128]{2,1,0:T(8,128)S(1)} %get-tuple-element.35.refs_0_), custom_call_target="tpu_custom_call" | custom-call | tf_op jit(solution)/shard_map/sweeps/pallas_call | solution.py:26
  22.0 0.0 collective-permute-done.4.refs_2_
  22.0 0.0 collective-permute-done.6.refs_5_
  22.0 0.0 collective-permute-done.5.refs_3_
  22.0 1.4 %strips.1 = (f32[8,8,8,128]{3,2,1,0:T(8,128)}, f32[39,256]{1,0:T(8,128)}) custom-call(f32[64,8,128]{2,1,0:T(8,128)S(1)} %sweeps.1.refs_0_, f32[16,1024]{1,0:T(8,128)S(1)} %get-tuple-element.36.refs_1_, f32[4,1024]{1,0:T(4,128)S(1)} %collective-permute-done.4.refs_2_, f32[8,1024]{1,0:T(8,128)S(1)} %collective-permute-done.5.refs_3_, ...), custom_call_target="tpu_custom_call" | custom-call | tf_op jit(solution)/shard_map/strips/pallas_call | solution.py:26
Async XLA Ops:
  3.9 6.8 %collective-permute-start = (bf16[400,128]{1,0:T(8,128)(2,1)S(1)}, bf16[400,128]{1,0:T(8,128)(2,1)S(1)}, u32[]{:S(2)}, u32[]{:S(2)}) collective-permute-start(bf16[400,128]{1,0:T(8,128)(2,1)S(1)} %get-tuple-element.30), channel_id=1, source_target_pairs={{0,4},{1,5},{2,6},{3,7},{4,0},{5,1},{6,2},{7,3},{8,12},{9,13},{10,... | collective-permute-start | bytes 307208 | tf_op jit(solution)/shard_map/ppermute | solution.py:462
  6.9 5.6 %collective-permute-start.1 = (bf16[304,128]{1,0:T(8,128)(2,1)S(1)}, bf16[304,128]{1,0:T(8,128)(2,1)S(1)}, u32[]{:S(2)}, u32[]{:S(2)}) collective-permute-start(bf16[304,128]{1,0:T(8,128)(2,1)S(1)} %get-tuple-element.33), channel_id=1, source_target_pairs={{0,1},{1,0},{2,3},{3,2},{4,8},{5,9},{6,10},{7,11},{8,4},{9,5},{10,... | collective-permute-start | bytes 233480 | tf_op jit(solution)/shard_map/ppermute | solution.py:462
  10.8 4.0 %collective-permute-start.2 = (bf16[144,128]{1,0:T(8,128)(2,1)S(1)}, bf16[144,128]{1,0:T(8,128)(2,1)S(1)}, u32[]{:S(2)}, u32[]{:S(2)}) collective-permute-start(bf16[144,128]{1,0:T(8,128)(2,1)S(1)} %get-tuple-element.31), channel_id=1, source_target_pairs={{0,8},{1,9},{2,10},{3,11},{4,12},{5,13},{6,14},{7,15},{8,0},{9,1},... | collective-permute-start | bytes 110600 | tf_op jit(solution)/shard_map/ppermute | solution.py:462
  12.5 1.7 %collective-permute-start.3 = (bf16[48,128]{1,0:T(8,128)(2,1)S(1)}, bf16[48,128]{1,0:T(8,128)(2,1)S(1)}, u32[]{:S(2)}, u32[]{:S(2)}) collective-permute-start(bf16[48,128]{1,0:T(8,128)(2,1)S(1)} %get-tuple-element.23.own_list.refs_2_.refs_1_), channel_id=1, source_target_pairs={{0,1},{1,0},{2,3},{3,2},{4,5},{5,4},{6,7},{7,6},{8,16},{9,17},{10,... | collective-permute-start | bytes 36872 | tf_op jit(solution)/shard_map/ppermute | solution.py:462
  16.2 5.8 %collective-permute-start.5 = (f32[8,1024]{1,0:T(8,128)S(1)}, f32[8,1024]{1,0:T(8,128)S(1)}, u32[]{:S(2)}, u32[]{:S(2)}) collective-permute-start(f32[8,1024]{1,0:T(8,128)S(1)} %get-tuple-element.38), channel_id=1, source_target_pairs={{0,3},{1,2},{2,1},{3,0},{4,7},{5,6},{6,5},{7,4},{8,11},{9,10},{10,... | collective-permute-start | bytes 98312 | tf_op jit(solution)/shard_map/ppermute | solution.py:462
  17.2 4.8 %collective-permute-start.6 = (f32[39,128]{1,0:T(8,128)S(1)}, f32[39,128]{1,0:T(8,128)S(1)}, u32[]{:S(2)}, u32[]{:S(2)}) collective-permute-start(f32[39,128]{1,0:T(8,128)S(1)} %get-tuple-element.40), channel_id=1, source_target_pairs={{0,16},{1,17},{2,18},{3,19},{4,20},{5,21},{6,22},{7,23},{8,24},{9,... | collective-permute-start | bytes 59912 | tf_op jit(solution)/shard_map/ppermute | solution.py:462
  19.5 2.5 %collective-permute-start.4 = (f32[4,1024]{1,0:T(4,128)S(1)}, f32[4,1024]{1,0:T(4,128)S(1)}, u32[]{:S(2)}, u32[]{:S(2)}) collective-permute-start(f32[4,1024]{1,0:T(4,128)S(1)} %get-tuple-element.37), channel_id=1, source_target_pairs={{0,1},{1,0},{2,3},{3,2},{4,5},{5,4},{6,7},{7,6},{8,9},{9,8},{10,11... | collective-permute-start | bytes 49160 | tf_op jit(solution)/shard_map/ppermute | solution.py:462

commit v7 on v6

--- a/solution.py
+++ b/solution.py
@@ -126,7 +126,9 @@
     total = jnp.sum(weight_c * current, axis=0, keepdims=True)
     for c in range(rows):
         drive[c : c + 1, :] = total[:, c * LANES : (c + 1) * LANES]
-    mothers = sum(jnp.dot(p, chosen[...], preferred_element_type=f32) for p in pieces(current)[:2])
+    stacked = [jnp.pad(p, ((0, PIECE_ROWS - species), (0, 0))) for p in pieces(current)[:2]]
+    both = jnp.dot(jnp.concatenate(stacked, axis=0), chosen[...], preferred_element_type=f32)
+    mothers = both[:species] + both[PIECE_ROWS : PIECE_ROWS + species]
     copies[-1].wait()
     x = drive[...]
     soft = jnp.maximum(x, 0.0) + jnp.log1p(jnp.exp(-jnp.abs(x)))

time: 23.6 us -> 23.6 us (level)
  transfers between devices with their start and end apart: 7 -> 7, of which waited for: 2 -> 2; matrix products, arithmetic and copies ran while one was open for 0% -> 0% of each run, Pallas kernels for 17% -> 18%
where the time goes in v7:
time: 23.6 us; the launch traced here: 23.4 us
  Pallas kernels  9.42 us (40%)
  starting transfers between devices  9.33 us (40%)
  waiting for transfers between devices  3.3 us (14%)
  between operations  1.35 us (6%)
    pallas_call x7, Pallas kernels, call(): pl.pallas_call(body, out_shape=tuple((jax.ShapeDtypeStruct(s, t) for s, t...  9.42 us
    ppermute x7, starting transfers between devices, swap(): return lax.ppermute(value, GRID, swap_pairs(grid_count, row_count, partner))  9.33 us
    ppermute x7, waiting for transfers between devices, swap(): return lax.ppermute(value, GRID, swap_pairs(grid_count, row_count, partner))  3.3 us
  transfers between devices with their start and end apart: 7, of which 2 were waited for; matrix products, arithmetic and copies ran while one was open for 0% of the time, Pallas kernels for 18%

profile of v7, /device:TPU:0, one launch (start us, length us, event | category | flops | bytes accessed | tf_op | source)
XLA Modules:
  0.0 23.4 jit_solution(10671417281313951997)
XLA Ops:
  1.3 2.6 %advance.1 = (f32[39,2048]{1,0:T(8,128)S(1)}, bf16[400,128]{1,0:T(8,128)(2,1)S(1)}, bf16[304,128]{1,0:T(8,128)(2,1)S(1)}, bf16[48,128]{1,0:T(8,128)(2,1)S(1)}, f32[39,256]{1,0:T(8,128)S(1)}) custom-call(s32[1]{0:T(128)S(6)} %copy.14.refs_0_, f32[39,2048]{1,0:T(8,128)} %refs_1_.1, f32[39,39]{1,0:T(8,128)} %refs_2_.1, f32[1,39]{1,0:T(1,128)} %bitcast.9, ...), custom_call_target="tpu_custom_call" | custom-call | tf_op jit(solution)/shard_map/advance/pallas_call | solution.py:26
  3.8 3.0 %collective-permute-start = (bf16[400,128]{1,0:T(8,128)(2,1)S(1)}, bf16[400,128]{1,0:T(8,128)(2,1)S(1)}, u32[]{:S(2)}, u32[]{:S(2)}) collective-permute-start(bf16[400,128]{1,0:T(8,128)(2,1)S(1)} %get-tuple-element.30), channel_id=1, source_target_pairs={{0,4},{1,5},{2,6},{3,7},{4,0},{5,1},{6,2},{7,3},{8,12},{9,13},{10,... | collective-permute-start | bytes 307208 | tf_op jit(solution)/shard_map/ppermute | solution.py:464
  6.9 0.0 collective-permute-start.1
  6.9 1.1 %own.1 = (f32[64,16,128]{2,1,0:T(8,128)S(1)}, f32[39,2048]{1,0:T(8,128)}) custom-call(f32[64,8,128]{2,1,0:T(8,128)} %oxygen_hbm.1, bf16[48,128]{1,0:T(8,128)(2,1)S(1)} %get-tuple-element.23.own_list.refs_2_.refs_1_, f32[39,2048]{1,0:T(8,128)S(1)} %get-tuple-element.24.state), custom_call_target="tpu_custom_call" | custom-call | tf_op jit(solution)/shard_map/own/pallas_call | solution.py:26
  8.0 2.7 %collective-permute-done.refs_1_.refs_2_ = bf16[400,128]{1,0:T(8,128)(2,1)S(1)} collective-permute-done((bf16[400,128]{1,0:T(8,128)(2,1)S(1)}, bf16[400,128]{1,0:T(8,128)(2,1)S(1)}, u32[]{:S(2)}, u32[]{:S(2)}) %collective-permute-start) | collective-permute-done | bytes 102432 | tf_op jit(solution)/shard_map/ppermute | solution.py:464
  10.7 0.1 relay.1
  10.8 1.7 %collective-permute-start.2 = (bf16[144,128]{1,0:T(8,128)(2,1)S(1)}, bf16[144,128]{1,0:T(8,128)(2,1)S(1)}, u32[]{:S(2)}, u32[]{:S(2)}) collective-permute-start(bf16[144,128]{1,0:T(8,128)(2,1)S(1)} %get-tuple-element.31), channel_id=1, source_target_pairs={{0,8},{1,9},{2,10},{3,11},{4,12},{5,13},{6,14},{7,15},{8,0},{9,1},... | collective-permute-start | bytes 110600 | tf_op jit(solution)/shard_map/ppermute | solution.py:464
  12.5 0.0 collective-permute-start.3
  12.5 0.0 collective-permute-done.1.refs_3_
  12.5 1.7 %near.1.refs_0_ = f32[64,16,128]{2,1,0:T(8,128)S(1)} custom-call(f32[64,16,128]{2,1,0:T(8,128)S(1)} %get-tuple-element.32.refs_0_, bf16[48,128]{1,0:T(8,128)(2,1)S(1)} %get-tuple-element.23.own_list.refs_2_.refs_1_, bf16[400,128]{1,0:T(8,128)(2,1)S(1)} %collective-permute-done.refs_1_.refs_2_, bf16[304,128]{1,0:T(8,128)(2,1)S(1)} %collective-permute-done.1.refs_3_), custom_call_target="tpu_custom_call" | custom-call | tf_op jit(solution)/shard_map/near/pallas_call | solution.py:26
  14.2 0.0 collective-permute-done.3.refs_5_
  14.2 0.6 %collective-permute-done.2.refs_4_ = bf16[144,128]{1,0:T(8,128)(2,1)S(1)} collective-permute-done((bf16[144,128]{1,0:T(8,128)(2,1)S(1)}, bf16[144,128]{1,0:T(8,128)(2,1)S(1)}, u32[]{:S(2)}, u32[]{:S(2)}) %collective-permute-start.2) | collective-permute-done | bytes 36896 | tf_op jit(solution)/shard_map/ppermute | solution.py:464
  14.8 1.3 %far.1 = (f32[64,16,128]{2,1,0:T(8,128)S(1)}, f32[16,1024]{1,0:T(8,128)S(1)}, f32[4,1024]{1,0:T(4,128)S(1)}, f32[8,1024]{1,0:T(8,128)S(1)}, f32[39,256]{1,0:T(8,128)S(1)}, /*index=5*/f32[39,128]{1,0:T(8,128)S(1)}) custom-call(f32[64,16,128]{2,1,0:T(8,128)S(1)} %near.1.refs_0_, f32[39,256]{1,0:T(8,128)S(1)} %get-tuple-element.34.refs_1_, ...), custom_call_target="tpu_custom_call" | custom-call | tf_op jit(solution)/shard_map/far/pallas_call | solution.py:26
  16.1 1.0 %collective-permute-start.5 = (f32[8,1024]{1,0:T(8,128)S(1)}, f32[8,1024]{1,0:T(8,128)S(1)}, u32[]{:S(2)}, u32[]{:S(2)}) collective-permute-start(f32[8,1024]{1,0:T(8,128)S(1)} %get-tuple-element.38), channel_id=1, source_target_pairs={{0,3},{1,2},{2,1},{3,0},{4,7},{5,6},{6,5},{7,4},{8,11},{9,10},{10,... | collective-permute-start | bytes 98312 | tf_op jit(solution)/shard_map/ppermute | solution.py:464
  17.1 2.3 %collective-permute-start.6 = (f32[39,128]{1,0:T(8,128)S(1)}, f32[39,128]{1,0:T(8,128)S(1)}, u32[]{:S(2)}, u32[]{:S(2)}) collective-permute-start(f32[39,128]{1,0:T(8,128)S(1)} %get-tuple-element.40), channel_id=1, source_target_pairs={{0,16},{1,17},{2,18},{3,19},{4,20},{5,21},{6,22},{7,23},{8,24},{9,... | collective-permute-start | bytes 59912 | tf_op jit(solution)/shard_map/ppermute | solution.py:464
  19.5 1.2 %collective-permute-start.4 = (f32[4,1024]{1,0:T(4,128)S(1)}, f32[4,1024]{1,0:T(4,128)S(1)}, u32[]{:S(2)}, u32[]{:S(2)}) collective-permute-start(f32[4,1024]{1,0:T(4,128)S(1)} %get-tuple-element.37), channel_id=1, source_target_pairs={{0,1},{1,0},{2,3},{3,2},{4,5},{5,4},{6,7},{7,6},{8,9},{9,8},{10,11... | collective-permute-start | bytes 49160 | tf_op jit(solution)/shard_map/ppermute | solution.py:464
  20.7 1.2 %sweeps.1.refs_0_ = f32[64,8,128]{2,1,0:T(8,128)S(1)} custom-call(f32[64,16,128]{2,1,0:T(8,128)S(1)} %get-tuple-element.35.refs_0_), custom_call_target="tpu_custom_call" | custom-call | tf_op jit(solution)/shard_map/sweeps/pallas_call | solution.py:26
  21.9 0.0 collective-permute-done.4.refs_2_
  21.9 0.0 collective-permute-done.6.refs_5_
  22.0 0.0 collective-permute-done.5.refs_3_
  22.0 1.4 %strips.1 = (f32[8,8,8,128]{3,2,1,0:T(8,128)}, f32[39,256]{1,0:T(8,128)}) custom-call(f32[64,8,128]{2,1,0:T(8,128)S(1)} %sweeps.1.refs_0_, f32[16,1024]{1,0:T(8,128)S(1)} %get-tuple-element.36.refs_1_, f32[4,1024]{1,0:T(4,128)S(1)} %collective-permute-done.4.refs_2_, f32[8,1024]{1,0:T(8,128)S(1)} %collective-permute-done.5.refs_3_, ...), custom_call_target="tpu_custom_call" | custom-call | tf_op jit(solution)/shard_map/strips/pallas_call | solution.py:26
Async XLA Ops:
  3.8 6.8 %collective-permute-start = (bf16[400,128]{1,0:T(8,128)(2,1)S(1)}, bf16[400,128]{1,0:T(8,128)(2,1)S(1)}, u32[]{:S(2)}, u32[]{:S(2)}) collective-permute-start(bf16[400,128]{1,0:T(8,128)(2,1)S(1)} %get-tuple-element.30), channel_id=1, source_target_pairs={{0,4},{1,5},{2,6},{3,7},{4,0},{5,1},{6,2},{7,3},{8,12},{9,13},{10,... | collective-permute-start | bytes 307208 | tf_op jit(solution)/shard_map/ppermute | solution.py:464
  6.9 5.6 %collective-permute-start.1 = (bf16[304,128]{1,0:T(8,128)(2,1)S(1)}, bf16[304,128]{1,0:T(8,128)(2,1)S(1)}, u32[]{:S(2)}, u32[]{:S(2)}) collective-permute-start(bf16[304,128]{1,0:T(8,128)(2,1)S(1)} %get-tuple-element.33), channel_id=1, source_target_pairs={{0,1},{1,0},{2,3},{3,2},{4,8},{5,9},{6,10},{7,11},{8,4},{9,5},{10,... | collective-permute-start | bytes 233480 | tf_op jit(solution)/shard_map/ppermute | solution.py:464
  10.8 4.0 %collective-permute-start.2 = (bf16[144,128]{1,0:T(8,128)(2,1)S(1)}, bf16[144,128]{1,0:T(8,128)(2,1)S(1)}, u32[]{:S(2)}, u32[]{:S(2)}) collective-permute-start(bf16[144,128]{1,0:T(8,128)(2,1)S(1)} %get-tuple-element.31), channel_id=1, source_target_pairs={{0,8},{1,9},{2,10},{3,11},{4,12},{5,13},{6,14},{7,15},{8,0},{9,1},... | collective-permute-start | bytes 110600 | tf_op jit(solution)/shard_map/ppermute | solution.py:464
  12.5 1.7 %collective-permute-start.3 = (bf16[48,128]{1,0:T(8,128)(2,1)S(1)}, bf16[48,128]{1,0:T(8,128)(2,1)S(1)}, u32[]{:S(2)}, u32[]{:S(2)}) collective-permute-start(bf16[48,128]{1,0:T(8,128)(2,1)S(1)} %get-tuple-element.23.own_list.refs_2_.refs_1_), channel_id=1, source_target_pairs={{0,1},{1,0},{2,3},{3,2},{4,5},{5,4},{6,7},{7,6},{8,16},{9,17},{10,... | collective-permute-start | bytes 36872 | tf_op jit(solution)/shard_map/ppermute | solution.py:464
  16.1 5.8 %collective-permute-start.5 = (f32[8,1024]{1,0:T(8,128)S(1)}, f32[8,1024]{1,0:T(8,128)S(1)}, u32[]{:S(2)}, u32[]{:S(2)}) collective-permute-start(f32[8,1024]{1,0:T(8,128)S(1)} %get-tuple-element.38), channel_id=1, source_target_pairs={{0,3},{1,2},{2,1},{3,0},{4,7},{5,6},{6,5},{7,4},{8,11},{9,10},{10,... | collective-permute-start | bytes 98312 | tf_op jit(solution)/shard_map/ppermute | solution.py:464
  17.1 4.8 %collective-permute-start.6 = (f32[39,128]{1,0:T(8,128)S(1)}, f32[39,128]{1,0:T(8,128)S(1)}, u32[]{:S(2)}, u32[]{:S(2)}) collective-permute-start(f32[39,128]{1,0:T(8,128)S(1)} %get-tuple-element.40), channel_id=1, source_target_pairs={{0,16},{1,17},{2,18},{3,19},{4,20},{5,21},{6,22},{7,23},{8,24},{9,... | collective-permute-start | bytes 59912 | tf_op jit(solution)/shard_map/ppermute | solution.py:464
  19.5 2.5 %collective-permute-start.4 = (f32[4,1024]{1,0:T(4,128)S(1)}, f32[4,1024]{1,0:T(4,128)S(1)}, u32[]{:S(2)}, u32[]{:S(2)}) collective-permute-start(f32[4,1024]{1,0:T(4,128)S(1)} %get-tuple-element.37), channel_id=1, source_target_pairs={{0,1},{1,0},{2,3},{3,2},{4,5},{5,4},{6,7},{7,6},{8,9},{9,8},{10,11... | collective-permute-start | bytes 49160 | tf_op jit(solution)/shard_map/ppermute | solution.py:464
